TPU v7x, 32 devices: a whole 2x2x4 slice. The times are simulated.
32 devices in a mesh: lat: 4 (over z), lon: 8 (over y, x, core).
Axes of the slice: x: 2, y: 2, z: 4, core: 2. Of those that a mesh axis runs over, the one named last changes fastest.
Arguments:
- layer_input: float32 [4, 768, 90, 180], P('lat', 'lon'), may hold values from -6 to 6
- grad_output: float32 [4, 768, 90, 180], P('lat', 'lon'), may hold values from -6 to 6
- first_weight: float32 [2, 8, 96, 96], replicated, may hold values from -0.625 to 0.625
- first_bias: float32 [2, 8, 96], replicated, may hold values from -3 to 3
- second_weight: float32 [2, 8, 96, 96], replicated, may hold values from -0.625 to 0.625
- second_bias: float32 [2, 8, 96], replicated, may hold values from -3 to 3
Outputs:
- grad_input: float32 [4, 768, 90, 180], P('lat', 'lon')
- grad_first_weight: float32 [2, 8, 96, 96], replicated
- grad_first_bias: float32 [2, 8, 96], replicated
- grad_second_weight: float32 [2, 8, 96, 96], replicated
- grad_second_bias: float32 [2, 8, 96], replicated
All inputs are finite; a program needn't handle non-finite values.
Results may differ from a plain program's by a relative error of at most 0.0003.
Values sent between devices are 32-bit elements; how exact they have to be, the bound alone decides.
No kernel may reach another device: no remote copies, remote signals or barrier semaphores. Data moves between devices by JAX's collectives and lax.ppermute only.
A program may use at most 192 MiB of HBM per device.

v0:
```python
import math

import jax
import jax.numpy as jnp
from jax import lax
from jax.sharding import PartitionSpec as P

SHRINK = 0.01
GELU_SCALE = math.sqrt(2.0 / math.pi)
GELU_CUBE = 0.044715
HIGHEST = lax.Precision.HIGHEST


def tables(length, count, limit):
    first = jnp.arange(length, dtype=jnp.int32)[:, None]
    second = jnp.arange(count, dtype=jnp.int32)[None, :]
    angle = 2.0 * math.pi / length * (first * second % length).astype(jnp.float32)
    keeper = (second < limit).astype(jnp.float32) / math.sqrt(length)
    return (jnp.cos(angle) * keeper, jnp.sin(angle) * keeper)


def cotangent_weight(length, count):
    index = jnp.arange(count, dtype=jnp.int32)
    edge = (index == 0) | (2 * index == length)
    return jnp.where(edge, 1.0, 2.0).astype(jnp.float32)


def gelu_slope(value):
    inner = GELU_SCALE * (value + GELU_CUBE * value * value * value)
    tangent = jnp.tanh(inner)
    return 0.5 * (1.0 + tangent) + 0.5 * value * (1.0 - tangent * tangent) * GELU_SCALE * (
        1.0 + 3.0 * GELU_CUBE * value * value
    )


def complex_matrix(weight):
    real_part = weight[0]
    imag_part = weight[1]
    upper = jnp.stack([real_part, imag_part], axis=2)
    lower = jnp.stack([-imag_part, real_part], axis=2)
    return jnp.stack([upper, lower], axis=1)


def forward_mix(left, matrix):
    return jnp.einsum("psbir,bpiqj->qsbjr", left, matrix, precision=HIGHEST)


def back_mix(left, matrix):
    return jnp.einsum("qsbjr,bpiqj->psbir", left, matrix, precision=HIGHEST)


def weight_grad(left, right):
    total = jnp.einsum("psbir,qsbjr->bpiqj", left, right, precision=HIGHEST)
    grad_real = total[:, 0, :, 0, :] + total[:, 1, :, 1, :]
    grad_imag = total[:, 0, :, 1, :] - total[:, 1, :, 0, :]
    return jnp.stack([grad_real, grad_imag])


def bias_view(vector):
    return vector[:, None, :, :, None]


def block_backward(x_both, g_both, first_weight, first_bias, second_weight, second_bias):
    parts, samples, channels, modes = x_both.shape
    blocks = first_weight.shape[1]
    width = first_weight.shape[2]
    shape_five = (parts, samples, blocks, width, modes)
    x_both = x_both.reshape(shape_five)
    g_both = g_both.reshape(shape_five)
    first_matrix = complex_matrix(first_weight)
    second_matrix = complex_matrix(second_weight)
    a_both = forward_mix(x_both, first_matrix) + bias_view(first_bias)
    o_both = jax.nn.gelu(a_both, approximate=True)
    z_both = forward_mix(o_both, second_matrix) + bias_view(second_bias)
    e_both = g_both * jnp.tanh(z_both / SHRINK) ** 2
    grad_w_two = weight_grad(o_both, e_both)
    grad_b_two = jnp.sum(e_both, axis=(1, 4))
    s_both = back_mix(e_both, second_matrix) * gelu_slope(a_both)
    grad_w_one = weight_grad(x_both, s_both)
    grad_b_one = jnp.sum(s_both, axis=(1, 4))
    d_both = back_mix(s_both, first_matrix)
    return (
        d_both.reshape((parts, samples, channels, modes)),
        (grad_w_one, grad_b_one, grad_w_two, grad_b_two),
    )


def on_device(layer_input, grad_output, first_weight, first_bias, second_weight, second_bias):
    lon_count = lax.axis_size("lon")
    samples, local_ch, lat_rows, lon_cols = layer_input.shape
    kept_freqs = lon_cols // 2 + 1
    freq_slots = (lon_cols // 2 + lon_count) // lon_count * lon_count
    lon_cos, lon_sin = tables(lon_cols, freq_slots, kept_freqs)
    factor_row = cotangent_weight(lon_cols, freq_slots)[None, :]
    lon_table = jnp.stack([lon_cos, -lon_sin], axis=1)
    cot_table = jnp.stack([lon_cos * factor_row, -lon_sin * factor_row], axis=1)
    lon_back = jnp.stack([lon_cos.T, -lon_sin.T])
    lat_cos, lat_sin = tables(lat_rows, lat_rows, lat_rows)
    lat_table = jnp.stack(
        [jnp.stack([lat_cos, -lat_sin], axis=1), jnp.stack([lat_sin, lat_cos], axis=1)]
    )
    lat_back = jnp.stack(
        [jnp.stack([lat_cos, lat_sin], axis=1), jnp.stack([-lat_sin, lat_cos], axis=1)]
    )

    def lon_forward(data, table):
        return jnp.einsum("schw,wqk->qsckh", data, table, precision=HIGHEST)

    def lat_forward(data):
        return jnp.einsum("psckh,phqm->qsckm", data, lat_table, precision=HIGHEST)

    x_both = lon_forward(layer_input, lon_table)
    g_both = lon_forward(grad_output, cot_table)
    x_both = lat_forward(x_both)
    g_both = lat_forward(g_both)
    flat_shape = (2, samples, local_ch, freq_slots * lat_rows)
    x_modes, g_modes = (
        lax.all_to_all(x_both.reshape(flat_shape), "lon", split_axis=3, concat_axis=2, tiled=True),
        lax.all_to_all(g_both.reshape(flat_shape), "lon", split_axis=3, concat_axis=2, tiled=True),
    )
    d_stack, partial_grads = block_backward(
        x_modes, g_modes, first_weight, first_bias, second_weight, second_bias
    )
    stacked = lax.all_to_all(d_stack, "lon", split_axis=2, concat_axis=3, tiled=True)
    shape_five = (2, stacked.shape[1], stacked.shape[2], freq_slots, lat_rows)
    grad_input = jnp.einsum(
        "qsckh,qkw->schw",
        jnp.einsum("psckm,pmqh->qsckh", stacked.reshape(shape_five), lat_back, precision=HIGHEST),
        lon_back,
        precision=HIGHEST,
    )
    flat_grads = jnp.concatenate([piece.reshape(-1) for piece in partial_grads])
    share = lax.psum_scatter(flat_grads, "lon", scatter_dimension=0, tiled=True)
    summed = lax.psum(share, "lat")
    whole = lax.all_gather(summed, "lon", axis=0, tiled=True)
    results = []
    offset = 0
    for piece in partial_grads:
        results.append(whole[offset : offset + piece.size].reshape(piece.shape))
        offset = offset + piece.size
    grad_w_one, grad_b_one, grad_w_two, grad_b_two = results
    return (grad_input, grad_w_one, grad_b_one, grad_w_two, grad_b_two)


def solution(mesh):
    placed = (P("lat", "lon", None, None), P("lat", "lon", None, None), P(), P(), P(), P())
    return jax.shard_map(
        on_device,
        mesh=mesh,
        in_specs=placed,
        out_specs=(P("lat", "lon", None, None), P(), P(), P(), P()),
        check_vma=False,
    )
```

profile of v0, /device:TPU:0, one launch (start us, length us, event | category | flops | bytes accessed | tf_op | source)
XLA Modules:
  0.0 626.7 jit_solution(1061869455097390078)
XLA Ops:
  8.1 14.8 %fusion.56 = f32[2,96,96,90]{1,2,3,0:T(8,128)} fusion(f32[1,96,90,180]{1,0,3,2:T(1,128)} %param.7, f32[180,1,96]{2,0,1:T(8,128)S(1)} %get-tuple-element.44, f32[180,1,96]{2,0,1:T(8,128)S(1)} %get-tuple-element.43), kind=kOutput, calls=%fused_computation.52 | convolution fusion | flops 3583215360 | bytes 12994560 | tf_op jit(solution)/shard_map/schw,wqk->qsckh/dot_general | solution.py:107
  23.0 12.4 %copy.98 = f32[2,96,96,90]{3,2,0,1:T(8,128)} copy(f32[2,96,96,90]{1,2,3,0:T(8,128)} %fusion.56) | data formatting | bytes 13271040 | tf_op jit(solution)/shard_map/reshape.2
  36.1 14.5 %fusion.50 = f32[2,1,96,96,90]{3,4,2,0,1:T(8,128)} fusion(f32[2,96,96,90]{3,2,0,1:T(8,128)} %copy.98, f32[1,90,2,90]{1,3,0,2:T(8,128)S(1)} %get-tuple-element.38, f32[1,90,2,90]{1,3,0,2:T(8,128)S(1)} %get-tuple-element.41), kind=kOutput, calls=%fused_computation.49 | convolution fusion | flops 3583213056 | bytes 13400640 | tf_op jit(solution)/shard_map/psckh,phqm->qsckm/dot_general | solution.py:110
  50.6 12.5 %copy.150 = f32[2,1,96,96,90]{2,0,4,3,1:T(2,128)} copy(f32[2,1,96,96,90]{3,4,2,0,1:T(8,128)} %fusion.50) | data formatting | bytes 13271040 | tf_op jit(solution)/shard_map/reshape | solution.py:119
  63.1 5.5 all-to-all-start
  68.6 14.8 %fusion.59 = f32[2,96,96,90]{1,2,3,0:T(8,128)} fusion(f32[1,96,90,180]{1,0,3,2:T(1,128)} %param.6, f32[180,1,96]{2,0,1:T(8,128)S(1)} %get-tuple-element.48, f32[180,1,96]{2,0,1:T(8,128)S(1)} %get-tuple-element.47), kind=kOutput, calls=%fused_computation.53 | convolution fusion | flops 3583215360 | bytes 12994560 | tf_op jit(solution)/shard_map/schw,wqk->qsckh/dot_general | solution.py:107
  83.4 12.4 %copy.103 = f32[2,96,96,90]{3,2,0,1:T(8,128)} copy(f32[2,96,96,90]{1,2,3,0:T(8,128)} %fusion.59) | data formatting | bytes 13271040 | tf_op jit(solution)/shard_map/reshape.7
  95.9 14.5 %fusion.53 = f32[2,1,96,96,90]{3,4,2,0,1:T(8,128)} fusion(f32[2,96,96,90]{3,2,0,1:T(8,128)} %copy.103, f32[1,90,2,90]{1,3,0,2:T(8,128)S(1)} %get-tuple-element.38, f32[1,90,2,90]{1,3,0,2:T(8,128)S(1)} %get-tuple-element.41), kind=kOutput, calls=%fused_computation.50 | convolution fusion | flops 3583213056 | bytes 13400640 | tf_op jit(solution)/shard_map/psckh,phqm->qsckm/dot_general | solution.py:110
  110.4 12.4 %copy.153 = f32[2,1,96,96,90]{2,0,4,3,1:T(2,128)} copy(f32[2,1,96,96,90]{3,4,2,0,1:T(8,128)} %fusion.53) | data formatting | bytes 13271040 | tf_op jit(solution)/shard_map/reshape | solution.py:118
  122.8 45.2 %all-to-all-done = f32[2,1,96,8640]{2,0,1,3:T(2,128)} async-done(((f32[2,1,96,8640]{2,0,1,3:T(2,128)}), f32[2,1,96,8640]{2,0,1,3:T(2,128)}, u32[]{:S(2)}, u32[]{:S(2)}) %all-to-all-start) | async-done | bytes 6635552 | tf_op jit(solution)/shard_map/all_to_all | solution.py:119
  168.0 5.1 all-to-all-start.1
  177.3 13.5 %copy.102 = f32[2,1,96,8,1080]{4,2,0,3,1:T(8,128)} copy(f32[2,1,96,8,1080]{2,0,4,3,1:T(2,128)} %bitcast.29) | data formatting | bytes 13271040 | tf_op jit(solution)/shard_map/all_to_all | solution.py:119
  190.8 81.3 %all-to-all-done.1 = f32[2,1,96,8640]{2,0,1,3:T(2,128)} async-done(((f32[2,1,96,8640]{2,0,1,3:T(2,128)}), f32[2,1,96,8640]{2,0,1,3:T(2,128)}, u32[]{:S(2)}, u32[]{:S(2)}) %all-to-all-start.1) | async-done | bytes 6635552 | tf_op jit(solution)/shard_map/all_to_all | solution.py:118
  272.1 13.5 %copy.107 = f32[2,1,96,8,1080]{4,2,0,3,1:T(8,128)} copy(f32[2,1,96,8,1080]{2,0,4,3,1:T(2,128)} %bitcast.43) | data formatting | bytes 13271040 | tf_op jit(solution)/shard_map/all_to_all | solution.py:118
  285.6 9.7 %fusion.43 = f32[8,2,96,1080,1]{3,2,4,1,0:T(8,128)S(1)} fusion(f32[2,1,96,8,1080]{4,2,0,3,1:T(8,128)} %copy.107, f32[8,1,96,2,96]{2,4,1,3,0:T(8,128)S(1)} %get-tuple-element.36, f32[8,1,96,2,96]{2,4,1,3,0:T(8,128)S(1)} %get-tuple-element.35), kind=kOutput, calls=%fused_computation.44 | convolution fusion | flops 3822354432 | bytes 14450688 | tf_op jit(solution)/shard_map/psbir,bpiqj->qsbjr/dot_general | solution.py:45
  295.4 11.7 %fusion.121 = (f32[2,8,96]{2,0,1:T(2,128)S(1)}, f32[2,1,8,96,1080]{4,3,0,2,1:T(8,128)S(1)}) fusion(f32[2,8,96]{2,0,1:T(2,128)S(1)} %copy.109, f32[2,8,96]{2,0,1:T(2,128)S(1)} %copy.108, f32[8,2,96,1080,1]{3,2,4,1,0:T(8,128)S(1)} %fusion.43, f32[8,1,96,2,96]{2,4,1,3,0:T(8,128)S(1)} %copy-done.5, f32[8,1,96,2,96]{2,4,1,3,0:T(8,128)S(1)} %copy-done.4, ...), kind=kOutput, calls=%fused_computation.153 | convolution fusion | flops 3845577216 | bytes 21104640 | tf_op jit(solution)/shard_map/psbir,bpiqj->qsbjr/dot_general | solution.py:45
  309.9 12.7 %fusion.31 = f32[8,2,96,2,96]{4,2,3,1,0:T(8,128)} fusion(f32[2,1,8,96,1080]{4,3,0,2,1:T(8,128)S(1)} %get-tuple-element.53, f32[8,2,96,1080,1]{3,2,4,1,0:T(8,128)S(1)} %fusion.43, f32[2,8,96]{2,0,1:T(2,128)S(1)} %copy.108), kind=kOutput, calls=%fused_computation.32 | convolution fusion | flops 3836989440 | bytes 14456832 | tf_op jit(solution)/shard_map/psbir,qsbjr->bpiqj/dot_general | solution.py:53
  322.6 15.4 %fusion.122 = (f32[2,8,96]{2,0,1:T(2,128)S(1)}, f32[2,1,8,96,1080]{4,3,0,2,1:T(8,128)S(1)}) fusion(f32[2,8,96]{2,0,1:T(2,128)S(1)} %copy.108, f32[8,2,96,1080,1]{3,2,4,1,0:T(8,128)S(1)} %fusion.43, f32[2,1,8,96,1080]{4,3,0,2,1:T(8,128)} %copy-done.13, f32[8,1,96,2,96]{2,4,1,3,0:T(8,128)} %get-tuple-element.34, f32[8,1,96,2,96]{2,4,1,3,0:T(8,128)S(1)} %copy-done.4), kind=kOutput, calls=%fused_computation.154 | convolution fusion | flops 3855530496 | bytes 21098496 | tf_op jit(solution)/shard_map/qsbjr,bpiqj->psbir/dot_general | solution.py:49
  338.1 8.6 %fusion.33 = f32[8,2,96,2,96]{4,2,3,1,0:T(8,128)S(1)} fusion(f32[2,1,96,8,1080]{4,2,0,3,1:T(8,128)S(1)} %bitcast.258, f32[2,1,8,96,1080]{4,3,0,2,1:T(8,128)S(1)} %get-tuple-element.55), kind=kOutput, calls=%fused_computation.34 | convolution fusion | flops 3822059520 | bytes 14450688 | tf_op jit(solution)/shard_map/psbir,qsbjr->bpiqj/dot_general | solution.py:53
  355.4 56.3 %all-reduce.6.cloned.1.call-done = f32[297984]{0:T(1024)} async-done(((f32[297984]{0:T(1024)}), f32[297984]{0:T(1024)}) %all-reduce.6.cloned.1.call-update) | async-done | bytes 1191952
  413.5 35.1 %all-reduce.4.cloned.1.call-done = f32[37248]{0:T(1024)} async-done(((f32[37248]{0:T(1024)}), f32[37248]{0:T(1024)}) %all-reduce.4.cloned.1.call-update) | async-done | bytes 149008 | tf_op jit(solution)/shard_map/psum | solution.py:134
  450.3 9.9 %fusion.47 = f32[2,1,8,96,1080]{4,3,0,2,1:T(8,128)S(1)} fusion(f32[2,1,8,96,1080]{4,3,0,2,1:T(8,128)} %copy-done, f32[8,1,96,2,96]{2,4,1,3,0:T(8,128)S(1)} %get-tuple-element.36, f32[8,1,96,2,96]{2,4,1,3,0:T(8,128)S(1)} %get-tuple-element.35), kind=kOutput, calls=%fused_computation.48 | convolution fusion | flops 3822354432 | bytes 14450688 | tf_op jit(solution)/shard_map/qsbjr,bpiqj->psbir/dot_general | solution.py:49
  460.2 3.4 copy.112
  463.6 11.4 %copy.113 = f32[2,1,768,1080]{3,0,1,2:T(2,128)} copy(f32[2,1,768,1080]{3,2,0,1:T(8,128)} %bitcast.261) | data formatting | bytes 13271040 | tf_op jit(solution)/shard_map/reshape | solution.py:83
  475.0 5.2 all-to-all-start.2
  486.3 74.0 %all-to-all-done.2 = f32[2,1,768,1080]{3,0,1,2:T(2,128)} async-done(((f32[2,1,768,1080]{3,0,1,2:T(2,128)}), f32[2,1,768,1080]{3,0,1,2:T(2,128)}, u32[]{:S(2)}, u32[]{:S(2)}) %all-to-all-start.2) | async-done | bytes 6635552 | tf_op jit(solution)/shard_map/all_to_all | solution.py:124
  560.2 3.5 copy.114
  563.7 7.1 %copy.156 = f32[2,1,96,8,1080]{4,3,0,2,1:T(8,128)} copy(f32[2,1,96,8,1080]{4,2,3,0,1:T(8,128)S(1)} %bitcast.262) | data formatting | bytes 13271040 | tf_op jit(solution)/shard_map/reshape.40
  570.8 10.7 %reshape.678 = f32[2,96,96,90,1]{3,2,0,1,4:T(8,128)} reshape(f32[2,1,96,8,1080]{4,3,0,2,1:T(8,128)} %copy.156) | data formatting | bytes 13271040 | tf_op jit(solution)/shard_map/reshape.40
  581.5 13.5 %convolution_bitcast_fusion = f32[2,96,96,90]{2,3,1,0:T(8,128)S(1)} fusion(f32[2,96,96,90,1]{3,2,0,1,4:T(8,128)} %reshape.678, f32[1,90,2,90]{1,3,2,0:T(8,128)S(1)} %copy-done.7, f32[1,90,2,90]{1,3,2,0:T(8,128)S(1)} %copy-done.6), kind=kOutput, calls=%fused_computation.51 | convolution fusion | flops 3583213056 | bytes 13400640 | tf_op jit(solution)/shard_map/psckm,pmqh->qsckh/dot_general | solution.py:128
  594.9 15.3 %fusion.62 = f32[1,96,90,180]{1,3,2,0:T(8,128)S(1)} fusion(f32[2,96,96,90]{2,3,1,0:T(8,128)S(1)} %convolution_bitcast_fusion, f32[1,96,180]{1,2,0:T(8,128)S(1)} %get-tuple-element.46, f32[1,96,180]{1,2,0:T(8,128)S(1)} %get-tuple-element.45), kind=kOutput, calls=%fused_computation.54 | convolution fusion | flops 3583215360 | bytes 12994560 | tf_op jit(solution)/shard_map/qsckh,qkw->schw/dot_general | solution.py:126
  610.3 9.7 %copy.125 = f32[1,96,90,180]{1,0,3,2:T(1,128)} copy(f32[1,96,90,180]{1,3,2,0:T(8,128)S(1)} %fusion.62) | data formatting | bytes 12441600
  (80 shorter events, 26.0 us)
Async XLA Ops:
  7.2 0.5 copy-start.10
  63.1 104.9 %all-to-all-start = ((f32[2,1,96,8640]{2,0,1,3:T(2,128)}), f32[2,1,96,8640]{2,0,1,3:T(2,128)}, u32[]{:S(2)}, u32[]{:S(2)}) async-start(f32[2,1,96,8640]{2,0,1,3:T(2,128)} %bitcast.260), calls=%async_computation | async-start | bytes 17694720 | tf_op jit(solution)/shard_map/all_to_all | solution.py:119
  168.0 5.7 copy-start.8
  168.0 5.7 copy-start.9
  168.0 5.7 copy-start.3
  168.0 104.1 %all-to-all-start.1 = ((f32[2,1,96,8640]{2,0,1,3:T(2,128)}), f32[2,1,96,8640]{2,0,1,3:T(2,128)}, u32[]{:S(2)}, u32[]{:S(2)}) async-start(f32[2,1,96,8640]{2,0,1,3:T(2,128)} %bitcast.259), calls=%async_computation.1 | async-start | bytes 17694720 | tf_op jit(solution)/shard_map/all_to_all | solution.py:118
  173.1 238.6 %all-reduce.6.cloned.1.call-start = ((), (), s32[]{:S(2)}) async-start(), calls=%async_computation.5 | async-start | bytes 2383872
  285.6 9.8 %copy-start.1 = (f32[2,1,96,8,1080]{4,2,0,3,1:T(8,128)S(1)}, f32[2,1,96,8,1080]{4,2,0,3,1:T(8,128)}, u32[]{:S(2)}) copy-start(f32[2,1,96,8,1080]{4,2,0,3,1:T(8,128)} %copy.102) | copy-start | bytes 19906564
  285.6 9.8 %copy-start.4 = (f32[8,1,96,2,96]{2,4,1,3,0:T(8,128)S(1)}, f32[8,1,96,2,96]{2,4,1,3,0:T(8,128)}, u32[]{:S(2)}) copy-start(f32[8,1,96,2,96]{2,4,1,3,0:T(8,128)} %get-tuple-element.33) | copy-start | bytes 1769476
  285.6 9.8 %copy-start.5 = (f32[8,1,96,2,96]{2,4,1,3,0:T(8,128)S(1)}, f32[8,1,96,2,96]{2,4,1,3,0:T(8,128)}, u32[]{:S(2)}) copy-start(f32[8,1,96,2,96]{2,4,1,3,0:T(8,128)} %get-tuple-element.34) | copy-start | bytes 1769476
  307.1 2.9 copy-start.13
  309.9 28.1 %slice-start = ((s8[7077888]{0:T(1024)(128)(4,1)}), s8[4194304]{0:T(1024)(128)(4,1)S(1)}, s32[]{:S(2)}) async-start(s8[7077888]{0:T(1024)(128)(4,1)} %bitcast.257), calls=%async_computation.6 | async-start | bytes 8388608
  322.6 15.5 %slice-start.1 = ((s8[7077888]{0:T(1024)(128)(4,1)}), s8[2883584]{0:T(1024)(128)(4,1)S(1)}, s32[]{:S(2)}) async-start(s8[7077888]{0:T(1024)(128)(4,1)} %bitcast.257), calls=%async_computation.7 | async-start | bytes 5767168
  338.0 8.7 %copy-start = (f32[2,1,8,96,1080]{4,3,0,2,1:T(8,128)}, f32[2,1,8,96,1080]{4,3,0,2,1:T(8,128)S(1)}, u32[]{:S(2)}) copy-start(f32[2,1,8,96,1080]{4,3,0,2,1:T(8,128)S(1)} %get-tuple-element.55) | copy-start | bytes 19906564
  338.1 9.5 %copy-start.2 = (f32[8,2,96,2,96]{4,2,3,1,0:T(8,128)S(1)}, f32[8,2,96,2,96]{4,2,3,1,0:T(8,128)}, u32[]{:S(2)}) copy-start(f32[8,2,96,2,96]{4,2,3,1,0:T(8,128)} %fusion.31) | copy-start | bytes 3538948
  346.7 7.4 %copy-start.12 = (u32[32]{0:T(128)S(1)}, u32[32]{0:T(128)}, u32[]{:S(2)}) copy-start(u32[32]{0:T(128)} %constant.64) | copy-start | bytes 388
  354.1 94.5 %all-reduce.4.cloned.1.call-start = ((), (), s32[]{:S(2)}) async-start(), calls=%async_computation.3 | async-start | bytes 303104 | tf_op jit(solution)/shard_map/psum | solution.py:134
  413.4 67.3 %all-gather.3.cloned.1.call-start = ((), (), s32[]{:S(2)}) async-start(), calls=%async_computation.4 | async-start | bytes 1340928 | tf_op jit(solution)/shard_map/all_gather | solution.py:135
  475.0 5.2 copy-start.11
  475.0 85.2 %all-to-all-start.2 = ((f32[2,1,768,1080]{3,0,1,2:T(2,128)}), f32[2,1,768,1080]{3,0,1,2:T(2,128)}, u32[]{:S(2)}, u32[]{:S(2)}) async-start(f32[2,1,768,1080]{3,0,1,2:T(2,128)} %copy.113), calls=%async_computation.2 | async-start | bytes 14155776 | tf_op jit(solution)/shard_map/all_to_all | solution.py:124
  570.8 10.7 %copy-start.6 = (f32[1,90,2,90]{1,3,2,0:T(8,128)S(1)}, f32[1,90,2,90]{1,3,2,0:T(8,128)}, u32[]{:S(2)}) copy-start(f32[1,90,2,90]{1,3,2,0:T(8,128)} %get-tuple-element.37) | copy-start | bytes 194404
  570.8 10.7 %copy-start.7 = (f32[1,90,2,90]{1,3,2,0:T(8,128)S(1)}, f32[1,90,2,90]{1,3,2,0:T(8,128)}, u32[]{:S(2)}) copy-start(f32[1,90,2,90]{1,3,2,0:T(8,128)} %get-tuple-element.42) | copy-start | bytes 194404
Sparse Core Ops, SparseCore 0:
  354.2 57.4 all-reduce.5
  414.7 33.8 all-reduce.3
  451.0 24.1 all-gather.2
where the time goes:
time: 637 us; the launch traced here: 627 us
  waiting for transfers between devices  292 us (46%)
  matrix products  156 us (24%)
  local copies, waits for them, and re-layouts  139 us (22%)
  starting transfers between devices  16.4 us (3%)
  between operations  15 us (2%)
  other arithmetic  8.95 us (1%)
    all_to_all x1, waiting for transfers between devices, on_device(): lax.all_to_all(x_both.reshape(flat_shape), 'lon', split_axis=3, concat_ax...  81.3 us
    all_to_all x1, waiting for transfers between devices, on_device(): lax.all_to_all(d_stack, 'lon', split_axis=2, concat_axis=3, tiled=True)  74 us
    unnamed x4, waiting for transfers between devices  56.4 us
    all_to_all x1, waiting for transfers between devices, on_device(): lax.all_to_all(g_both.reshape(flat_shape), 'lon', split_axis=3, concat_ax...  45.2 us
    another operation x4, local copies, waits for them, and re-layouts  42.5 us
    psum x1, waiting for transfers between devices, on_device(): summed = lax.psum(share, 'lat')  35.1 us
    dot_general x2, matrix products, lon_forward(): return jnp.einsum('schw,wqk->qsckh', data, table, precision=HIGHEST)  29.7 us
    dot_general x2, matrix products, lat_forward(): return jnp.einsum('psckh,phqm->qsckm', data, lat_table, precision=HIGHEST)  29.1 us
  transfers between devices with their start and end apart: 6, of which 5 were waited for; matrix products, arithmetic and copies ran while one was open for 16% of the time, Pallas kernels for 0%

commit v1 on v0

v1 whole, which is shorter than its diff:
```python
import math

import jax
import jax.numpy as jnp
from jax import lax
from jax.sharding import PartitionSpec as P

SHRINK = 0.01
GELU_SCALE = math.sqrt(2.0 / math.pi)
GELU_CUBE = 0.044715
PREC = lax.Precision.HIGH


def tables(length, count, limit):
    first = jnp.arange(length, dtype=jnp.int32)[:, None]
    second = jnp.arange(count, dtype=jnp.int32)[None, :]
    angle = 2.0 * math.pi / length * (first * second % length).astype(jnp.float32)
    keeper = (second < limit).astype(jnp.float32) / math.sqrt(length)
    return (jnp.cos(angle) * keeper, jnp.sin(angle) * keeper)


def cotangent_weight(length, count):
    index = jnp.arange(count, dtype=jnp.int32)
    edge = (index == 0) | (2 * index == length)
    return jnp.where(edge, 1.0, 2.0).astype(jnp.float32)


def gelu_slope(value):
    inner = GELU_SCALE * (value + GELU_CUBE * value * value * value)
    tangent = jnp.tanh(inner)
    return 0.5 * (1.0 + tangent) + 0.5 * value * (1.0 - tangent * tangent) * GELU_SCALE * (
        1.0 + 3.0 * GELU_CUBE * value * value
    )


def complex_matrix(weight):
    real_part = weight[0]
    imag_part = weight[1]
    upper = jnp.stack([real_part, imag_part], axis=1)
    lower = jnp.stack([-imag_part, real_part], axis=1)
    return jnp.stack([upper, lower], axis=0)


def forward_mix(left, matrix):
    return jnp.einsum("psir,piqj->qsjr", left, matrix, precision=PREC)


def back_mix(left, matrix):
    return jnp.einsum("qsjr,piqj->psir", left, matrix, precision=PREC)


def weight_grad(left, right):
    total = jnp.einsum("psir,qsjr->piqj", left, right, precision=PREC)
    return jnp.stack(
        [total[0, :, 0, :] + total[1, :, 1, :], total[0, :, 1, :] - total[1, :, 0, :]]
    )


def bias_view(vector):
    return vector[:, None, :, None]


def block_backward(x_both, g_both, first_weight, first_bias, second_weight, second_bias):
    first_matrix = complex_matrix(first_weight)
    second_matrix = complex_matrix(second_weight)
    a_both = forward_mix(x_both, first_matrix) + bias_view(first_bias)
    o_both = jax.nn.gelu(a_both, approximate=True)
    z_both = forward_mix(o_both, second_matrix) + bias_view(second_bias)
    e_both = g_both * jnp.tanh(z_both / SHRINK) ** 2
    grad_w_two = weight_grad(o_both, e_both)
    grad_b_two = jnp.sum(e_both, axis=(1, 3))
    s_both = back_mix(e_both, second_matrix) * gelu_slope(a_both)
    grad_w_one = weight_grad(x_both, s_both)
    grad_b_one = jnp.sum(s_both, axis=(1, 3))
    d_both = back_mix(s_both, first_matrix)
    return d_both, (grad_w_one, grad_b_one, grad_w_two, grad_b_two)


def on_device(layer_input, grad_output, first_weight, first_bias, second_weight, second_bias):
    lon_count = lax.axis_size("lon")
    samples, local_ch, lat_rows, lon_cols = layer_input.shape
    blocks, width = first_weight.shape[1], first_weight.shape[2]
    group = width // local_ch
    groups = [list(range(at, at + group)) for at in range(0, lon_count, group)]
    block = lax.axis_index("lon") // group
    kept_freqs = lon_cols // 2 + 1
    freq_slots = -(-kept_freqs // group) * group
    lon_cos, lon_sin = tables(lon_cols, freq_slots, kept_freqs)
    factor_row = cotangent_weight(lon_cols, freq_slots)[None, :]
    lon_table = jnp.stack([lon_cos, -lon_sin], axis=1)
    cot_table = jnp.stack([lon_cos * factor_row, -lon_sin * factor_row], axis=1)
    lon_back = jnp.stack([lon_cos.T, -lon_sin.T])
    lat_cos, lat_sin = tables(lat_rows, lat_rows, lat_rows)
    lat_table = jnp.stack(
        [jnp.stack([lat_cos, -lat_sin], axis=1), jnp.stack([lat_sin, lat_cos], axis=1)]
    )
    lat_back = jnp.stack(
        [jnp.stack([lat_cos, lat_sin], axis=1), jnp.stack([-lat_sin, lat_cos], axis=1)]
    )

    def spectrum(data, table):
        half = jnp.einsum("schw,wqk->qsckh", data, table, precision=PREC)
        full = jnp.einsum("psckh,phqm->qsckm", half, lat_table, precision=PREC)
        return full.reshape((2, samples, local_ch, freq_slots * lat_rows))

    def share(data, split, concat):
        if group == 1:
            return data
        return lax.all_to_all(
            data, "lon", split_axis=split, concat_axis=concat, axis_index_groups=groups, tiled=True
        )

    x_modes = share(spectrum(layer_input, lon_table), 3, 2)
    g_modes = share(spectrum(grad_output, cot_table), 3, 2)

    def mine(weight):
        return lax.dynamic_index_in_dim(weight, block, axis=1, keepdims=False)

    d_modes, partial_grads = block_backward(
        x_modes, g_modes, mine(first_weight), mine(first_bias), mine(second_weight), mine(second_bias)
    )
    flat_grads = jnp.concatenate([piece.reshape(-1) for piece in partial_grads])
    summed = lax.psum(flat_grads, "lat")
    if group > 1:
        summed = lax.psum(summed, "lon", axis_index_groups=groups)
    whole = lax.all_gather(summed, "lon", axis=0, tiled=False)[::group]
    stacked = share(d_modes, 2, 3)
    shape_five = (2, samples, local_ch, freq_slots, lat_rows)
    grad_input = jnp.einsum(
        "qsckh,qkw->schw",
        jnp.einsum("psckm,pmqh->qsckh", stacked.reshape(shape_five), lat_back, precision=PREC),
        lon_back,
        precision=PREC,
    )
    results = []
    offset = 0
    for piece in partial_grads:
        part = whole[:, offset : offset + piece.size].reshape((blocks,) + piece.shape)
        results.append(jnp.moveaxis(part, 0, 1))
        offset = offset + piece.size
    grad_w_one, grad_b_one, grad_w_two, grad_b_two = results
    return (grad_input, grad_w_one, grad_b_one, grad_w_two, grad_b_two)


def solution(mesh):
    placed = (P("lat", "lon", None, None), P("lat", "lon", None, None), P(), P(), P(), P())
    return jax.shard_map(
        on_device,
        mesh=mesh,
        in_specs=placed,
        out_specs=(P("lat", "lon", None, None), P(), P(), P(), P()),
        check_vma=False,
    )
```

time: 637 us -> 255 us (0.40)
  waiting for transfers between devices: 292 us -> 37.1 us
  local copies, waits for them, and re-layouts: 139 us -> 84.4 us
  matrix products: 156 us -> 108 us
  starting transfers between devices: 16.4 us -> 0.08 us
    all_to_all x3 -> x0, waiting for transfers between devices: 200 us -> none  [the longest x1 81.3 us: on_device(): lax.all_to_all(x_both.reshape(flat_shape), 'lon', split_axis=3, concat_ax...]
    unnamed x4 -> x2, waiting for transfers between devices: 56.4 us -> 0.03 us
    dot_general x10, matrix products: 127 us -> 94.3 us  [the longest x2 24.5 us: back_mix(): return jnp.einsum('qsjr,piqj->psir', left, matrix, precision=PREC)]
    all_to_all x3 -> x0, local copies, waits for them, and re-layouts: 30.5 us -> none  [the longest x1 13.5 us: on_device(): lax.all_to_all(g_both.reshape(flat_shape), 'lon', split_axis=3, concat_ax...]
    reshape x7 -> x6, local copies, waits for them, and re-layouts: 39.8 us -> 18.5 us  [the longest x2 17.8 us: spectrum(): return full.reshape((2, samples, local_ch, freq_slots * lat_rows))]
    dot_general x0 -> x1, local copies, waits for them, and re-layouts: none -> 17.9 us  [back_mix(): return jnp.einsum('qsjr,piqj->psir', left, matrix, precision=PREC)]
    all_to_all x3 -> x0, starting transfers between devices: 15.8 us -> none  [the longest x1 5.51 us: on_device(): lax.all_to_all(g_both.reshape(flat_shape), 'lon', split_axis=3, concat_ax...]
    another operation x4 -> x3, local copies, waits for them, and re-layouts: 42.5 us -> 30.3 us
  transfers between devices with their start and end apart: 6 -> 2, of which waited for: 5 -> 1; matrix products, arithmetic and copies ran while one was open for 16% -> 21% of each run, Pallas kernels for 0% -> 0%
where the time goes in v1:
time: 255 us; the launch traced here: 251 us
  matrix products  108 us (42%)
  local copies, waits for them, and re-layouts  84.4 us (33%)
  waiting for transfers between devices  37.1 us (15%)
  between operations  14.6 us (6%)
  other arithmetic  6.14 us (2%)
    psum x1, waiting for transfers between devices, on_device(): summed = lax.psum(flat_grads, 'lat')  37.1 us
    another operation x3, local copies, waits for them, and re-layouts  30.3 us
    dot_general x2, matrix products, back_mix(): return jnp.einsum('qsjr,piqj->psir', left, matrix, precision=PREC)  24.5 us
    dot_general x2, matrix products, spectrum(): half = jnp.einsum('schw,wqk->qsckh', data, table, precision=PREC)  22.1 us
    dot_general x2, matrix products, spectrum(): full = jnp.einsum('psckh,phqm->qsckm', half, lat_table, precision=PREC)  18.8 us
    dot_general x1, local copies, waits for them, and re-layouts, back_mix(): return jnp.einsum('qsjr,piqj->psir', left, matrix, precision=PREC)  17.9 us
    reshape x2, local copies, waits for them, and re-layouts, spectrum(): return full.reshape((2, samples, local_ch, freq_slots * lat_rows))  17.8 us
    dot_general x2, matrix products, weight_grad(): total = jnp.einsum('psir,qsjr->piqj', left, right, precision=PREC)  15.3 us
  transfers between devices with their start and end apart: 2, of which 1 were waited for; matrix products, arithmetic and copies ran while one was open for 21% of the time, Pallas kernels for 0%

profile of v1, /device:TPU:0, one launch (start us, length us, event | category | flops | bytes accessed | tf_op | source)
XLA Modules:
  0.0 250.5 jit_solution(10574886828943491357)
XLA Ops:
  7.2 0.9 constant_dynamic-slice_fusion.4
  8.3 0.4 broadcast_multiply_fusion.1
  8.8 11.1 %fusion.64 = f32[2,96,91,90]{1,2,3,0:T(8,128)} fusion(f32[1,96,90,180]{1,0,3,2:T(1,128)} %param.6, f32[180,1,91]{2,0,1:T(8,128)S(1)} %get-tuple-element.49, f32[180,1,91]{2,0,1:T(8,128)S(1)} %get-tuple-element.48), kind=kOutput, calls=%fused_computation.64 | convolution fusion | flops 1698311168 | bytes 12641760 | tf_op jit(solution)/shard_map/schw,wqk->qsckh/dot_general | solution.py:102
  19.8 10.7 %copy.49 = f32[2,96,91,90]{3,1,0,2:T(8,128)} copy(f32[2,96,91,90]{1,2,3,0:T(8,128)} %fusion.64) | data formatting | bytes 12579840 | tf_op jit(solution)/shard_map/reshape.31
  30.7 9.4 %fusion.55 = f32[2,1,96,91,90]{2,4,3,0,1:T(8,128)} fusion(f32[2,96,91,90]{3,1,0,2:T(8,128)} %copy.49, f32[1,90,2,90]{1,3,0,2:T(8,128)S(1)} %get-tuple-element.35, f32[1,90,2,90]{1,3,0,2:T(8,128)S(1)} %get-tuple-element.38), kind=kOutput, calls=%fused_computation.61 | convolution fusion | flops 1698310784 | bytes 12709440 | tf_op jit(solution)/shard_map/psckh,phqm->qsckm/dot_general | solution.py:103
  40.2 9.2 %reshape.710 = f32[2,96,8190]{1,2,0:T(8,128)} reshape(f32[2,1,96,91,90]{2,4,3,0,1:T(8,128)} %fusion.55) | data formatting | bytes 12579840 | tf_op jit(solution)/shard_map/reshape.33
  49.5 11.1 %fusion.61 = f32[2,96,91,90]{1,2,3,0:T(8,128)} fusion(f32[1,96,90,180]{1,0,3,2:T(1,128)} %param.7, f32[180,1,91]{2,0,1:T(8,128)S(1)} %get-tuple-element.45, f32[180,1,91]{2,0,1:T(8,128)S(1)} %get-tuple-element.44), kind=kOutput, calls=%fused_computation.63 | convolution fusion | flops 1698311168 | bytes 12641760 | tf_op jit(solution)/shard_map/schw,wqk->qsckh/dot_general | solution.py:102
  60.6 10.5 %copy.47 = f32[2,96,91,90]{3,1,0,2:T(8,128)} copy(f32[2,96,91,90]{1,2,3,0:T(8,128)} %fusion.61) | data formatting | bytes 12579840 | tf_op jit(solution)/shard_map/reshape.22
  71.1 9.4 %fusion.52 = f32[2,1,96,91,90]{2,4,3,0,1:T(8,128)} fusion(f32[2,96,91,90]{3,1,0,2:T(8,128)} %copy.47, f32[1,90,2,90]{1,3,0,2:T(8,128)S(1)} %get-tuple-element.35, f32[1,90,2,90]{1,3,0,2:T(8,128)S(1)} %get-tuple-element.38), kind=kOutput, calls=%fused_computation.60 | convolution fusion | flops 1698310784 | bytes 12709440 | tf_op jit(solution)/shard_map/psckh,phqm->qsckm/dot_general | solution.py:103
  80.5 9.0 %reshape.708 = f32[2,96,8190]{1,2,0:T(8,128)} reshape(f32[2,1,96,91,90]{2,4,3,0,1:T(8,128)} %fusion.52) | data formatting | bytes 12579840 | tf_op jit(solution)/shard_map/reshape | solution.py:104
  89.5 8.7 %copy.82 = f32[2,96,8190]{2,1,0:T(8,128)} copy(f32[2,96,8190]{1,2,0:T(8,128)} %reshape.708) | data formatting | bytes 12579840 | tf_op jit(solution)/shard_map/reshape | solution.py:104
  98.2 0.7 constant_dynamic-slice_fusion.2
  99.0 7.4 %fusion.24 = f32[2,96,8190,1]{2,1,3,0:T(8,128)S(1)} fusion(f32[2,96,8190]{1,2,0:T(8,128)} %reshape.710, f32[1,96,2,96]{1,3,0,2:T(8,128)S(1)} %get-tuple-element.43, f32[1,96,2,96]{1,3,0,2:T(8,128)S(1)} %get-tuple-element.42), kind=kOutput, calls=%fused_computation.30 | convolution fusion | flops 1811533824 | bytes 12727296 | tf_op jit(solution)/shard_map/psir,piqj->qsjr/dot_general | solution.py:45
  106.4 6.3 %fusion.125 = (f32[2,96]{1,0:T(2,128)S(1)}, f32[2,96,8190]{2,1,0:T(8,128)S(1)}) fusion(f32[2,96,8190]{2,1,0:T(8,128)S(1)} %bitcast.225, f32[2,96]{1,0:T(2,128)S(1)} %bitcast.241, f32[2,96]{1,0:T(2,128)S(1)} %bitcast.237, f32[2,96,8190,1]{2,1,3,0:T(8,128)S(1)} %fusion.24, f32[1,96,2,96]{1,3,0,2:T(8,128)S(1)} %get-tuple-element.41, ...), kind=kOutput, calls=%fused_computation.166 | convolution fusion | flops 1833548288 | bytes 19019520 | tf_op jit(solution)/shard_map/psir,piqj->qsjr/dot_general | solution.py:45
  112.7 5.2 %fusion.45 = f32[2,96,2,96]{3,1,2,0:T(8,128)S(1)} fusion(f32[2,96,8190]{2,1,0:T(8,128)S(1)} %get-tuple-element.56, f32[2,96,8190,1]{2,1,3,0:T(8,128)S(1)} %fusion.24, f32[2,96]{1,0:T(2,128)S(1)} %bitcast.238), kind=kOutput, calls=%fused_computation.51 | convolution fusion | flops 1825649280 | bytes 12728064 | tf_op jit(solution)/shard_map/psir,qsjr->piqj/dot_general | solution.py:53
  118.2 14.2 %fusion.38 = (f32[8190,96,2]{0,1,2:T(8,128)}, f32[2,96,8190,1]{2,1,0,3:T(8,128)S(1)}) fusion(f32[2,96,8190,1]{2,1,3,0:T(8,128)} %copy-done, f32[96,2]{0,1:T(2,128)S(1)} %bitcast.239, f32[2,96,8190]{2,1,0:T(8,128)} %copy-done.1, f32[1,96,2,96]{1,3,0,2:T(8,128)S(1)} %get-tuple-element.41, f32[1,96,2,96]{1,3,0,2:T(8,128)S(1)} %get-tuple-element.40), kind=kOutput, calls=%fused_computation.44 | convolution fusion | flops 1841410944 | bytes 25307904 | tf_op jit(solution)/shard_map/qsjr,piqj->psir/dot_general | solution.py:49
  132.4 4.9 %fusion.121 = (f32[2,96]{1,0:T(2,128)S(1)}, f32[2,96,8190]{2,1,0:T(8,128)S(1)}) fusion(f32[2,96]{1,0:T(2,128)S(1)} %bitcast.240, f32[2,96,8190,1]{2,1,3,0:T(8,128)S(1)} %bitcast.223, f32[2,96,8190,1]{2,1,0,3:T(8,128)S(1)} %get-tuple-element.54), kind=kLoop, calls=%fused_computation.163 | loop fusion | flops 31449408 | bytes 18871296 | tf_op jit(solution)/shard_map/reduce_sum | solution.py:74
  137.3 10.0 %fusion.22 = f32[2,96,2,96]{3,1,2,0:T(8,128)S(1)} fusion(f32[2,96,8190]{1,2,0:T(8,128)} %reshape.710, f32[2,96,8190]{2,1,0:T(8,128)S(1)} %get-tuple-element.21), kind=kOutput, calls=%fused_computation.28 | convolution fusion | flops 1811496960 | bytes 12727296 | tf_op jit(solution)/shard_map/psir,qsjr->piqj/dot_general | solution.py:53
  147.8 0.8 all_gather.6
  148.7 37.1 %all-reduce.2.cloned.1.call-done = f32[1,37248]{1,0:T(1,128)} async-done(((f32[1,37248]{1,0:T(1,128)}), f32[1,37248]{1,0:T(1,128)}) %all-reduce.2.cloned.1.call-update) | async-done | bytes 149008 | tf_op jit(solution)/shard_map/psum | solution.py:123
  185.8 17.9 %dot_general.70 = f32[91,90,96,2]{1,0,2,3:T(8,128)} reshape(f32[8190,96,2]{0,1,2:T(8,128)} %get-tuple-element.53) | data formatting | bytes 12579840 | tf_op jit(solution)/shard_map/qsjr,piqj->psir/dot_general | solution.py:49
  203.7 0.4 cosine_multiply_fusion
  204.1 10.2 %fusion.7 = f32[2,96,91,90,1]{3,1,0,4,2:T(8,128)S(1)} fusion(f32[91,90,96,2,1]{1,0,2,3,4:T(8,128)} %bitcast.221, f32[1,96,2,96]{1,3,0,2:T(8,128)S(1)} %get-tuple-element.43, f32[1,96,2,96]{1,3,0,2:T(8,128)S(1)} %get-tuple-element.42), kind=kOutput, calls=%fused_computation.13 | convolution fusion | flops 1811533824 | bytes 12727296 | tf_op jit(solution)/shard_map/qsjr,piqj->psir/dot_general | solution.py:49
  214.3 4.8 %fusion.58 = f32[2,96,91,90]{1,3,2,0:T(8,128)S(1)} fusion(f32[2,96,91,90,1]{3,1,0,4,2:T(8,128)S(1)} %fusion.7, f32[1,90,2,90]{1,3,2,0:T(8,128)S(1)} %get-tuple-element.39, f32[1,90,2,90]{1,3,2,0:T(8,128)S(1)} %get-tuple-element.34), kind=kOutput, calls=%fused_computation.62 | convolution fusion | flops 1698310784 | bytes 12709440 | tf_op jit(solution)/shard_map/psckm,pmqh->qsckh/dot_general | solution.py:131
  219.1 9.1 %fusion.67 = f32[1,96,90,180]{1,3,2,0:T(8,128)S(1)} fusion(f32[2,96,91,90]{1,3,2,0:T(8,128)S(1)} %fusion.58, f32[1,91,180]{1,2,0:T(8,128)S(1)} %get-tuple-element.47, f32[1,91,180]{1,2,0:T(8,128)S(1)} %get-tuple-element.46), kind=kOutput, calls=%fused_computation.65 | convolution fusion | flops 1698311168 | bytes 12641760 | tf_op jit(solution)/shard_map/qsckh,qkw->schw/dot_general | solution.py:129
  228.2 9.7 %copy.56 = f32[1,96,90,180]{1,0,3,2:T(1,128)} copy(f32[1,96,90,180]{1,3,2,0:T(8,128)S(1)} %fusion.67) | data formatting | bytes 12441600
  237.9 1.4 copy.118
  239.6 0.3 reshape.677
  239.9 0.9 copy.57
  241.1 0.9 copy.59
  242.2 0.6 copy.58
  242.8 0.6 copy.60
  (45 shorter events, 2.1 us)
Async XLA Ops:
  7.2 178.6 %all-reduce.2.cloned.1.call-start = ((), (), s32[]{:S(2)}) async-start(), calls=%async_computation | async-start | bytes 297984 | tf_op jit(solution)/shard_map/psum | solution.py:123
  99.0 7.4 %slice-start.2 = ((s8[6291456]{0:T(1024)(128)(4,1)}), s8[4194304]{0:T(1024)(128)(4,1)S(1)}, s32[]{:S(2)}) async-start(s8[6291456]{0:T(1024)(128)(4,1)} %bitcast.224), calls=%async_computation.4 | async-start | bytes 8388608
  99.0 7.4 %slice-start.3 = ((s8[6291456]{0:T(1024)(128)(4,1)}), s8[2097152]{0:T(1024)(128)(4,1)S(1)}, s32[]{:S(2)}) async-start(s8[6291456]{0:T(1024)(128)(4,1)} %bitcast.224), calls=%async_computation.5 | async-start | bytes 4194304
  106.4 6.3 %copy-start = (f32[2,96,8190,1]{2,1,3,0:T(8,128)}, f32[2,96,8190,1]{2,1,3,0:T(8,128)S(1)}, u32[]{:S(2)}) copy-start(f32[2,96,8190,1]{2,1,3,0:T(8,128)S(1)} %fusion.24) | copy-start | bytes 18869764
  112.7 5.3 %copy-start.1 = (f32[2,96,8190]{2,1,0:T(8,128)}, f32[2,96,8190]{2,1,0:T(8,128)S(1)}, u32[]{:S(2)}) copy-start(f32[2,96,8190]{2,1,0:T(8,128)S(1)} %get-tuple-element.56) | copy-start | bytes 18869764
  118.0 14.4 %slice-start = ((s8[6291456]{0:T(1024)(128)(4,1)}), s8[2097152]{0:T(1024)(128)(4,1)S(1)}, s32[]{:S(2)}) async-start(s8[6291456]{0:T(1024)(128)(4,1)} %bitcast.222), calls=%async_computation.2 | async-start | bytes 4194304
  118.1 14.3 %slice-start.1 = ((s8[6291456]{0:T(1024)(128)(4,1)}), s8[4194304]{0:T(1024)(128)(4,1)S(1)}, s32[]{:S(2)}) async-start(s8[6291456]{0:T(1024)(128)(4,1)} %bitcast.222), calls=%async_computation.3 | async-start | bytes 8388608
  148.6 89.3 %all-gather.3.cloned.1.call-start = ((), (), s32[]{:S(2)}) async-start(), calls=%async_computation.1 | async-start | bytes 1340928 | tf_op jit(solution)/shard_map/all_gather | solution.py:126
Sparse Core Ops, SparseCore 0:
  148.7 36.9 all-reduce.1
  187.8 24.1 all-gather.2

commit v2 on v1

--- a/solution.py
+++ b/solution.py
@@ -1,14 +1,439 @@
+import functools
 import math
 
 import jax
 import jax.numpy as jnp
+import ml_dtypes
+import numpy as np
 from jax import lax
+from jax.experimental import pallas as pl
+from jax.experimental.pallas import tpu as pltpu
 from jax.sharding import PartitionSpec as P
 
 SHRINK = 0.01
 GELU_SCALE = math.sqrt(2.0 / math.pi)
 GELU_CUBE = 0.044715
-PREC = lax.Precision.HIGH
+PRECISION = lax.Precision.HIGH
+LANES = 128
+SUB = 8
+F32 = jnp.float32
+BF16 = jnp.bfloat16
+VMEM_LIMIT = 56 << 20
+
+
+def round_up(value, unit):
+    return -(-value // unit) * unit
+
+
+def halves(table):
+    high = table.astype(ml_dtypes.bfloat16)
+    low = (table - high.astype(np.float64)).astype(ml_dtypes.bfloat16)
+    return high, low
+
+
+def split(value):
+    high = value.astype(BF16)
+    return high, (value - high.astype(F32)).astype(BF16)
+
+
+def dot(left, right):
+    return jnp.dot(left, right, preferred_element_type=F32)
+
+
+def dot_tn(left, right):
+    return lax.dot_general(left, right, (((0,), (0,)), ((), ())), preferred_element_type=F32)
+
+
+def side_by_side(left, right):
+    return jnp.concatenate([left, right], axis=1)
+
+
+def trig(length, count):
+    first = np.arange(count)[:, None]
+    second = np.arange(length)[None, :]
+    angle = 2.0 * np.pi / length * (first * second % length)
+    return np.cos(angle) / math.sqrt(length), np.sin(angle) / math.sqrt(length)
+
+
+class Sizes:
+    def __init__(self, rows, cols):
+        self.rows, self.cols = rows, cols
+        self.pairs = rows // 2 + 1
+        self.half = round_up(self.pairs, SUB)
+        self.both = 2 * self.half
+        self.freqs = cols // 2 + 1
+        self.slots = round_up(self.freqs, 16)
+        self.row_slots = round_up(rows, 16)
+        self.col_slots = round_up(cols, 16)
+        self.band = max((n for n in range(2, 7, 2) if rows % n == 0 and n * cols % SUB == 0), default=0)
+        self.batch = max(n for n in range(1, 9) if self.freqs % n == 0)
+
+    def fits(self):
+        return self.band > 0 and self.batch * self.both % 16 == 0
+
+
+def lat_table(size, cotangent):
+    cos, sin = trig(size.rows, size.pairs)
+    if cotangent:
+        own = np.array([2 * m % size.rows == 0 for m in range(size.pairs)])
+        cos, sin = (part * np.where(own, 0.5, 1.0)[:, None] for part in (cos, sin))
+    table = np.zeros((size.both, size.row_slots))
+    table[: size.pairs, : size.rows] = cos
+    table[size.half : size.half + size.pairs, : size.rows] = sin
+    return table
+
+
+def lon_table(size, cotangent):
+    cos, sin = trig(size.cols, size.freqs)
+    if cotangent:
+        index = np.arange(size.freqs)
+        factor = np.where((index == 0) | (2 * index == size.cols), 1.0, 2.0)[:, None]
+        cos, sin = cos * factor, sin * factor
+    table = np.zeros((2 * size.slots, size.col_slots))
+    table[: size.freqs, : size.cols] = cos
+    table[size.slots : size.slots + size.freqs, : size.cols] = sin
+    return table
+
+
+def four_way(table):
+    high, low = halves(table)
+    return np.concatenate([np.concatenate([high, high], 1), np.concatenate([low, low], 1)], 0)
+
+
+def stacked(table):
+    return np.concatenate(halves(table), 0)
+
+
+def four_product(table_ref, data):
+    two = dot(table_ref[...], jnp.concatenate(split(data), axis=0))
+    count = two.shape[0] // 2
+    return two[:count] + two[count:]
+
+
+def three_product(table_ref, high, low):
+    count = table_ref.shape[0] // 2
+    two = dot(table_ref[...], high)
+    return two[:count] + two[count:] + dot(table_ref[:count], low)
+
+
+def mix(weight_ref, which, high, low):
+    return dot(high, weight_ref[which, 0]) + dot(low, weight_ref[which, 0]) + dot(high, weight_ref[which, 1])
+
+
+def gradient_kernel(
+    size, width, bands, batches, x_ref, g_ref, tx_ref, tg_ref, fx_ref, fg_ref, w_ref, b_ref,
+    s_ref, grad_ref, fold, spectra, keep, plain, total, bias_total,
+):
+    step = pl.program_id(0)
+    cols, slots, both, half = size.cols, size.slots, size.both, size.half
+    lines = 2 * slots
+    rows = size.batch * both
+
+    @pl.when(step == 0)
+    def _():
+        fold[...] = jnp.zeros_like(fold)
+        total[...] = jnp.zeros_like(total)
+        bias_total[...] = jnp.zeros_like(bias_total)
+        for which in range(2):
+            spectra[which, size.rows * lines :] = jnp.zeros(((size.row_slots - size.rows) * lines, LANES), F32)
+
+    @pl.when(step < bands)
+    def _():
+        for which, (field, table) in enumerate(((x_ref, tx_ref), (g_ref, tg_ref))):
+            data = field.reshape(size.band * cols, width)
+            for pair in range(size.band // 2):
+                slot = which * (size.band // 2) + pair
+                for i in range(2):
+                    at = (2 * pair + i) * cols
+                    high, low = split(data[at : at + cols, :])
+                    fold[slot, 0, :cols, i * LANES : i * LANES + width] = high
+                    fold[slot, 1, :cols, i * LANES : i * LANES + width] = low
+                out = three_product(table, fold[slot, 0], fold[slot, 1])
+                for i in range(2):
+                    base = pl.multiple_of((step * size.band + 2 * pair + i) * lines, lines)
+                    spectra[which, pl.ds(base, lines), :] = out[:, i * LANES : (i + 1) * LANES]
+
+    @pl.when(step >= bands)
+    def _():
+        first = (step - bands) * size.batch
+        for k in range(size.batch):
+            at = k * both
+            for which, table in enumerate((fx_ref, fg_ref)):
+                data = side_by_side(
+                    spectra[which, pl.ds(first + k, size.row_slots, stride=lines), :],
+                    spectra[which, pl.ds(first + k + slots, size.row_slots, stride=lines), :],
+                )
+                out = four_product(table, data)
+                cos_one, cos_two = out[:half, :LANES], out[:half, LANES:]
+                sin_one, sin_two = out[half:, :LANES], out[half:, LANES:]
+                plus = side_by_side(cos_one - sin_two, -(cos_two + sin_one))
+                minus = side_by_side(cos_one + sin_two, sin_one - cos_two)
+                if which == 0:
+                    for part, value in ((0, plus), (1, minus)):
+                        high, low = split(value)
+                        here = slice(at + part * half, at + (part + 1) * half)
+                        keep[0, 0, here] = high
+                        keep[0, 1, here] = low
+                else:
+                    plain[0, at : at + half] = plus
+                    plain[0, at + half : at + both] = minus
+        piece = 16 * math.gcd(rows // 16, 2)
+
+        plain[1] = mix(w_ref, 0, keep[0, 0], keep[0, 1])
+        for at in range(0, rows, piece):
+            here = slice(at, at + piece)
+            a = plain[1, here] + b_ref[0]
+            square = a * a
+            tangent = jnp.tanh(a * (GELU_SCALE + (GELU_SCALE * GELU_CUBE) * square))
+            part = 0.5 * a
+            plain[2, here] = 0.5 + 0.5 * tangent + part * (1.0 - tangent * tangent) * (
+                GELU_SCALE + (3.0 * GELU_SCALE * GELU_CUBE) * square
+            )
+            high, low = split(part + part * tangent)
+            keep[1, 0, here] = high
+            keep[1, 1, here] = low
+        plain[1] = mix(w_ref, 1, keep[1, 0], keep[1, 1])
+        sums = jnp.zeros((SUB, 2 * LANES), F32)
+        for at in range(0, rows, piece):
+            here = slice(at, at + piece)
+            gate = jnp.tanh((plain[1, here] + b_ref[1]) * (1.0 / SHRINK))
+            e = plain[0, here] * (gate * gate)
+            for i in range(0, piece, SUB):
+                sums = sums + e[i : i + SUB]
+            high, low = split(e)
+            keep[2, 0, here] = high
+            keep[2, 1, here] = low
+        bias_total[1] += sums
+        plain[1] = mix(w_ref, 2, keep[2, 0], keep[2, 1])
+        sums = jnp.zeros((SUB, 2 * LANES), F32)
+        for at in range(0, rows, piece):
+            here = slice(at, at + piece)
+            s = plain[1, here] * plain[2, here]
+            s_ref[here] = s
+            for i in range(0, piece, SUB):
+                sums = sums + s[i : i + SUB]
+            high, low = split(s)
+            keep[3, 0, here] = high
+            keep[3, 1, here] = low
+        bias_total[0] += sums
+        for layer, left, right in ((0, 0, 3), (1, 1, 2)):
+            total[layer] += (
+                dot_tn(keep[left, 0], keep[right, 0])
+                + dot_tn(keep[left, 1], keep[right, 0])
+                + dot_tn(keep[left, 0], keep[right, 1])
+            )
+
+    @pl.when(step == bands + batches - 1)
+    def _():
+        for layer in range(2):
+            upper = total[layer, :width]
+            lower = total[layer, LANES : LANES + width]
+            grad_ref[layer, 0, :width] = upper[:, :LANES] + lower[:, LANES:]
+            grad_ref[layer, 1, :width] = upper[:, LANES:] - lower[:, :LANES]
+            bias = jnp.broadcast_to(jnp.sum(bias_total[layer], axis=0, keepdims=True), (SUB, 2 * LANES))
+            grad_ref[layer, 0, width:] = bias[:, :LANES]
+            grad_ref[layer, 1, width:] = bias[:, LANES:]
+
+
+def lat_back_kernel(size, s_ref, w_ref, f_ref, v_ref, keep, plain):
+    both, half = size.both, size.half
+    rows = size.batch * both
+    for at in range(0, rows, both):
+        high, low = split(s_ref[at : at + both])
+        keep[0, at : at + both] = high
+        keep[1, at : at + both] = low
+    plain[...] = mix(w_ref, 0, keep[0], keep[1])
+    for k in range(size.batch):
+        at = k * both
+        plus, minus = plain[at : at + half], plain[at + half : at + both]
+        add, sub = plus + minus, plus - minus
+        data = jnp.concatenate(
+            [
+                side_by_side(add[:, :LANES], -add[:, LANES:]),
+                side_by_side(sub[:, LANES:], sub[:, :LANES]),
+            ],
+            axis=0,
+        )
+        out = four_product(f_ref, data)
+        for q in range(2):
+            v_ref[q, k] = out[:, q * LANES : (q + 1) * LANES]
+
+
+def lon_back_kernel(size, width, v_hbm, t_ref, out_ref, v_ref, sem):
+    cols, slots = size.cols, size.slots
+    step = pl.program_id(0)
+    stride = size.row_slots
+    flat = out_ref.reshape(size.band * cols, width)
+
+    @pl.when(step == 0)
+    def _():
+        copies = []
+        for q in range(2):
+            tail = slots - size.freqs
+            if tail:
+                v_ref[pl.ds((q * slots + size.freqs) * stride, tail * stride), :] = jnp.zeros((tail * stride, LANES), F32)
+            copies.append(
+                pltpu.make_async_copy(
+                    v_hbm.at[q], v_ref.at[pl.ds(q * slots * stride, size.freqs * stride), :], sem.at[q]
+                )
+            )
+            copies[-1].start()
+        for copy in copies:
+            copy.wait()
+
+    for pair in range(size.band // 2):
+        data = side_by_side(
+            *(
+                v_ref[pl.ds(step * size.band + 2 * pair + i, 2 * slots, stride=stride), :]
+                for i in range(2)
+            )
+        )
+        high, low = split(data)
+        out = three_product(t_ref, high, low)
+        for i in range(2):
+            at = (2 * pair + i) * cols
+            flat[at : at + cols, :] = out[:cols, i * LANES : i * LANES + width]
+
+
+def whole_spec(array):
+    zeros = (0,) * array.ndim
+    return pl.BlockSpec(array.shape, lambda *_: zeros)
+
+
+def spectral_gradients(size, width, fields, weights, biases):
+    tables = [stacked(lon_table(size, which)) for which in (False, True)]
+    tables += [four_way(lat_table(size, which)) for which in (False, True)]
+    consts = [jnp.asarray(table) for table in tables] + [weights, biases]
+    bands, batches = size.rows // size.band, size.freqs // size.batch
+    rows = size.batch * size.both
+    field = pl.BlockSpec((size.band * size.cols // SUB, SUB, width), lambda i: (jnp.minimum(i, bands - 1), 0, 0))
+    return pl.pallas_call(
+        functools.partial(gradient_kernel, size, width, bands, batches),
+        grid=(bands + batches,),
+        in_specs=[field, field] + [whole_spec(const) for const in consts],
+        out_specs=[
+            pl.BlockSpec((rows, 2 * LANES), lambda i: (jnp.maximum(i - bands, 0), 0)),
+            pl.BlockSpec((2, 2, width + SUB, LANES), lambda i: (0, 0, 0, 0)),
+        ],
+        out_shape=[
+            jax.ShapeDtypeStruct((size.freqs * size.both, 2 * LANES), F32),
+            jax.ShapeDtypeStruct((2, 2, width + SUB, LANES), F32),
+        ],
+        scratch_shapes=[
+            pltpu.VMEM((size.band, 2, size.col_slots, 2 * LANES), BF16),
+            pltpu.VMEM((2, size.row_slots * 2 * size.slots, LANES), F32),
+            pltpu.VMEM((4, 2, rows, 2 * LANES), BF16),
+            pltpu.VMEM((3, rows, 2 * LANES), F32),
+            pltpu.VMEM((2, 2 * LANES, 2 * LANES), F32),
+            pltpu.VMEM((2, SUB, 2 * LANES), F32),
+        ],
+        compiler_params=pltpu.CompilerParams(vmem_limit_bytes=VMEM_LIMIT),
+        name="spectral_gradients",
+    )(*fields, *consts)
+
+
+def lat_back(size, s_modes, weights):
+    lat = lat_table(size, False).T.copy()
+    lat[:, size.half :] *= -1.0
+    consts = [weights, jnp.asarray(four_way(lat))]
+    rows = size.batch * size.both
+    return pl.pallas_call(
+        functools.partial(lat_back_kernel, size),
+        grid=(size.freqs // size.batch,),
+        in_specs=[pl.BlockSpec((rows, 2 * LANES), lambda i: (i, 0))] + [whole_spec(const) for const in consts],
+        out_specs=pl.BlockSpec((2, size.batch, size.row_slots, LANES), lambda i: (0, i, 0, 0)),
+        out_shape=jax.ShapeDtypeStruct((2, size.freqs, size.row_slots, LANES), F32),
+        scratch_shapes=[
+            pltpu.VMEM((2, rows, 2 * LANES), BF16),
+            pltpu.VMEM((rows, 2 * LANES), F32),
+        ],
+        compiler_params=pltpu.CompilerParams(vmem_limit_bytes=VMEM_LIMIT),
+        name="lat_back",
+    )(s_modes, *consts)
+
+
+def lon_back(size, width, v_modes):
+    lon = lon_table(size, False).T
+    table = jnp.asarray(stacked(lon))
+    flat = v_modes.reshape(2, size.freqs * size.row_slots, LANES)
+    return pl.pallas_call(
+        functools.partial(lon_back_kernel, size, width),
+        grid=(size.rows // size.band,),
+        in_specs=[pl.BlockSpec(memory_space=pl.ANY), whole_spec(table)],
+        out_specs=pl.BlockSpec((size.band * size.cols // SUB, SUB, width), lambda i: (i, 0, 0)),
+        out_shape=jax.ShapeDtypeStruct((size.rows * size.cols // SUB, SUB, width), F32),
+        scratch_shapes=[
+            pltpu.VMEM((2 * size.slots * size.row_slots, LANES), F32),
+            pltpu.SemaphoreType.DMA((2,)),
+        ],
+        compiler_params=pltpu.CompilerParams(vmem_limit_bytes=VMEM_LIMIT),
+        name="lon_back",
+    )(flat, table)
+
+
+def mix_matrices(first, second):
+    def matrix(weight):
+        pad = LANES - weight.shape[-1]
+        real, imag = (jnp.pad(part, ((0, pad), (0, pad))) for part in (weight[0], weight[1]))
+        return jnp.concatenate([side_by_side(real, imag), side_by_side(-imag, real)], 0)
+
+    one, two = matrix(first), matrix(second)
+    every = jnp.stack([one, two, two.T, one.T])
+    high = lax.reduce_precision(every, 8, 7)
+    return jnp.stack([high, every - high], axis=1).astype(BF16)
+
+
+def bias_rows(first, second):
+    pad = LANES - first.shape[-1]
+    return jnp.stack([jnp.pad(part, ((0, 0), (0, pad))).reshape(1, 2 * LANES) for part in (first, second)])
+
+
+def sum_over_lat(value):
+    count = lax.axis_size("lat")
+    if count != 4:
+        return lax.psum(value, "lat")
+    one, two, three = (
+        lax.ppermute(value, "lat", [(i, (i + s) % count) for i in range(count)]) for s in (1, 2, 3)
+    )
+    return (value + two) + (one + three)
+
+
+def gather_over_lon(value):
+    count = lax.axis_size("lon")
+    me = lax.axis_index("lon")
+    parts = [value] + [lax.ppermute(value, "lon", [(i, i ^ s) for i in range(count)]) for s in range(1, count)]
+    return parts, me
+
+
+def whole_block(layer_input, grad_output, first_weight, first_bias, second_weight, second_bias):
+    _, width, lat_rows, lon_cols = layer_input.shape
+    size = Sizes(lat_rows, lon_cols)
+    block = lax.axis_index("lon")
+
+    def mine(weight):
+        return lax.dynamic_index_in_dim(weight, block, axis=1, keepdims=False)
+
+    fields = [
+        jnp.transpose(field, (0, 2, 3, 1)).reshape(-1, SUB, width)
+        for field in (layer_input, grad_output)
+    ]
+    weights = mix_matrices(mine(first_weight), mine(second_weight))
+    s_modes, partial = spectral_gradients(
+        size, width, fields, weights[:3], bias_rows(mine(first_bias), mine(second_bias))
+    )
+    summed = sum_over_lat(partial)
+    v_modes = lat_back(size, s_modes, weights[3:])
+    summed, v_modes = lax.optimization_barrier((summed, v_modes))
+    parts, me = gather_over_lon(summed)
+    out = lon_back(size, width, v_modes)
+    grad_input = out.reshape(lat_rows * lon_cols, width).T.reshape(1, width, lat_rows, lon_cols)
+    stack = jnp.stack(parts)
+    whole = jnp.stack(
+        [lax.dynamic_index_in_dim(stack, me ^ b, 0, keepdims=False) for b in range(len(parts))], axis=2
+    )
+    weight_grads = whole[:, :, :, :width, :width]
+    bias_grads = whole[:, :, :, width, :width]
+    return (grad_input, weight_grads[0], bias_grads[0], weight_grads[1], bias_grads[1])
 
 
 def tables(length, count, limit):
@@ -42,15 +467,15 @@
 
 
 def forward_mix(left, matrix):
-    return jnp.einsum("psir,piqj->qsjr", left, matrix, precision=PREC)
+    return jnp.einsum("psir,piqj->qsjr", left, matrix, precision=PRECISION)
 
 
 def back_mix(left, matrix):
-    return jnp.einsum("qsjr,piqj->psir", left, matrix, precision=PREC)
+    return jnp.einsum("qsjr,piqj->psir", left, matrix, precision=PRECISION)
 
 
 def weight_grad(left, right):
-    total = jnp.einsum("psir,qsjr->piqj", left, right, precision=PREC)
+    total = jnp.einsum("psir,qsjr->piqj", left, right, precision=PRECISION)
     return jnp.stack(
         [total[0, :, 0, :] + total[1, :, 1, :], total[0, :, 1, :] - total[1, :, 0, :]]
     )
@@ -76,7 +501,7 @@
     return d_both, (grad_w_one, grad_b_one, grad_w_two, grad_b_two)
 
 
-def on_device(layer_input, grad_output, first_weight, first_bias, second_weight, second_bias):
+def spread_block(layer_input, grad_output, first_weight, first_bias, second_weight, second_bias):
     lon_count = lax.axis_size("lon")
     samples, local_ch, lat_rows, lon_cols = layer_input.shape
     blocks, width = first_weight.shape[1], first_weight.shape[2]
@@ -99,8 +524,8 @@
     )
 
     def spectrum(data, table):
-        half = jnp.einsum("schw,wqk->qsckh", data, table, precision=PREC)
-        full = jnp.einsum("psckh,phqm->qsckm", half, lat_table, precision=PREC)
+        half = jnp.einsum("schw,wqk->qsckh", data, table, precision=PRECISION)
+        full = jnp.einsum("psckh,phqm->qsckm", half, lat_table, precision=PRECISION)
         return full.reshape((2, samples, local_ch, freq_slots * lat_rows))
 
     def share(data, split, concat):
@@ -128,9 +553,9 @@
     shape_five = (2, samples, local_ch, freq_slots, lat_rows)
     grad_input = jnp.einsum(
         "qsckh,qkw->schw",
-        jnp.einsum("psckm,pmqh->qsckh", stacked.reshape(shape_five), lat_back, precision=PREC),
+        jnp.einsum("psckm,pmqh->qsckh", stacked.reshape(shape_five), lat_back, precision=PRECISION),
         lon_back,
-        precision=PREC,
+        precision=PRECISION,
     )
     results = []
     offset = 0
@@ -142,6 +567,14 @@
     return (grad_input, grad_w_one, grad_b_one, grad_w_two, grad_b_two)
 
 
+def on_device(layer_input, grad_output, first_weight, first_bias, second_weight, second_bias):
+    samples, local_ch, lat_rows, lon_cols = layer_input.shape
+    width = first_weight.shape[2]
+    one_device = samples == 1 and local_ch == width <= LANES and width % SUB == 0
+    run = whole_block if one_device and Sizes(lat_rows, lon_cols).fits() else spread_block
+    return run(layer_input, grad_output, first_weight, first_bias, second_weight, second_bias)
+
+
 def solution(mesh):
     placed = (P("lat", "lon", None, None), P("lat", "lon", None, None), P(), P(), P(), P())
     return jax.shard_map(

time: 255 us -> 135 us (0.53); the launches traced: 251 us -> 134 us
  matrix products: 108 us -> 0 us
  Pallas kernels: 0 us -> 102 us
  local copies, waits for them, and re-layouts: 84.4 us -> 5.8 us
  waiting for transfers between devices: 37.1 us -> 10.1 us
  between operations: 14.6 us -> 0.94 us
  starting transfers between devices: 0.08 us -> 12.5 us
  other arithmetic: 6.14 us -> 2.55 us
    dot_general x12 -> x0, matrix products: 108 us -> none  [the longest x2 24.5 us: back_mix(): return jnp.einsum('qsjr,piqj->psir', left, matrix, precision=PREC)]
    pallas_call x0 -> x3, Pallas kernels: none -> 102 us  [the longest x1 68.8 us: spectral_gradients(): pl.pallas_call(functools.partial(gradient_kernel, size, width, bands, bat...]
    psum x1 -> x0, waiting for transfers between devices: 37.1 us -> none  [on_device(): summed = lax.psum(flat_grads, 'lat')]
    another operation x3 -> x4, local copies, waits for them, and re-layouts: 30.3 us -> 0.3 us  [the longest x2 0.26 us: mix_matrices(): every = jnp.stack([one, two, two.T, one.T])]
    reshape x10 -> x0, local copies, waits for them, and re-layouts: 18.9 us -> none  [the longest x2 17.8 us: spectrum(): return full.reshape((2, samples, local_ch, freq_slots * lat_rows))]
    dot_general x1 -> x0, local copies, waits for them, and re-layouts: 17.9 us -> none  [back_mix(): return jnp.einsum('qsjr,piqj->psir', left, matrix, precision=PREC)]
    unnamed x22, local copies, waits for them, and re-layouts: 14.5 us -> 1.81 us
    ppermute x0 -> x10, starting transfers between devices: none -> 12.5 us  [the longest x7 6.47 us: gather_over_lon(): lax.ppermute(value, 'lon', [(i, i ^ s) for i in range(count)])]
  transfers between devices with their start and end apart: 2 -> 10, of which waited for: 1 -> 3; matrix products, arithmetic and copies ran while one was open for 21% -> 1% of each run, Pallas kernels for 0% -> 25%
where the time goes in v2:
time: 135 us; the launch traced here: 134 us
  Pallas kernels  102 us (76%)
  starting transfers between devices  12.5 us (9%)
  waiting for transfers between devices  10.1 us (7%)
  local copies, waits for them, and re-layouts  5.8 us (4%)
  other arithmetic  2.55 us (2%)
    pallas_call x1, Pallas kernels, spectral_gradients(): pl.pallas_call(functools.partial(gradient_kernel, size, width, bands, bat...  68.8 us
    pallas_call x1, Pallas kernels, lat_back(): pl.pallas_call(functools.partial(lat_back_kernel, size), grid=(size.freqs...  17 us
    pallas_call x1, Pallas kernels, lon_back(): pl.pallas_call(functools.partial(lon_back_kernel, size, width), grid=(siz...  16.4 us
    ppermute x7, waiting for transfers between devices, gather_over_lon(): lax.ppermute(value, 'lon', [(i, i ^ s) for i in range(count)])  9.7 us
    ppermute x7, starting transfers between devices, gather_over_lon(): lax.ppermute(value, 'lon', [(i, i ^ s) for i in range(count)])  6.47 us
    ppermute x3, starting transfers between devices, sum_over_lat(): lax.ppermute(value, 'lat', [(i, (i + s) % count) for i in range(count)])  6.05 us
  transfers between devices with their start and end apart: 10, of which 3 were waited for; matrix products, arithmetic and copies ran while one was open for 1% of the time, Pallas kernels for 25%

profile of v2, /device:TPU:0, one launch (start us, length us, event | category | flops | bytes accessed | tf_op | source)
XLA Modules:
  0.0 134.1 jit_solution(18311082842252615621)
XLA Ops:
  0.6 0.9 constant_dynamic-slice_fusion.4
  1.5 0.1 copy.30
  1.6 0.1 copy.31
  1.7 0.1 copy.33
  2.0 0.1 copy.24
  2.2 0.1 copy.23
  2.3 0.7 constant_dynamic-slice_fusion.2
  3.1 0.2 fusion
  3.2 0.9 fusion.1.w_ref
  4.2 0.6 pad_maximum_fusion.2.b_ref
  4.8 68.8 %spectral_gradients.1 = (f32[8736,256]{1,0:T(8,128)}, f32[2,2,104,128]{3,2,1,0:T(8,128)}) custom-call(f32[2025,8,96]{2,1,0:T(8,128)} %bitcast.74, f32[2025,8,96]{2,1,0:T(8,128)} %bitcast.75, bf16[384,192]{1,0:T(8,128)(2,1)} %constant.65.clone.tx_ref, bf16[384,192]{1,0:T(8,128)(2,1)} %constant.66.clone.tg_ref, bf16[192,192]{1,0:T(8,128)(2,1)} %constant.67.clone.fx_ref, ...), custom_call_target="tpu_custom_call" | custom-call | tf_op jit(solution)/shard_map/spectral_gradients/pallas_call | solution.py:310
  73.6 3.0 %collective-permute-start.1 = (f32[2,2,104,128]{3,2,1,0:T(8,128)}, f32[2,2,104,128]{3,2,1,0:T(8,128)S(1)}, u32[]{:S(2)}, u32[]{:S(2)}) collective-permute-start(f32[2,2,104,128]{3,2,1,0:T(8,128)} %get-tuple-element.9), channel_id=1, source_target_pairs={{0,8},{8,16},{16,24},{24,0},{1,9},{9,17},{17,25},{25,1},{2,10},{10... | collective-permute-start | bytes 638984 | tf_op jit(solution)/shard_map/ppermute | solution.py:396
  76.6 2.1 %collective-permute-start.2 = (f32[2,2,104,128]{3,2,1,0:T(8,128)}, f32[2,2,104,128]{3,2,1,0:T(8,128)S(1)}, u32[]{:S(2)}, u32[]{:S(2)}) collective-permute-start(f32[2,2,104,128]{3,2,1,0:T(8,128)} %get-tuple-element.9), channel_id=1, source_target_pairs={{0,24},{8,0},{16,8},{24,16},{1,25},{9,1},{17,9},{25,17},{2,26},{10... | collective-permute-start | bytes 638984 | tf_op jit(solution)/shard_map/ppermute | solution.py:396
  78.7 0.9 collective-permute-start
  79.6 0.7 pad_maximum_fusion.1.w_ref
  80.3 17.0 %lat_back.1 = f32[2,91,96,128]{3,2,1,0:T(8,128)} custom-call(f32[8736,256]{1,0:T(8,128)} %get-tuple-element.10.s_ref, bf16[1,2,256,256]{3,2,1,0:T(8,128)(2,1)} %pad_maximum_fusion.1.w_ref, bf16[192,192]{1,0:T(8,128)(2,1)} %constant.69.clone.f_ref), custom_call_target="tpu_custom_call" | custom-call | tf_op jit(solution)/shard_map/lat_back/pallas_call | solution.py:340
  97.4 0.4 collective-permute-done
  97.8 0.1 collective-permute-start.3
  97.9 1.6 %collective-permute-start.4 = (f32[2,2,104,128]{3,2,1,0:T(8,128)S(1)}, f32[2,2,104,128]{3,2,1,0:T(8,128)S(1)}, u32[]{:S(2)}, u32[]{:S(2)}) collective-permute-start(f32[2,2,104,128]{3,2,1,0:T(8,128)S(1)} %add_add_fusion), channel_id=1, source_target_pairs={{0,2},{1,3},{2,0},{3,1},{4,6},{5,7},{6,4},{7,5},{8,10},{9,11},{10,... | collective-permute-start | bytes 638984 | tf_op jit(solution)/shard_map/ppermute | solution.py:404
  99.4 0.3 collective-permute-start.5
  99.7 1.5 %collective-permute-start.6 = (f32[2,2,104,128]{3,2,1,0:T(8,128)S(1)}, f32[2,2,104,128]{3,2,1,0:T(8,128)S(1)}, u32[]{:S(2)}, u32[]{:S(2)}) collective-permute-start(f32[2,2,104,128]{3,2,1,0:T(8,128)S(1)} %add_add_fusion), channel_id=1, source_target_pairs={{0,4},{1,5},{2,6},{3,7},{4,0},{5,1},{6,2},{7,3},{8,12},{9,13},{10,... | collective-permute-start | bytes 638984 | tf_op jit(solution)/shard_map/ppermute | solution.py:404
  101.3 0.2 collective-permute-start.7
  101.4 16.4 %lon_back.1 = f32[2025,8,96]{2,1,0:T(8,128)} custom-call(f32[2,8736,128]{2,1,0:T(8,128)} %bitcast.72, bf16[384,192]{1,0:T(8,128)(2,1)} %constant.70.clone.t_ref), custom_call_target="tpu_custom_call" | custom-call | tf_op jit(solution)/shard_map/lon_back/pallas_call | solution.py:359
  117.9 2.5 %collective-permute-start.8 = (f32[2,2,104,128]{3,2,1,0:T(8,128)S(1)}, f32[2,2,104,128]{3,2,1,0:T(8,128)S(1)}, u32[]{:S(2)}, u32[]{:S(2)}) collective-permute-start(f32[2,2,104,128]{3,2,1,0:T(8,128)S(1)} %add_add_fusion), channel_id=1, source_target_pairs={{0,6},{1,7},{2,4},{3,5},{4,2},{5,3},{6,0},{7,1},{8,14},{9,15},{10,... | collective-permute-start | bytes 638984 | tf_op jit(solution)/shard_map/ppermute | solution.py:404
  120.4 0.3 collective-permute-start.9
  120.9 6.0 %collective-permute-done.8 = f32[2,2,104,128]{3,2,1,0:T(8,128)S(1)} collective-permute-done((f32[2,2,104,128]{3,2,1,0:T(8,128)S(1)}, f32[2,2,104,128]{3,2,1,0:T(8,128)S(1)}, u32[]{:S(2)}, u32[]{:S(2)}) %collective-permute-start.8) | collective-permute-done | bytes 213024 | tf_op jit(solution)/shard_map/ppermute | solution.py:404
  126.9 3.7 %collective-permute-done.9 = f32[2,2,104,128]{3,2,1,0:T(8,128)S(1)} collective-permute-done((f32[2,2,104,128]{3,2,1,0:T(8,128)S(1)}, f32[2,2,104,128]{3,2,1,0:T(8,128)S(1)}, u32[]{:S(2)}, u32[]{:S(2)}) %collective-permute-start.9) | collective-permute-done | bytes 213024 | tf_op jit(solution)/shard_map/ppermute | solution.py:404
  130.8 0.2 fusion.7
  131.0 0.9 copy.38
  132.0 0.6 copy.27
  132.6 0.9 copy.37
  133.5 0.6 copy.28
  (36 shorter events, 0.6 us)
Async XLA Ops:
  73.6 23.8 %collective-permute-start.1 = (f32[2,2,104,128]{3,2,1,0:T(8,128)}, f32[2,2,104,128]{3,2,1,0:T(8,128)S(1)}, u32[]{:S(2)}, u32[]{:S(2)}) collective-permute-start(f32[2,2,104,128]{3,2,1,0:T(8,128)} %get-tuple-element.9), channel_id=1, source_target_pairs={{0,8},{8,16},{16,24},{24,0},{1,9},{9,17},{17,25},{25,1},{2,10},{10... | collective-permute-start | bytes 638984 | tf_op jit(solution)/shard_map/ppermute | solution.py:396
  76.6 20.8 %collective-permute-start.2 = (f32[2,2,104,128]{3,2,1,0:T(8,128)}, f32[2,2,104,128]{3,2,1,0:T(8,128)S(1)}, u32[]{:S(2)}, u32[]{:S(2)}) collective-permute-start(f32[2,2,104,128]{3,2,1,0:T(8,128)} %get-tuple-element.9), channel_id=1, source_target_pairs={{0,24},{8,0},{16,8},{24,16},{1,25},{9,1},{17,9},{25,17},{2,26},{10... | collective-permute-start | bytes 638984 | tf_op jit(solution)/shard_map/ppermute | solution.py:396
  78.7 19.1 %collective-permute-start = (f32[2,2,104,128]{3,2,1,0:T(8,128)}, f32[2,2,104,128]{3,2,1,0:T(8,128)S(1)}, u32[]{:S(2)}, u32[]{:S(2)}) collective-permute-start(f32[2,2,104,128]{3,2,1,0:T(8,128)} %get-tuple-element.9), channel_id=1, source_target_pairs={{0,16},{8,24},{16,0},{24,8},{1,17},{9,25},{17,1},{25,9},{2,18},{10... | collective-permute-start | bytes 638984 | tf_op jit(solution)/shard_map/ppermute | solution.py:396
  80.3 17.4 %copy-start = (f32[2,2,104,128]{3,2,1,0:T(8,128)S(1)}, f32[2,2,104,128]{3,2,1,0:T(8,128)}, u32[]{:S(2)}) copy-start(f32[2,2,104,128]{3,2,1,0:T(8,128)} %get-tuple-element.9) | copy-start | bytes 638980
  97.8 20.1 %collective-permute-start.3 = (f32[2,2,104,128]{3,2,1,0:T(8,128)S(1)}, f32[2,2,104,128]{3,2,1,0:T(8,128)S(1)}, u32[]{:S(2)}, u32[]{:S(2)}) collective-permute-start(f32[2,2,104,128]{3,2,1,0:T(8,128)S(1)} %add_add_fusion), channel_id=1, source_target_pairs={{0,1},{1,0},{2,3},{3,2},{4,5},{5,4},{6,7},{7,6},{8,9},{9,8},{10,11... | collective-permute-start | bytes 638984 | tf_op jit(solution)/shard_map/ppermute | solution.py:404
  97.9 22.5 %collective-permute-start.4 = (f32[2,2,104,128]{3,2,1,0:T(8,128)S(1)}, f32[2,2,104,128]{3,2,1,0:T(8,128)S(1)}, u32[]{:S(2)}, u32[]{:S(2)}) collective-permute-start(f32[2,2,104,128]{3,2,1,0:T(8,128)S(1)} %add_add_fusion), channel_id=1, source_target_pairs={{0,2},{1,3},{2,0},{3,1},{4,6},{5,7},{6,4},{7,5},{8,10},{9,11},{10,... | collective-permute-start | bytes 638984 | tf_op jit(solution)/shard_map/ppermute | solution.py:404
  99.4 21.3 %collective-permute-start.5 = (f32[2,2,104,128]{3,2,1,0:T(8,128)S(1)}, f32[2,2,104,128]{3,2,1,0:T(8,128)S(1)}, u32[]{:S(2)}, u32[]{:S(2)}) collective-permute-start(f32[2,2,104,128]{3,2,1,0:T(8,128)S(1)} %add_add_fusion), channel_id=1, source_target_pairs={{0,3},{1,2},{2,1},{3,0},{4,7},{5,6},{6,5},{7,4},{8,11},{9,10},{10,... | collective-permute-start | bytes 638984 | tf_op jit(solution)/shard_map/ppermute | solution.py:404
  99.7 21.0 %collective-permute-start.6 = (f32[2,2,104,128]{3,2,1,0:T(8,128)S(1)}, f32[2,2,104,128]{3,2,1,0:T(8,128)S(1)}, u32[]{:S(2)}, u32[]{:S(2)}) collective-permute-start(f32[2,2,104,128]{3,2,1,0:T(8,128)S(1)} %add_add_fusion), channel_id=1, source_target_pairs={{0,4},{1,5},{2,6},{3,7},{4,0},{5,1},{6,2},{7,3},{8,12},{9,13},{10,... | collective-permute-start | bytes 638984 | tf_op jit(solution)/shard_map/ppermute | solution.py:404
  101.3 19.5 %collective-permute-start.7 = (f32[2,2,104,128]{3,2,1,0:T(8,128)S(1)}, f32[2,2,104,128]{3,2,1,0:T(8,128)S(1)}, u32[]{:S(2)}, u32[]{:S(2)}) collective-permute-start(f32[2,2,104,128]{3,2,1,0:T(8,128)S(1)} %add_add_fusion), channel_id=1, source_target_pairs={{0,5},{1,4},{2,7},{3,6},{4,1},{5,0},{6,3},{7,2},{8,13},{9,12},{10,... | collective-permute-start | bytes 638984 | tf_op jit(solution)/shard_map/ppermute | solution.py:404
  117.9 9.0 %collective-permute-start.8 = (f32[2,2,104,128]{3,2,1,0:T(8,128)S(1)}, f32[2,2,104,128]{3,2,1,0:T(8,128)S(1)}, u32[]{:S(2)}, u32[]{:S(2)}) collective-permute-start(f32[2,2,104,128]{3,2,1,0:T(8,128)S(1)} %add_add_fusion), channel_id=1, source_target_pairs={{0,6},{1,7},{2,4},{3,5},{4,2},{5,3},{6,0},{7,1},{8,14},{9,15},{10,... | collective-permute-start | bytes 638984 | tf_op jit(solution)/shard_map/ppermute | solution.py:404
  120.4 10.1 %collective-permute-start.9 = (f32[2,2,104,128]{3,2,1,0:T(8,128)S(1)}, f32[2,2,104,128]{3,2,1,0:T(8,128)S(1)}, u32[]{:S(2)}, u32[]{:S(2)}) collective-permute-start(f32[2,2,104,128]{3,2,1,0:T(8,128)S(1)} %add_add_fusion), channel_id=1, source_target_pairs={{0,7},{1,6},{2,5},{3,4},{4,3},{5,2},{6,1},{7,0},{8,15},{9,14},{10,... | collective-permute-start | bytes 638984 | tf_op jit(solution)/shard_map/ppermute | solution.py:404

commit v3 on v2

--- a/solution.py
+++ b/solution.py
@@ -18,7 +18,7 @@
 SUB = 8
 F32 = jnp.float32
 BF16 = jnp.bfloat16
-VMEM_LIMIT = 56 << 20
+CHUNK = 4
 
 
 def round_up(value, unit):
@@ -38,10 +38,6 @@
 
 def dot(left, right):
     return jnp.dot(left, right, preferred_element_type=F32)
-
-
-def dot_tn(left, right):
-    return lax.dot_general(left, right, (((0,), (0,)), ((), ())), preferred_element_type=F32)
 
 
 def side_by_side(left, right):
@@ -63,13 +59,14 @@
         self.both = 2 * self.half
         self.freqs = cols // 2 + 1
         self.slots = round_up(self.freqs, 16)
+        self.stride = round_up(2 * self.slots, 2 * SUB) + SUB
         self.row_slots = round_up(rows, 16)
         self.col_slots = round_up(cols, 16)
-        self.band = max((n for n in range(2, 7, 2) if rows % n == 0 and n * cols % SUB == 0), default=0)
-        self.batch = max(n for n in range(1, 9) if self.freqs % n == 0)
+        self.band = max((n for n in range(2, 11, 2) if rows % n == 0 and n * cols % SUB == 0), default=0)
+        self.batch = SUB
 
     def fits(self):
-        return self.band > 0 and self.batch * self.both % 16 == 0
+        return self.band > 0 and self.cols % 4 == 0
 
 
 def lat_table(size, cotangent):
@@ -100,8 +97,9 @@
     return np.concatenate([np.concatenate([high, high], 1), np.concatenate([low, low], 1)], 0)
 
 
-def stacked(table):
-    return np.concatenate(halves(table), 0)
+def three_way(table):
+    high, low = halves(table)
+    return np.concatenate([high, low, high], 1)
 
 
 def four_product(table_ref, data):
@@ -111,13 +109,11 @@
 
 
 def three_product(table_ref, high, low):
-    count = table_ref.shape[0] // 2
-    two = dot(table_ref[...], high)
-    return two[:count] + two[count:] + dot(table_ref[:count], low)
+    return dot(table_ref[...], jnp.concatenate([high, high, low], axis=0))
 
 
 def mix(weight_ref, which, high, low):
-    return dot(high, weight_ref[which, 0]) + dot(low, weight_ref[which, 0]) + dot(high, weight_ref[which, 1])
+    return dot(jnp.concatenate([high, low, high], axis=1), weight_ref[which])
 
 
 def gradient_kernel(
@@ -126,6 +122,7 @@
 ):
     step = pl.program_id(0)
     cols, slots, both, half = size.cols, size.slots, size.both, size.half
+    stride = size.stride
     lines = 2 * slots
     rows = size.batch * both
 
@@ -135,7 +132,7 @@
         total[...] = jnp.zeros_like(total)
         bias_total[...] = jnp.zeros_like(bias_total)
         for which in range(2):
-            spectra[which, size.rows * lines :] = jnp.zeros(((size.row_slots - size.rows) * lines, LANES), F32)
+            spectra[which, size.rows * stride :] = jnp.zeros(((size.row_slots - size.rows) * stride, LANES), F32)
 
     @pl.when(step < bands)
     def _():
@@ -150,84 +147,110 @@
                     fold[slot, 1, :cols, i * LANES : i * LANES + width] = low
                 out = three_product(table, fold[slot, 0], fold[slot, 1])
                 for i in range(2):
-                    base = pl.multiple_of((step * size.band + 2 * pair + i) * lines, lines)
+                    base = pl.multiple_of((step * size.band + 2 * pair + i) * stride, SUB)
                     spectra[which, pl.ds(base, lines), :] = out[:, i * LANES : (i + 1) * LANES]
 
     @pl.when(step >= bands)
     def _():
         first = (step - bands) * size.batch
-        for k in range(size.batch):
-            at = k * both
-            for which, table in enumerate((fx_ref, fg_ref)):
-                data = side_by_side(
-                    spectra[which, pl.ds(first + k, size.row_slots, stride=lines), :],
-                    spectra[which, pl.ds(first + k + slots, size.row_slots, stride=lines), :],
+        span = CHUNK * both
+        piece = 16
+
+        def transform(chunk):
+            for k in range(chunk * CHUNK, (chunk + 1) * CHUNK):
+                at = k * both
+                for which, table in enumerate((fx_ref, fg_ref)):
+                    data = side_by_side(
+                        spectra[which, pl.ds(first + k, size.row_slots, stride=stride), :],
+                        spectra[which, pl.ds(first + k + slots, size.row_slots, stride=stride), :],
+                    )
+                    out = four_product(table, data)
+                    cos_one, cos_two = out[:half, :LANES], out[:half, LANES:]
+                    sin_one, sin_two = out[half:, :LANES], out[half:, LANES:]
+                    plus = side_by_side(cos_one - sin_two, -(cos_two + sin_one))
+                    minus = side_by_side(cos_one + sin_two, sin_one - cos_two)
+                    for part, value in ((0, plus), (1, minus)):
+                        here = slice(at + part * half, at + (part + 1) * half)
+                        if which == 0:
+                            keep_split(0, here, value)
+                        else:
+                            plain[0, here] = value
+
+        def keep_split(which, here, value):
+            high, low = split(value)
+            keep[which, 0, here] = high
+            keep[which, 1, here] = low
+
+        def multiply(which, chunk):
+            here = slice(chunk * span, (chunk + 1) * span)
+            plain[1 + which, here] = mix(w_ref, which, keep[which, 0, here], keep[which, 1, here])
+
+        def pieces(chunk):
+            return [slice(at, at + piece) for at in range(chunk * span, (chunk + 1) * span, piece)]
+
+        def activate(chunk):
+            for here in pieces(chunk):
+                a = plain[1, here] + b_ref[0]
+                square = a * a
+                tangent = jnp.tanh(a * (GELU_SCALE + (GELU_SCALE * GELU_CUBE) * square))
+                part = 0.5 * a
+                plain[1, here] = 0.5 + 0.5 * tangent + part * (1.0 - tangent * tangent) * (
+                    GELU_SCALE + (3.0 * GELU_SCALE * GELU_CUBE) * square
                 )
-                out = four_product(table, data)
-                cos_one, cos_two = out[:half, :LANES], out[:half, LANES:]
-                sin_one, sin_two = out[half:, :LANES], out[half:, LANES:]
-                plus = side_by_side(cos_one - sin_two, -(cos_two + sin_one))
-                minus = side_by_side(cos_one + sin_two, sin_one - cos_two)
-                if which == 0:
-                    for part, value in ((0, plus), (1, minus)):
-                        high, low = split(value)
-                        here = slice(at + part * half, at + (part + 1) * half)
-                        keep[0, 0, here] = high
-                        keep[0, 1, here] = low
-                else:
-                    plain[0, at : at + half] = plus
-                    plain[0, at + half : at + both] = minus
-        piece = 16 * math.gcd(rows // 16, 2)
-
-        plain[1] = mix(w_ref, 0, keep[0, 0], keep[0, 1])
-        for at in range(0, rows, piece):
-            here = slice(at, at + piece)
-            a = plain[1, here] + b_ref[0]
-            square = a * a
-            tangent = jnp.tanh(a * (GELU_SCALE + (GELU_SCALE * GELU_CUBE) * square))
-            part = 0.5 * a
-            plain[2, here] = 0.5 + 0.5 * tangent + part * (1.0 - tangent * tangent) * (
-                GELU_SCALE + (3.0 * GELU_SCALE * GELU_CUBE) * square
+                keep_split(1, here, part + part * tangent)
+
+        def gate(chunk):
+            sums = jnp.zeros((SUB, 2 * LANES), F32)
+            for here in pieces(chunk):
+                tangent = jnp.tanh((plain[2, here] + b_ref[1]) * (1.0 / SHRINK))
+                e = plain[0, here] * (tangent * tangent)
+                for i in range(0, piece, SUB):
+                    sums = sums + e[i : i + SUB]
+                keep_split(2, here, e)
+            bias_total[1] += sums
+
+        def slope(chunk):
+            sums = jnp.zeros((SUB, 2 * LANES), F32)
+            for here in pieces(chunk):
+                value = plain[3, here] * plain[1, here]
+                s_ref[here] = value
+                for i in range(0, piece, SUB):
+                    sums = sums + value[i : i + SUB]
+                keep_split(3, here, value)
+            bias_total[0] += sums
+
+        def turned(which):
+            parts = [keep[which, i].T for i in range(2)]
+            return [jnp.concatenate([part[:width], part[LANES : LANES + width]], axis=0) for part in parts]
+
+        def weight_grad(layer, left, right):
+            high, low = turned(left)
+            total[layer] += dot(
+                jnp.concatenate([high, low, high], axis=1),
+                jnp.concatenate([keep[right, 0], keep[right, 0], keep[right, 1]], axis=0),
             )
-            high, low = split(part + part * tangent)
-            keep[1, 0, here] = high
-            keep[1, 1, here] = low
-        plain[1] = mix(w_ref, 1, keep[1, 0], keep[1, 1])
-        sums = jnp.zeros((SUB, 2 * LANES), F32)
-        for at in range(0, rows, piece):
-            here = slice(at, at + piece)
-            gate = jnp.tanh((plain[1, here] + b_ref[1]) * (1.0 / SHRINK))
-            e = plain[0, here] * (gate * gate)
-            for i in range(0, piece, SUB):
-                sums = sums + e[i : i + SUB]
-            high, low = split(e)
-            keep[2, 0, here] = high
-            keep[2, 1, here] = low
-        bias_total[1] += sums
-        plain[1] = mix(w_ref, 2, keep[2, 0], keep[2, 1])
-        sums = jnp.zeros((SUB, 2 * LANES), F32)
-        for at in range(0, rows, piece):
-            here = slice(at, at + piece)
-            s = plain[1, here] * plain[2, here]
-            s_ref[here] = s
-            for i in range(0, piece, SUB):
-                sums = sums + s[i : i + SUB]
-            high, low = split(s)
-            keep[3, 0, here] = high
-            keep[3, 1, here] = low
-        bias_total[0] += sums
-        for layer, left, right in ((0, 0, 3), (1, 1, 2)):
-            total[layer] += (
-                dot_tn(keep[left, 0], keep[right, 0])
-                + dot_tn(keep[left, 1], keep[right, 0])
-                + dot_tn(keep[left, 0], keep[right, 1])
-            )
+
+        count = size.batch // CHUNK
+        for t in range(count + 3):
+            if t < count:
+                transform(t)
+                multiply(0, t)
+            if 0 <= t - 1 < count:
+                activate(t - 1)
+                multiply(1, t - 1)
+            if 0 <= t - 2 < count:
+                gate(t - 2)
+                multiply(2, t - 2)
+            if 0 <= t - 3 < count:
+                slope(t - 3)
+        weight_grad(1, 1, 2)
+        weight_grad(0, 0, 3)
 
     @pl.when(step == bands + batches - 1)
     def _():
         for layer in range(2):
             upper = total[layer, :width]
-            lower = total[layer, LANES : LANES + width]
+            lower = total[layer, width:]
             grad_ref[layer, 0, :width] = upper[:, :LANES] + lower[:, LANES:]
             grad_ref[layer, 1, :width] = upper[:, LANES:] - lower[:, :LANES]
             bias = jnp.broadcast_to(jnp.sum(bias_total[layer], axis=0, keepdims=True), (SUB, 2 * LANES))
@@ -235,61 +258,46 @@
             grad_ref[layer, 1, width:] = bias[:, LANES:]
 
 
-def lat_back_kernel(size, s_ref, w_ref, f_ref, v_ref, keep, plain):
+def lat_back_kernel(size, s_ref, w_ref, f_ref, v_ref, plain):
     both, half = size.both, size.half
-    rows = size.batch * both
-    for at in range(0, rows, both):
-        high, low = split(s_ref[at : at + both])
-        keep[0, at : at + both] = high
-        keep[1, at : at + both] = low
-    plain[...] = mix(w_ref, 0, keep[0], keep[1])
-    for k in range(size.batch):
-        at = k * both
-        plus, minus = plain[at : at + half], plain[at + half : at + both]
-        add, sub = plus + minus, plus - minus
-        data = jnp.concatenate(
-            [
-                side_by_side(add[:, :LANES], -add[:, LANES:]),
-                side_by_side(sub[:, LANES:], sub[:, :LANES]),
-            ],
-            axis=0,
-        )
-        out = four_product(f_ref, data)
-        for q in range(2):
-            v_ref[q, k] = out[:, q * LANES : (q + 1) * LANES]
-
-
-def lon_back_kernel(size, width, v_hbm, t_ref, out_ref, v_ref, sem):
-    cols, slots = size.cols, size.slots
-    step = pl.program_id(0)
-    stride = size.row_slots
-    flat = out_ref.reshape(size.band * cols, width)
-
-    @pl.when(step == 0)
-    def _():
-        copies = []
-        for q in range(2):
-            tail = slots - size.freqs
-            if tail:
-                v_ref[pl.ds((q * slots + size.freqs) * stride, tail * stride), :] = jnp.zeros((tail * stride, LANES), F32)
-            copies.append(
-                pltpu.make_async_copy(
-                    v_hbm.at[q], v_ref.at[pl.ds(q * slots * stride, size.freqs * stride), :], sem.at[q]
-                )
+    span = CHUNK * both
+
+    def multiply(chunk):
+        here = slice(chunk * span, (chunk + 1) * span)
+        plain[here] = mix(w_ref, 0, *split(s_ref[here]))
+
+    def transform(chunk):
+        for k in range(chunk * CHUNK, (chunk + 1) * CHUNK):
+            at = k * both
+            plus, minus = plain[at : at + half], plain[at + half : at + both]
+            add, sub = plus + minus, plus - minus
+            data = jnp.concatenate(
+                [
+                    side_by_side(add[:, :LANES], -add[:, LANES:]),
+                    side_by_side(sub[:, LANES:], sub[:, :LANES]),
+                ],
+                axis=0,
             )
-            copies[-1].start()
-        for copy in copies:
-            copy.wait()
-
-    for pair in range(size.band // 2):
-        data = side_by_side(
-            *(
-                v_ref[pl.ds(step * size.band + 2 * pair + i, 2 * slots, stride=stride), :]
-                for i in range(2)
-            )
-        )
-        high, low = split(data)
-        out = three_product(t_ref, high, low)
+            out = four_product(f_ref, data)
+            for q in range(2):
+                v_ref[q, k] = out[:, q * LANES : (q + 1) * LANES]
+
+    count = size.batch // CHUNK
+    for t in range(count + 1):
+        if t < count:
+            multiply(t)
+        if t > 0:
+            transform(t - 1)
+
+
+def lon_back_kernel(size, width, v_ref, t_ref, out_ref):
+    cols = size.cols
+    lines = 2 * size.slots
+    flat = out_ref.reshape(SUB * cols, width)
+    rows = v_ref.reshape(lines * SUB, LANES)
+    for pair in range(SUB // 2):
+        data = side_by_side(*(rows[pl.ds(2 * pair + i, lines, stride=SUB), :] for i in range(2)))
+        out = three_product(t_ref, *split(data))
         for i in range(2):
             at = (2 * pair + i) * cols
             flat[at : at + cols, :] = out[:cols, i * LANES : i * LANES + width]
@@ -301,10 +309,10 @@
 
 
 def spectral_gradients(size, width, fields, weights, biases):
-    tables = [stacked(lon_table(size, which)) for which in (False, True)]
+    tables = [three_way(lon_table(size, which)) for which in (False, True)]
     tables += [four_way(lat_table(size, which)) for which in (False, True)]
     consts = [jnp.asarray(table) for table in tables] + [weights, biases]
-    bands, batches = size.rows // size.band, size.freqs // size.batch
+    bands, batches = size.rows // size.band, size.slots // size.batch
     rows = size.batch * size.both
     field = pl.BlockSpec((size.band * size.cols // SUB, SUB, width), lambda i: (jnp.minimum(i, bands - 1), 0, 0))
     return pl.pallas_call(
@@ -316,18 +324,18 @@
             pl.BlockSpec((2, 2, width + SUB, LANES), lambda i: (0, 0, 0, 0)),
         ],
         out_shape=[
-            jax.ShapeDtypeStruct((size.freqs * size.both, 2 * LANES), F32),
+            jax.ShapeDtypeStruct((size.slots * size.both, 2 * LANES), F32),
             jax.ShapeDtypeStruct((2, 2, width + SUB, LANES), F32),
         ],
         scratch_shapes=[
             pltpu.VMEM((size.band, 2, size.col_slots, 2 * LANES), BF16),
-            pltpu.VMEM((2, size.row_slots * 2 * size.slots, LANES), F32),
+            pltpu.VMEM((2, size.row_slots * size.stride, LANES), F32),
             pltpu.VMEM((4, 2, rows, 2 * LANES), BF16),
-            pltpu.VMEM((3, rows, 2 * LANES), F32),
-            pltpu.VMEM((2, 2 * LANES, 2 * LANES), F32),
+            pltpu.VMEM((4, rows, 2 * LANES), F32),
+            pltpu.VMEM((2, 2 * width, 2 * LANES), F32),
             pltpu.VMEM((2, SUB, 2 * LANES), F32),
         ],
-        compiler_params=pltpu.CompilerParams(vmem_limit_bytes=VMEM_LIMIT),
+        compiler_params=pltpu.CompilerParams(vmem_limit_bytes=40 << 20),
         name="spectral_gradients",
     )(*fields, *consts)
 
@@ -339,36 +347,28 @@
     rows = size.batch * size.both
     return pl.pallas_call(
         functools.partial(lat_back_kernel, size),
-        grid=(size.freqs // size.batch,),
+        grid=(size.slots // size.batch,),
         in_specs=[pl.BlockSpec((rows, 2 * LANES), lambda i: (i, 0))] + [whole_spec(const) for const in consts],
         out_specs=pl.BlockSpec((2, size.batch, size.row_slots, LANES), lambda i: (0, i, 0, 0)),
-        out_shape=jax.ShapeDtypeStruct((2, size.freqs, size.row_slots, LANES), F32),
-        scratch_shapes=[
-            pltpu.VMEM((2, rows, 2 * LANES), BF16),
-            pltpu.VMEM((rows, 2 * LANES), F32),
-        ],
-        compiler_params=pltpu.CompilerParams(vmem_limit_bytes=VMEM_LIMIT),
+        out_shape=jax.ShapeDtypeStruct((2, size.slots, size.row_slots, LANES), F32),
+        scratch_shapes=[pltpu.VMEM((rows, 2 * LANES), F32)],
+        compiler_params=pltpu.CompilerParams(vmem_limit_bytes=12 << 20),
         name="lat_back",
     )(s_modes, *consts)
 
 
 def lon_back(size, width, v_modes):
     lon = lon_table(size, False).T
-    table = jnp.asarray(stacked(lon))
-    flat = v_modes.reshape(2, size.freqs * size.row_slots, LANES)
+    table = jnp.asarray(three_way(lon))
     return pl.pallas_call(
         functools.partial(lon_back_kernel, size, width),
-        grid=(size.rows // size.band,),
-        in_specs=[pl.BlockSpec(memory_space=pl.ANY), whole_spec(table)],
-        out_specs=pl.BlockSpec((size.band * size.cols // SUB, SUB, width), lambda i: (i, 0, 0)),
+        grid=(size.row_slots // SUB,),
+        in_specs=[pl.BlockSpec((2, size.slots, SUB, LANES), lambda i: (0, 0, i, 0)), whole_spec(table)],
+        out_specs=pl.BlockSpec((size.cols, SUB, width), lambda i: (i, 0, 0)),
         out_shape=jax.ShapeDtypeStruct((size.rows * size.cols // SUB, SUB, width), F32),
-        scratch_shapes=[
-            pltpu.VMEM((2 * size.slots * size.row_slots, LANES), F32),
-            pltpu.SemaphoreType.DMA((2,)),
-        ],
-        compiler_params=pltpu.CompilerParams(vmem_limit_bytes=VMEM_LIMIT),
+        compiler_params=pltpu.CompilerParams(vmem_limit_bytes=12 << 20),
         name="lon_back",
-    )(flat, table)
+    )(v_modes, table)
 
 
 def mix_matrices(first, second):
@@ -380,7 +380,7 @@
     one, two = matrix(first), matrix(second)
     every = jnp.stack([one, two, two.T, one.T])
     high = lax.reduce_precision(every, 8, 7)
-    return jnp.stack([high, every - high], axis=1).astype(BF16)
+    return jnp.concatenate([high, high, every - high], axis=1).astype(BF16)
 
 
 def bias_rows(first, second):

time: 135 us -> 106 us (0.79)
  Pallas kernels: 102 us -> 64.3 us
  local copies, waits for them, and re-layouts: 5.8 us -> 13.2 us
  waiting for transfers between devices: 10.1 us -> 13.9 us
  other arithmetic: 2.55 us -> 0.43 us
    pallas_call x1, Pallas kernels: 68.8 us -> 44.7 us  [spectral_gradients(): pl.pallas_call(functools.partial(gradient_kernel, size, width, bands, bat...]
    unnamed x22 -> x36, local copies, waits for them, and re-layouts: 1.81 us -> 8.97 us
    pallas_call x1, Pallas kernels: 17 us -> 9.98 us  [lat_back(): pl.pallas_call(functools.partial(lat_back_kernel, size), grid=(size.slots...]
    pallas_call x1, Pallas kernels: 16.4 us -> 9.58 us  [lon_back(): pl.pallas_call(functools.partial(lon_back_kernel, size, width), grid=(siz...]
    ppermute x3, waiting for transfers between devices: 0.41 us -> 4.21 us  [sum_over_lat(): lax.ppermute(value, 'lat', [(i, (i + s) % count) for i in range(count)])]
    another operation x3 -> x1, other arithmetic: 1.83 us -> 0.16 us  [the longest x2 1.68 us: mix_matrices(): return jnp.stack([high, every - high], axis=1).astype(BF16)]
  transfers between devices with their start and end apart: 10 -> 10, of which waited for: 3 -> 3; matrix products, arithmetic and copies ran while one was open for 1% -> 0% of each run, Pallas kernels for 25% -> 19%
where the time goes in v3:
time: 106 us; the launch traced here: 105 us
  Pallas kernels  64.3 us (61%)
  waiting for transfers between devices  13.9 us (13%)
  local copies, waits for them, and re-layouts  13.2 us (12%)
  starting transfers between devices  12.5 us (12%)
    pallas_call x1, Pallas kernels, spectral_gradients(): pl.pallas_call(functools.partial(gradient_kernel, size, width, bands, bat...  44.7 us
    pallas_call x1, Pallas kernels, lat_back(): pl.pallas_call(functools.partial(lat_back_kernel, size), grid=(size.slots...  9.98 us
    ppermute x7, waiting for transfers between devices, gather_over_lon(): lax.ppermute(value, 'lon', [(i, i ^ s) for i in range(count)])  9.7 us
    pallas_call x1, Pallas kernels, lon_back(): pl.pallas_call(functools.partial(lon_back_kernel, size, width), grid=(siz...  9.58 us
    unnamed x36, local copies, waits for them, and re-layouts  8.97 us
    ppermute x7, starting transfers between devices, gather_over_lon(): lax.ppermute(value, 'lon', [(i, i ^ s) for i in range(count)])  6.47 us
    ppermute x3, starting transfers between devices, sum_over_lat(): lax.ppermute(value, 'lat', [(i, (i + s) % count) for i in range(count)])  6.07 us
    ppermute x3, waiting for transfers between devices, sum_over_lat(): lax.ppermute(value, 'lat', [(i, (i + s) % count) for i in range(count)])  4.21 us
  transfers between devices with their start and end apart: 10, of which 3 were waited for; matrix products, arithmetic and copies ran while one was open for 0% of the time, Pallas kernels for 19%

profile of v3, /device:TPU:0, one launch (start us, length us, event | category | flops | bytes accessed | tf_op | source)
XLA Modules:
  0.0 105.4 jit_solution(3307579234339042651)
XLA Ops:
  0.6 0.9 constant_dynamic-slice_fusion.4
  1.5 0.1 copy.30
  1.6 0.1 copy.31
  1.8 0.1 copy.34
  2.0 0.1 copy.24
  2.2 0.1 copy.23
  2.3 0.2 reduce-precision_convert_fusion
  2.5 0.1 pad_maximum_fusion
  2.7 0.9 constant_dynamic-slice_fusion.2
  3.8 3.4 %copy-done.1 = f32[1,96,90,180]{1,0,3,2:T(1,128)S(1)} copy-done((f32[1,96,90,180]{1,0,3,2:T(1,128)S(1)}, f32[1,96,90,180]{1,0,3,2:T(1,128)}, u32[]{:S(2)}) %copy-start.1) | copy-done | bytes 6220824
  7.1 44.7 %spectral_gradients.1 = (f32[9216,256]{1,0:T(8,128)}, f32[2,2,104,128]{3,2,1,0:T(8,128)S(1)}) custom-call(f32[2025,8,96]{2,1,0:T(8,128)S(1)} %bitcast.71, f32[2025,8,96]{2,1,0:T(8,128)} %bitcast.72, bf16[192,576]{1,0:T(8,128)(2,1)S(1)} %copy-done.3, bf16[192,576]{1,0:T(8,128)(2,1)S(1)} %copy-done.4, bf16[192,192]{1,0:T(8,128)(2,1)S(1)} %copy-done.6, ...), custom_call_target="tpu_custom_call" | custom-call | tf_op jit(solution)/shard_map/spectral_gradients/pallas_call | solution.py:318
  51.9 3.0 %collective-permute-start.1 = (f32[2,2,104,128]{3,2,1,0:T(8,128)S(1)}, f32[2,2,104,128]{3,2,1,0:T(8,128)S(1)}, u32[]{:S(2)}, u32[]{:S(2)}) collective-permute-start(f32[2,2,104,128]{3,2,1,0:T(8,128)S(1)} %get-tuple-element.9), channel_id=1, source_target_pairs={{0,8},{8,16},{16,24},{24,0},{1,9},{9,17},{17,25},{25,1},{2,10},{10... | collective-permute-start | bytes 638984 | tf_op jit(solution)/shard_map/ppermute | solution.py:396
  54.9 2.0 %collective-permute-start.2 = (f32[2,2,104,128]{3,2,1,0:T(8,128)S(1)}, f32[2,2,104,128]{3,2,1,0:T(8,128)S(1)}, u32[]{:S(2)}, u32[]{:S(2)}) collective-permute-start(f32[2,2,104,128]{3,2,1,0:T(8,128)S(1)} %get-tuple-element.9), channel_id=1, source_target_pairs={{0,24},{8,0},{16,8},{24,16},{1,25},{9,1},{17,9},{25,17},{2,26},{10... | collective-permute-start | bytes 638984 | tf_op jit(solution)/shard_map/ppermute | solution.py:396
  56.9 1.0 collective-permute-start
  58.0 3.7 %copy-done = f32[9216,256]{1,0:T(8,128)S(1)} copy-done((f32[9216,256]{1,0:T(8,128)S(1)}, f32[9216,256]{1,0:T(8,128)}, u32[]{:S(2)}) %copy-start) | copy-done | bytes 9437208
  61.7 10.0 %lat_back.1.v_ref = f32[2,96,96,128]{3,2,1,0:T(8,128)S(1)} custom-call(f32[9216,256]{1,0:T(8,128)S(1)} %copy-done, bf16[1,768,256]{2,1,0:T(8,128)(2,1)S(1)} %pad_maximum_fusion.2.w_ref, bf16[192,192]{1,0:T(8,128)(2,1)S(1)} %copy-done.5), custom_call_target="tpu_custom_call" | custom-call | tf_op jit(solution)/shard_map/lat_back/pallas_call | solution.py:348
  71.7 4.2 %collective-permute-done = f32[2,2,104,128]{3,2,1,0:T(8,128)S(1)} collective-permute-done((f32[2,2,104,128]{3,2,1,0:T(8,128)S(1)}, f32[2,2,104,128]{3,2,1,0:T(8,128)S(1)}, u32[]{:S(2)}, u32[]{:S(2)}) %collective-permute-start) | collective-permute-done | bytes 213024 | tf_op jit(solution)/shard_map/ppermute | solution.py:396
  75.9 0.1 collective-permute-start.3
  76.0 1.6 %collective-permute-start.4 = (f32[2,2,104,128]{3,2,1,0:T(8,128)S(1)}, f32[2,2,104,128]{3,2,1,0:T(8,128)S(1)}, u32[]{:S(2)}, u32[]{:S(2)}) collective-permute-start(f32[2,2,104,128]{3,2,1,0:T(8,128)S(1)} %add_add_fusion), channel_id=1, source_target_pairs={{0,2},{1,3},{2,0},{3,1},{4,6},{5,7},{6,4},{7,5},{8,10},{9,11},{10,... | collective-permute-start | bytes 638984 | tf_op jit(solution)/shard_map/ppermute | solution.py:404
  77.6 0.3 collective-permute-start.5
  77.9 1.5 %collective-permute-start.6 = (f32[2,2,104,128]{3,2,1,0:T(8,128)S(1)}, f32[2,2,104,128]{3,2,1,0:T(8,128)S(1)}, u32[]{:S(2)}, u32[]{:S(2)}) collective-permute-start(f32[2,2,104,128]{3,2,1,0:T(8,128)S(1)} %add_add_fusion), channel_id=1, source_target_pairs={{0,4},{1,5},{2,6},{3,7},{4,0},{5,1},{6,2},{7,3},{8,12},{9,13},{10,... | collective-permute-start | bytes 638984 | tf_op jit(solution)/shard_map/ppermute | solution.py:404
  79.4 0.2 collective-permute-start.7
  79.6 9.6 %lon_back.1 = f32[2025,8,96]{2,1,0:T(8,128)} custom-call(f32[2,96,96,128]{3,2,1,0:T(8,128)S(1)} %lat_back.1.v_ref, bf16[192,576]{1,0:T(8,128)(2,1)S(1)} %copy-done.2), custom_call_target="tpu_custom_call" | custom-call | tf_op jit(solution)/shard_map/lon_back/pallas_call | solution.py:363
  89.2 2.5 %collective-permute-start.8 = (f32[2,2,104,128]{3,2,1,0:T(8,128)S(1)}, f32[2,2,104,128]{3,2,1,0:T(8,128)S(1)}, u32[]{:S(2)}, u32[]{:S(2)}) collective-permute-start(f32[2,2,104,128]{3,2,1,0:T(8,128)S(1)} %add_add_fusion), channel_id=1, source_target_pairs={{0,6},{1,7},{2,4},{3,5},{4,2},{5,3},{6,0},{7,1},{8,14},{9,15},{10,... | collective-permute-start | bytes 638984 | tf_op jit(solution)/shard_map/ppermute | solution.py:404
  91.7 0.3 collective-permute-start.9
  92.2 6.0 %collective-permute-done.8 = f32[2,2,104,128]{3,2,1,0:T(8,128)S(1)} collective-permute-done((f32[2,2,104,128]{3,2,1,0:T(8,128)S(1)}, f32[2,2,104,128]{3,2,1,0:T(8,128)S(1)}, u32[]{:S(2)}, u32[]{:S(2)}) %collective-permute-start.8) | collective-permute-done | bytes 213024 | tf_op jit(solution)/shard_map/ppermute | solution.py:404
  98.2 3.7 %collective-permute-done.9 = f32[2,2,104,128]{3,2,1,0:T(8,128)S(1)} collective-permute-done((f32[2,2,104,128]{3,2,1,0:T(8,128)S(1)}, f32[2,2,104,128]{3,2,1,0:T(8,128)S(1)}, u32[]{:S(2)}, u32[]{:S(2)}) %collective-permute-start.9) | collective-permute-done | bytes 213024 | tf_op jit(solution)/shard_map/ppermute | solution.py:404
  102.1 0.2 fusion.6
  102.3 0.9 copy.38
  103.3 0.6 copy.27
  103.9 0.9 copy.37
  104.8 0.6 copy.28
  (51 shorter events, 0.8 us)
Async XLA Ops:
  2.6 1.1 %copy-start.3 = (bf16[192,576]{1,0:T(8,128)(2,1)S(1)}, bf16[192,576]{1,0:T(8,128)(2,1)}, u32[]{:S(2)}) copy-start(bf16[192,576]{1,0:T(8,128)(2,1)} %constant.65.clone.tx_ref) | copy-start | bytes 663556
  2.6 1.1 %copy-start.4 = (bf16[192,576]{1,0:T(8,128)(2,1)S(1)}, bf16[192,576]{1,0:T(8,128)(2,1)}, u32[]{:S(2)}) copy-start(bf16[192,576]{1,0:T(8,128)(2,1)} %constant.66.clone.tg_ref) | copy-start | bytes 663556
  2.6 1.1 %copy-start.6 = (bf16[192,192]{1,0:T(8,128)(2,1)S(1)}, bf16[192,192]{1,0:T(8,128)(2,1)}, u32[]{:S(2)}) copy-start(bf16[192,192]{1,0:T(8,128)(2,1)} %constant.67.clone.fx_ref) | copy-start | bytes 221188
  2.6 1.2 %copy-start.7 = (bf16[192,192]{1,0:T(8,128)(2,1)S(1)}, bf16[192,192]{1,0:T(8,128)(2,1)}, u32[]{:S(2)}) copy-start(bf16[192,192]{1,0:T(8,128)(2,1)} %constant.68.clone.fg_ref) | copy-start | bytes 221188
  3.8 3.4 %copy-start.1 = (f32[1,96,90,180]{1,0,3,2:T(1,128)S(1)}, f32[1,96,90,180]{1,0,3,2:T(1,128)}, u32[]{:S(2)}) copy-start(f32[1,96,90,180]{1,0,3,2:T(1,128)} %param.12) | copy-start | bytes 18662404
  7.1 50.8 %copy-start.5 = (bf16[192,192]{1,0:T(8,128)(2,1)S(1)}, bf16[192,192]{1,0:T(8,128)(2,1)}, u32[]{:S(2)}) copy-start(bf16[192,192]{1,0:T(8,128)(2,1)} %constant.69.clone.f_ref) | copy-start | bytes 221188
  51.9 19.8 %collective-permute-start.1 = (f32[2,2,104,128]{3,2,1,0:T(8,128)S(1)}, f32[2,2,104,128]{3,2,1,0:T(8,128)S(1)}, u32[]{:S(2)}, u32[]{:S(2)}) collective-permute-start(f32[2,2,104,128]{3,2,1,0:T(8,128)S(1)} %get-tuple-element.9), channel_id=1, source_target_pairs={{0,8},{8,16},{16,24},{24,0},{1,9},{9,17},{17,25},{25,1},{2,10},{10... | collective-permute-start | bytes 638984 | tf_op jit(solution)/shard_map/ppermute | solution.py:396
  54.9 16.8 %collective-permute-start.2 = (f32[2,2,104,128]{3,2,1,0:T(8,128)S(1)}, f32[2,2,104,128]{3,2,1,0:T(8,128)S(1)}, u32[]{:S(2)}, u32[]{:S(2)}) collective-permute-start(f32[2,2,104,128]{3,2,1,0:T(8,128)S(1)} %get-tuple-element.9), channel_id=1, source_target_pairs={{0,24},{8,0},{16,8},{24,16},{1,25},{9,1},{17,9},{25,17},{2,26},{10... | collective-permute-start | bytes 638984 | tf_op jit(solution)/shard_map/ppermute | solution.py:396
  56.9 18.9 %collective-permute-start = (f32[2,2,104,128]{3,2,1,0:T(8,128)S(1)}, f32[2,2,104,128]{3,2,1,0:T(8,128)S(1)}, u32[]{:S(2)}, u32[]{:S(2)}) collective-permute-start(f32[2,2,104,128]{3,2,1,0:T(8,128)S(1)} %get-tuple-element.9), channel_id=1, source_target_pairs={{0,16},{8,24},{16,0},{24,8},{1,17},{9,25},{17,1},{25,9},{2,18},{10... | collective-permute-start | bytes 638984 | tf_op jit(solution)/shard_map/ppermute | solution.py:396
  58.0 3.7 %copy-start = (f32[9216,256]{1,0:T(8,128)S(1)}, f32[9216,256]{1,0:T(8,128)}, u32[]{:S(2)}) copy-start(f32[9216,256]{1,0:T(8,128)} %get-tuple-element.10.s_ref) | copy-start | bytes 28311556
  61.7 17.9 %copy-start.2 = (bf16[192,576]{1,0:T(8,128)(2,1)S(1)}, bf16[192,576]{1,0:T(8,128)(2,1)}, u32[]{:S(2)}) copy-start(bf16[192,576]{1,0:T(8,128)(2,1)} %constant.70.clone.t_ref) | copy-start | bytes 663556
  75.9 13.2 %collective-permute-start.3 = (f32[2,2,104,128]{3,2,1,0:T(8,128)S(1)}, f32[2,2,104,128]{3,2,1,0:T(8,128)S(1)}, u32[]{:S(2)}, u32[]{:S(2)}) collective-permute-start(f32[2,2,104,128]{3,2,1,0:T(8,128)S(1)} %add_add_fusion), channel_id=1, source_target_pairs={{0,1},{1,0},{2,3},{3,2},{4,5},{5,4},{6,7},{7,6},{8,9},{9,8},{10,11... | collective-permute-start | bytes 638984 | tf_op jit(solution)/shard_map/ppermute | solution.py:404
  76.0 15.7 %collective-permute-start.4 = (f32[2,2,104,128]{3,2,1,0:T(8,128)S(1)}, f32[2,2,104,128]{3,2,1,0:T(8,128)S(1)}, u32[]{:S(2)}, u32[]{:S(2)}) collective-permute-start(f32[2,2,104,128]{3,2,1,0:T(8,128)S(1)} %add_add_fusion), channel_id=1, source_target_pairs={{0,2},{1,3},{2,0},{3,1},{4,6},{5,7},{6,4},{7,5},{8,10},{9,11},{10,... | collective-permute-start | bytes 638984 | tf_op jit(solution)/shard_map/ppermute | solution.py:404
  77.6 14.5 %collective-permute-start.5 = (f32[2,2,104,128]{3,2,1,0:T(8,128)S(1)}, f32[2,2,104,128]{3,2,1,0:T(8,128)S(1)}, u32[]{:S(2)}, u32[]{:S(2)}) collective-permute-start(f32[2,2,104,128]{3,2,1,0:T(8,128)S(1)} %add_add_fusion), channel_id=1, source_target_pairs={{0,3},{1,2},{2,1},{3,0},{4,7},{5,6},{6,5},{7,4},{8,11},{9,10},{10,... | collective-permute-start | bytes 638984 | tf_op jit(solution)/shard_map/ppermute | solution.py:404
  77.9 14.2 %collective-permute-start.6 = (f32[2,2,104,128]{3,2,1,0:T(8,128)S(1)}, f32[2,2,104,128]{3,2,1,0:T(8,128)S(1)}, u32[]{:S(2)}, u32[]{:S(2)}) collective-permute-start(f32[2,2,104,128]{3,2,1,0:T(8,128)S(1)} %add_add_fusion), channel_id=1, source_target_pairs={{0,4},{1,5},{2,6},{3,7},{4,0},{5,1},{6,2},{7,3},{8,12},{9,13},{10,... | collective-permute-start | bytes 638984 | tf_op jit(solution)/shard_map/ppermute | solution.py:404
  79.4 12.7 %collective-permute-start.7 = (f32[2,2,104,128]{3,2,1,0:T(8,128)S(1)}, f32[2,2,104,128]{3,2,1,0:T(8,128)S(1)}, u32[]{:S(2)}, u32[]{:S(2)}) collective-permute-start(f32[2,2,104,128]{3,2,1,0:T(8,128)S(1)} %add_add_fusion), channel_id=1, source_target_pairs={{0,5},{1,4},{2,7},{3,6},{4,1},{5,0},{6,3},{7,2},{8,13},{9,12},{10,... | collective-permute-start | bytes 638984 | tf_op jit(solution)/shard_map/ppermute | solution.py:404
  89.2 9.0 %collective-permute-start.8 = (f32[2,2,104,128]{3,2,1,0:T(8,128)S(1)}, f32[2,2,104,128]{3,2,1,0:T(8,128)S(1)}, u32[]{:S(2)}, u32[]{:S(2)}) collective-permute-start(f32[2,2,104,128]{3,2,1,0:T(8,128)S(1)} %add_add_fusion), channel_id=1, source_target_pairs={{0,6},{1,7},{2,4},{3,5},{4,2},{5,3},{6,0},{7,1},{8,14},{9,15},{10,... | collective-permute-start | bytes 638984 | tf_op jit(solution)/shard_map/ppermute | solution.py:404
  91.7 10.1 %collective-permute-start.9 = (f32[2,2,104,128]{3,2,1,0:T(8,128)S(1)}, f32[2,2,104,128]{3,2,1,0:T(8,128)S(1)}, u32[]{:S(2)}, u32[]{:S(2)}) collective-permute-start(f32[2,2,104,128]{3,2,1,0:T(8,128)S(1)} %add_add_fusion), channel_id=1, source_target_pairs={{0,7},{1,6},{2,5},{3,4},{4,3},{5,2},{6,1},{7,0},{8,15},{9,14},{10,... | collective-permute-start | bytes 638984 | tf_op jit(solution)/shard_map/ppermute | solution.py:404

commit v4 on v3

--- a/solution.py
+++ b/solution.py
@@ -19,6 +19,11 @@
 F32 = jnp.float32
 BF16 = jnp.bfloat16
 CHUNK = 4
+BAND_MOST = 10
+PARTS = 2
+GRADIENT_VMEM = 54 << 20
+LAT_VMEM = 24 << 20
+LON_VMEM = 24 << 20
 
 
 def round_up(value, unit):
@@ -62,7 +67,7 @@
         self.stride = round_up(2 * self.slots, 2 * SUB) + SUB
         self.row_slots = round_up(rows, 16)
         self.col_slots = round_up(cols, 16)
-        self.band = max((n for n in range(2, 11, 2) if rows % n == 0 and n * cols % SUB == 0), default=0)
+        self.band = max((n for n in range(2, BAND_MOST + 1, 2) if rows % n == 0 and n * cols % SUB == 0), default=0)
         self.batch = SUB
 
     def fits(self):
@@ -116,9 +121,22 @@
     return dot(jnp.concatenate([high, low, high], axis=1), weight_ref[which])
 
 
+def fill_matrix(out, width, real, imag, turned):
+    if turned:
+        real, imag = real.T, imag.T
+    sign = -1.0 if turned else 1.0
+    span = 2 * LANES
+    for row, column, value in ((0, 0, real), (1, 1, real), (0, 1, sign * imag), (1, 0, -sign * imag)):
+        high, low = split(value)
+        columns = slice(column * LANES, column * LANES + width)
+        for third, part in enumerate((high, high, low)):
+            at = third * span + row * LANES
+            out[at : at + width, columns] = part
+
+
 def gradient_kernel(
-    size, width, bands, batches, x_ref, g_ref, tx_ref, tg_ref, fx_ref, fg_ref, w_ref, b_ref,
-    s_ref, grad_ref, fold, spectra, keep, plain, total, bias_total,
+    size, width, bands, batches, at_ref, x_ref, g_ref, tx_ref, tg_ref, fx_ref, fg_ref, wa_ref, wb_ref, ba_ref, bb_ref,
+    s_ref, grad_ref, fold, spectra, keep, plain, total, bias_total, w_ref, b_ref,
 ):
     step = pl.program_id(0)
     cols, slots, both, half = size.cols, size.slots, size.both, size.half
@@ -131,6 +149,15 @@
         fold[...] = jnp.zeros_like(fold)
         total[...] = jnp.zeros_like(total)
         bias_total[...] = jnp.zeros_like(bias_total)
+        w_ref[...] = jnp.zeros_like(w_ref)
+        b_ref[...] = jnp.zeros_like(b_ref)
+        fill_matrix(w_ref.at[0], width, wa_ref[0, 0], wa_ref[1, 0], False)
+        fill_matrix(w_ref.at[1], width, wb_ref[0, 0], wb_ref[1, 0], False)
+        fill_matrix(w_ref.at[2], width, wb_ref[0, 0], wb_ref[1, 0], True)
+        for layer, bias in enumerate((ba_ref, bb_ref)):
+            for q in range(2):
+                row = bias[q, pl.ds(at_ref[1], 1), :]
+                b_ref[layer, :, q * LANES : q * LANES + width] = jnp.broadcast_to(row, (SUB, width))
         for which in range(2):
             spectra[which, size.rows * stride :] = jnp.zeros(((size.row_slots - size.rows) * stride, LANES), F32)
 
@@ -190,7 +217,7 @@
 
         def activate(chunk):
             for here in pieces(chunk):
-                a = plain[1, here] + b_ref[0]
+                a = plain[1, here] + b_ref[0, :1]
                 square = a * a
                 tangent = jnp.tanh(a * (GELU_SCALE + (GELU_SCALE * GELU_CUBE) * square))
                 part = 0.5 * a
@@ -202,7 +229,7 @@
         def gate(chunk):
             sums = jnp.zeros((SUB, 2 * LANES), F32)
             for here in pieces(chunk):
-                tangent = jnp.tanh((plain[2, here] + b_ref[1]) * (1.0 / SHRINK))
+                tangent = jnp.tanh((plain[2, here] + b_ref[1, :1]) * (1.0 / SHRINK))
                 e = plain[0, here] * (tangent * tangent)
                 for i in range(0, piece, SUB):
                     sums = sums + e[i : i + SUB]
@@ -258,9 +285,14 @@
             grad_ref[layer, 1, width:] = bias[:, LANES:]
 
 
-def lat_back_kernel(size, s_ref, w_ref, f_ref, v_ref, plain):
+def lat_back_kernel(size, width, at_ref, s_ref, wa_ref, f_ref, v_ref, plain, w_ref):
     both, half = size.both, size.half
     span = CHUNK * both
+
+    @pl.when(pl.program_id(0) == 0)
+    def _():
+        w_ref[...] = jnp.zeros_like(w_ref)
+        fill_matrix(w_ref.at[0], width, wa_ref[0, 0], wa_ref[1, 0], True)
 
     def multiply(chunk):
         here = slice(chunk * span, (chunk + 1) * span)
@@ -290,150 +322,184 @@
             transform(t - 1)
 
 
-def lon_back_kernel(size, width, v_ref, t_ref, out_ref):
+def lon_back_kernel(size, width, *refs):
+    v_refs, (t_ref, out_ref) = refs[:PARTS], refs[PARTS:]
     cols = size.cols
-    lines = 2 * size.slots
+    lines = size.slots // PARTS
     flat = out_ref.reshape(SUB * cols, width)
-    rows = v_ref.reshape(lines * SUB, LANES)
+    rows = [ref.reshape(2 * lines * SUB, LANES) for ref in v_refs]
     for pair in range(SUB // 2):
-        data = side_by_side(*(rows[pl.ds(2 * pair + i, lines, stride=SUB), :] for i in range(2)))
+        data = side_by_side(
+            *(
+                jnp.concatenate(
+                    [
+                        part[pl.ds(q * lines * SUB + 2 * pair + i, lines, stride=SUB), :]
+                        for q in range(2)
+                        for part in rows
+                    ],
+                    axis=0,
+                )
+                for i in range(2)
+            )
+        )
         out = three_product(t_ref, *split(data))
         for i in range(2):
             at = (2 * pair + i) * cols
             flat[at : at + cols, :] = out[:cols, i * LANES : i * LANES + width]
 
 
+def assemble_kernel(width, count, at_ref, *refs):
+    parts, (wa_ref, wb_ref, ba_ref, bb_ref) = refs[:count], refs[count:]
+    for l, (weight, bias) in enumerate(((wa_ref, ba_ref), (wa_ref, ba_ref), (wb_ref, bb_ref), (wb_ref, bb_ref))):
+        shift = lax.rem(at_ref[0] + 4 - l, 4)
+        for x in range(count):
+            block = at_ref[2 + x]
+            weight[l % 2, block] = parts[x][shift, :width, :width]
+            bias[l % 2, pl.ds(block, 1), :] = parts[x][shift, width : width + 1, :width]
+
+
 def whole_spec(array):
     zeros = (0,) * array.ndim
     return pl.BlockSpec(array.shape, lambda *_: zeros)
 
 
-def spectral_gradients(size, width, fields, weights, biases):
+def spectral_gradients(size, place, fields, first_weight, first_bias, second_weight, second_bias):
+    width = first_weight.shape[-1]
     tables = [three_way(lon_table(size, which)) for which in (False, True)]
     tables += [four_way(lat_table(size, which)) for which in (False, True)]
-    consts = [jnp.asarray(table) for table in tables] + [weights, biases]
+    consts = [jnp.asarray(table) for table in tables]
+    weight = pl.BlockSpec((2, 1, width, width), lambda i, at: (0, at[1], 0, 0))
+    bias = whole_spec(first_bias)
     bands, batches = size.rows // size.band, size.slots // size.batch
     rows = size.batch * size.both
-    field = pl.BlockSpec((size.band * size.cols // SUB, SUB, width), lambda i: (jnp.minimum(i, bands - 1), 0, 0))
+    field = pl.BlockSpec((size.band * size.cols // SUB, SUB, width), lambda i, at: (jnp.minimum(i, bands - 1), 0, 0))
     return pl.pallas_call(
         functools.partial(gradient_kernel, size, width, bands, batches),
-        grid=(bands + batches,),
-        in_specs=[field, field] + [whole_spec(const) for const in consts],
-        out_specs=[
-            pl.BlockSpec((rows, 2 * LANES), lambda i: (jnp.maximum(i - bands, 0), 0)),
-            pl.BlockSpec((2, 2, width + SUB, LANES), lambda i: (0, 0, 0, 0)),
-        ],
+        grid_spec=pltpu.PrefetchScalarGridSpec(
+            num_scalar_prefetch=1,
+            grid=(bands + batches,),
+            in_specs=[field, field] + [whole_spec(const) for const in consts] + [weight, weight, bias, bias],
+            out_specs=[
+                pl.BlockSpec((rows, 2 * LANES), lambda i, at: (jnp.maximum(i - bands, 0), 0)),
+                pl.BlockSpec((2, 2, width + SUB, LANES), lambda i, at: (0, 0, 0, 0)),
+            ],
+            scratch_shapes=[
+                pltpu.VMEM((size.band, 2, size.col_slots, 2 * LANES), BF16),
+                pltpu.VMEM((2, size.row_slots * size.stride, LANES), F32),
+                pltpu.VMEM((4, 2, rows, 2 * LANES), BF16),
+                pltpu.VMEM((4, rows, 2 * LANES), F32),
+                pltpu.VMEM((2, 2 * width, 2 * LANES), F32),
+                pltpu.VMEM((2, SUB, 2 * LANES), F32),
+                pltpu.VMEM((3, 6 * LANES, 2 * LANES), BF16),
+                pltpu.VMEM((2, SUB, 2 * LANES), F32),
+            ],
+        ),
         out_shape=[
             jax.ShapeDtypeStruct((size.slots * size.both, 2 * LANES), F32),
             jax.ShapeDtypeStruct((2, 2, width + SUB, LANES), F32),
         ],
-        scratch_shapes=[
-            pltpu.VMEM((size.band, 2, size.col_slots, 2 * LANES), BF16),
-            pltpu.VMEM((2, size.row_slots * size.stride, LANES), F32),
-            pltpu.VMEM((4, 2, rows, 2 * LANES), BF16),
-            pltpu.VMEM((4, rows, 2 * LANES), F32),
-            pltpu.VMEM((2, 2 * width, 2 * LANES), F32),
-            pltpu.VMEM((2, SUB, 2 * LANES), F32),
-        ],
-        compiler_params=pltpu.CompilerParams(vmem_limit_bytes=40 << 20),
+        compiler_params=pltpu.CompilerParams(vmem_limit_bytes=GRADIENT_VMEM),
         name="spectral_gradients",
-    )(*fields, *consts)
-
-
-def lat_back(size, s_modes, weights):
+    )(place, *fields, *consts, first_weight, second_weight, first_bias, second_bias)
+
+
+def lat_back(size, place, s_modes, weight, part):
+    width = weight.shape[-1]
     lat = lat_table(size, False).T.copy()
     lat[:, size.half :] *= -1.0
-    consts = [weights, jnp.asarray(four_way(lat))]
+    table = jnp.asarray(four_way(lat))
     rows = size.batch * size.both
+    steps = size.slots // size.batch // PARTS
     return pl.pallas_call(
-        functools.partial(lat_back_kernel, size),
-        grid=(size.slots // size.batch,),
-        in_specs=[pl.BlockSpec((rows, 2 * LANES), lambda i: (i, 0))] + [whole_spec(const) for const in consts],
-        out_specs=pl.BlockSpec((2, size.batch, size.row_slots, LANES), lambda i: (0, i, 0, 0)),
-        out_shape=jax.ShapeDtypeStruct((2, size.slots, size.row_slots, LANES), F32),
-        scratch_shapes=[pltpu.VMEM((rows, 2 * LANES), F32)],
-        compiler_params=pltpu.CompilerParams(vmem_limit_bytes=12 << 20),
+        functools.partial(lat_back_kernel, size, width),
+        grid_spec=pltpu.PrefetchScalarGridSpec(
+            num_scalar_prefetch=1,
+            grid=(steps,),
+            in_specs=[
+                pl.BlockSpec((rows, 2 * LANES), lambda i, at: (part * steps + i, 0)),
+                pl.BlockSpec((2, 1, width, width), lambda i, at: (0, at[1], 0, 0)),
+                whole_spec(table),
+            ],
+            out_specs=pl.BlockSpec((2, size.batch, size.row_slots, LANES), lambda i, at: (0, i, 0, 0)),
+            scratch_shapes=[pltpu.VMEM((rows, 2 * LANES), F32), pltpu.VMEM((1, 6 * LANES, 2 * LANES), BF16)],
+        ),
+        out_shape=jax.ShapeDtypeStruct((2, size.slots // PARTS, size.row_slots, LANES), F32),
+        compiler_params=pltpu.CompilerParams(vmem_limit_bytes=LAT_VMEM),
         name="lat_back",
-    )(s_modes, *consts)
-
-
-def lon_back(size, width, v_modes):
-    lon = lon_table(size, False).T
-    table = jnp.asarray(three_way(lon))
+    )(place, s_modes, weight, table)
+
+
+def lon_back(size, width, v_parts):
+    table = jnp.asarray(three_way(lon_table(size, False).T))
+    field = pl.BlockSpec((2, size.slots // PARTS, SUB, LANES), lambda i: (0, 0, i, 0))
     return pl.pallas_call(
         functools.partial(lon_back_kernel, size, width),
         grid=(size.row_slots // SUB,),
-        in_specs=[pl.BlockSpec((2, size.slots, SUB, LANES), lambda i: (0, 0, i, 0)), whole_spec(table)],
+        in_specs=[field] * PARTS + [whole_spec(table)],
         out_specs=pl.BlockSpec((size.cols, SUB, width), lambda i: (i, 0, 0)),
         out_shape=jax.ShapeDtypeStruct((size.rows * size.cols // SUB, SUB, width), F32),
-        compiler_params=pltpu.CompilerParams(vmem_limit_bytes=12 << 20),
+        compiler_params=pltpu.CompilerParams(vmem_limit_bytes=LON_VMEM),
         name="lon_back",
-    )(v_modes, table)
-
-
-def mix_matrices(first, second):
-    def matrix(weight):
-        pad = LANES - weight.shape[-1]
-        real, imag = (jnp.pad(part, ((0, pad), (0, pad))) for part in (weight[0], weight[1]))
-        return jnp.concatenate([side_by_side(real, imag), side_by_side(-imag, real)], 0)
-
-    one, two = matrix(first), matrix(second)
-    every = jnp.stack([one, two, two.T, one.T])
-    high = lax.reduce_precision(every, 8, 7)
-    return jnp.concatenate([high, high, every - high], axis=1).astype(BF16)
-
-
-def bias_rows(first, second):
-    pad = LANES - first.shape[-1]
-    return jnp.stack([jnp.pad(part, ((0, 0), (0, pad))).reshape(1, 2 * LANES) for part in (first, second)])
-
-
-def sum_over_lat(value):
-    count = lax.axis_size("lat")
-    if count != 4:
-        return lax.psum(value, "lat")
-    one, two, three = (
-        lax.ppermute(value, "lat", [(i, (i + s) % count) for i in range(count)]) for s in (1, 2, 3)
-    )
-    return (value + two) + (one + three)
-
-
-def gather_over_lon(value):
-    count = lax.axis_size("lon")
-    me = lax.axis_index("lon")
-    parts = [value] + [lax.ppermute(value, "lon", [(i, i ^ s) for i in range(count)]) for s in range(1, count)]
-    return parts, me
+    )(*v_parts, table)
+
+
+def assemble(place, parts, width):
+    count = len(parts)
+    shapes = [(2, count, width, width)] * 2 + [(2, count, width)] * 2
+    memory = pl.BlockSpec(memory_space=pltpu.VMEM)
+    return pl.pallas_call(
+        functools.partial(assemble_kernel, width, count),
+        in_specs=[pl.BlockSpec(memory_space=pltpu.SMEM)] + [memory] * count,
+        out_specs=[memory] * 4,
+        out_shape=[jax.ShapeDtypeStruct(shape, F32) for shape in shapes],
+        compiler_params=pltpu.CompilerParams(vmem_limit_bytes=LON_VMEM),
+        name="assemble",
+    )(place, *parts)
+
+
+def shifted(value, axis, shift):
+    count = lax.axis_size(axis)
+    return lax.ppermute(value, axis, [(i, (i + shift) % count) for i in range(count)])
+
+
+def crossed(value, axis, mask):
+    count = lax.axis_size(axis)
+    return lax.ppermute(value, axis, [(i, i ^ mask) for i in range(count)])
 
 
 def whole_block(layer_input, grad_output, first_weight, first_bias, second_weight, second_bias):
     _, width, lat_rows, lon_cols = layer_input.shape
     size = Sizes(lat_rows, lon_cols)
-    block = lax.axis_index("lon")
-
-    def mine(weight):
-        return lax.dynamic_index_in_dim(weight, block, axis=1, keepdims=False)
-
+    at_lat, at_lon = lax.axis_index("lat"), lax.axis_index("lon")
+    place = jnp.stack([at_lat, at_lon] + [at_lon ^ x for x in range(lax.axis_size("lon"))])
     fields = [
-        jnp.transpose(field, (0, 2, 3, 1)).reshape(-1, SUB, width)
-        for field in (layer_input, grad_output)
+        jnp.transpose(field, (0, 2, 3, 1)).reshape(-1, SUB, width) for field in (layer_input, grad_output)
     ]
-    weights = mix_matrices(mine(first_weight), mine(second_weight))
     s_modes, partial = spectral_gradients(
-        size, width, fields, weights[:3], bias_rows(mine(first_bias), mine(second_bias))
-    )
-    summed = sum_over_lat(partial)
-    v_modes = lat_back(size, s_modes, weights[3:])
-    summed, v_modes = lax.optimization_barrier((summed, v_modes))
-    parts, me = gather_over_lon(summed)
-    out = lon_back(size, width, v_modes)
+        size, place, fields, first_weight, first_bias, second_weight, second_bias
+    )
+    matrices = partial.reshape(4, width + SUB, LANES)
+
+    def matrix(shift):
+        return lax.dynamic_index_in_dim(matrices, (at_lat + shift) % 4, 0, keepdims=False)
+
+    far = [shifted(matrix(shift), "lat", shift) for shift in (1, 2, 3)]
+    v_first = lat_back(size, place, s_modes, first_weight, 0)
+    far, v_first, s_modes = lax.optimization_barrier((far, v_first, s_modes))
+    mine = (matrix(0) + far[1]) + (far[0] + far[2])
+    others = [shifted(mine, "lat", shift) for shift in (1, 2, 3)]
+    v_second = lat_back(size, place, s_modes, first_weight, 1)
+    others, v_first, v_second = lax.optimization_barrier((others, v_first, v_second))
+    own = jnp.stack([mine] + others)
+    chips = [crossed(own, "lon", mask) for mask in (2, 4, 6)]
+    near = crossed(own, "lon", 1)
+    out = lon_back(size, width, [v_first, v_second])
+    chips, near, out = lax.optimization_barrier((chips, near, out))
+    rest = [crossed(chip, "lon", 1) for chip in chips]
+    parts = [own, near, chips[0], rest[0], chips[1], rest[1], chips[2], rest[2]]
+    weight_one, weight_two, bias_one, bias_two = assemble(place, parts, width)
     grad_input = out.reshape(lat_rows * lon_cols, width).T.reshape(1, width, lat_rows, lon_cols)
-    stack = jnp.stack(parts)
-    whole = jnp.stack(
-        [lax.dynamic_index_in_dim(stack, me ^ b, 0, keepdims=False) for b in range(len(parts))], axis=2
-    )
-    weight_grads = whole[:, :, :, :width, :width]
-    bias_grads = whole[:, :, :, width, :width]
-    return (grad_input, weight_grads[0], bias_grads[0], weight_grads[1], bias_grads[1])
+    return (grad_input, weight_one, bias_one, weight_two, bias_two)
 
 
 def tables(length, count, limit):
@@ -571,6 +637,7 @@
     samples, local_ch, lat_rows, lon_cols = layer_input.shape
     width = first_weight.shape[2]
     one_device = samples == 1 and local_ch == width <= LANES and width % SUB == 0
+    one_device = one_device and lax.axis_size("lat") == 4 and lax.axis_size("lon") == 8
     run = whole_block if one_device and Sizes(lat_rows, lon_cols).fits() else spread_block
     return run(layer_input, grad_output, first_weight, first_bias, second_weight, second_bias)
 

time: 106 us -> 94.2 us (0.89)
  waiting for transfers between devices: 13.9 us -> 1.56 us
  local copies, waits for them, and re-layouts: 13.2 us -> 5.19 us
  Pallas kernels: 64.3 us -> 70.9 us
  starting transfers between devices: 12.5 us -> 14.4 us
    ppermute x10 -> x13, waiting for transfers between devices: 13.9 us -> 1.56 us  [the longest x7 1.51 us: crossed(): return lax.ppermute(value, axis, [(i, i ^ mask) for i in range(count)])]
    unnamed x36 -> x10, local copies, waits for them, and re-layouts: 8.97 us -> 3.7 us
    pallas_call x1 -> x3, Pallas kernels: 9.98 us -> 13.6 us  [the longest x2 11.8 us: lat_back(): pl.pallas_call(functools.partial(lat_back_kernel, size, width), grid_spec...]
    slice x6 -> x0, local copies, waits for them, and re-layouts: 3.02 us -> none  [the longest x2 1.11 us: whole_block(): weight_grads[1]]
    pallas_call x1, Pallas kernels: 44.7 us -> 47.7 us  [spectral_gradients(): pl.pallas_call(functools.partial(gradient_kernel, size, width, bands, bat...]
    ppermute x10 -> x13, starting transfers between devices: 12.5 us -> 14.4 us  [the longest x6 10.1 us: shifted(): lax.ppermute(value, axis, [(i, (i + shift) % count) for i in range(count)])]
  transfers between devices with their start and end apart: 10 -> 13, of which waited for: 3 -> 3; matrix products, arithmetic and copies ran while one was open for 0% -> 0% of each run, Pallas kernels for 19% -> 23%
where the time goes in v4:
time: 94.2 us; the launch traced here: 93.7 us
  Pallas kernels  70.9 us (75%)
  starting transfers between devices  14.4 us (15%)
  local copies, waits for them, and re-layouts  5.19 us (6%)
  waiting for transfers between devices  1.56 us (2%)
    pallas_call x1, Pallas kernels, spectral_gradients(): pl.pallas_call(functools.partial(gradient_kernel, size, width, bands, bat...  47.7 us
    pallas_call x2, Pallas kernels, lat_back(): pl.pallas_call(functools.partial(lat_back_kernel, size, width), grid_spec...  11.8 us
    ppermute x6, starting transfers between devices, shifted(): lax.ppermute(value, axis, [(i, (i + shift) % count) for i in range(count)])  10.1 us
    pallas_call x1, Pallas kernels, lon_back(): pl.pallas_call(functools.partial(lon_back_kernel, size, width), grid=(siz...  9.64 us
    ppermute x7, starting transfers between devices, crossed(): return lax.ppermute(value, axis, [(i, i ^ mask) for i in range(count)])  4.26 us
    unnamed x10, local copies, waits for them, and re-layouts  3.7 us
  transfers between devices with their start and end apart: 13, of which 3 were waited for; matrix products, arithmetic and copies ran while one was open for 0% of the time, Pallas kernels for 23%

profile of v4, /device:TPU:0, one launch (start us, length us, event | category | flops | bytes accessed | tf_op | source)
XLA Modules:
  0.0 93.7 jit_solution(3979268193867562039)
XLA Ops:
  0.7 0.6 stack.55.at_ref
  1.3 47.7 %spectral_gradients.1 = (f32[9216,256]{1,0:T(8,128)}, f32[2,2,104,128]{3,2,1,0:T(8,128)}) custom-call(s32[10]{0:T(128)} %stack.55.at_ref, f32[2025,8,96]{2,1,0:T(8,128)} %bitcast.35, f32[2025,8,96]{2,1,0:T(8,128)} %bitcast.36, bf16[192,576]{1,0:T(8,128)(2,1)} %constant.66.clone.tx_ref, bf16[192,576]{1,0:T(8,128)(2,1)} %constant.67.clone.tg_ref, ...), custom_call_target="tpu_custom_call" | custom-call | tf_op jit(solution)/shard_map/spectral_gradients/pallas_call | solution.py:376
  49.0 0.9 dynamic-slice_bitcast_fusion
  49.9 5.1 %collective-permute-start.2 = (f32[104,128]{1,0:T(8,128)S(1)}, f32[104,128]{1,0:T(8,128)S(1)}, u32[]{:S(2)}, u32[]{:S(2)}) collective-permute-start(f32[104,128]{1,0:T(8,128)S(1)} %get-tuple-element.47), channel_id=1, source_target_pairs={{0,24},{8,0},{16,8},{24,16},{1,25},{9,1},{17,9},{25,17},{2,26},{10... | collective-permute-start | bytes 159752 | tf_op jit(solution)/shard_map/ppermute | solution.py:462
  55.0 0.0 collective-permute-start.1
  55.0 1.0 %collective-permute-start = (f32[104,128]{1,0:T(8,128)S(1)}, f32[104,128]{1,0:T(8,128)S(1)}, u32[]{:S(2)}, u32[]{:S(2)}) collective-permute-start(f32[104,128]{1,0:T(8,128)S(1)} %get-tuple-element.49), channel_id=1, source_target_pairs={{0,8},{8,16},{16,24},{24,0},{1,9},{9,17},{17,25},{25,1},{2,10},{10... | collective-permute-start | bytes 159752 | tf_op jit(solution)/shard_map/ppermute | solution.py:462
  56.0 3.7 %copy-done = f32[9216,256]{1,0:T(8,128)S(1)} copy-done((f32[9216,256]{1,0:T(8,128)S(1)}, f32[9216,256]{1,0:T(8,128)}, u32[]{:S(2)}) %copy-start) | copy-done | bytes 9437208
  59.7 5.9 %lat_back.2.refs_0_ = f32[2,48,96,128]{3,2,1,0:T(8,128)S(1)} custom-call(s32[10]{0:T(128)S(1)} %copy-done.4, f32[9216,256]{1,0:T(8,128)S(1)} %copy-done, f32[2,8,96,96]{3,2,1,0:T(8,128)S(1)} %copy-done.1, bf16[192,192]{1,0:T(8,128)(2,1)S(1)} %copy-done.2), custom_call_target="tpu_custom_call" | custom-call | tf_op jit(solution)/shard_map/lat_back/pallas_call | solution.py:413
  65.6 0.0 copy-start.3
  65.6 0.0 collective-permute-done.1
  65.6 0.0 collective-permute-done
  65.6 0.9 fusion
  66.5 2.9 %collective-permute-start.5 = (f32[104,128]{1,0:T(8,128)S(1)}, f32[104,128]{1,0:T(8,128)S(1)}, u32[]{:S(2)}, u32[]{:S(2)}) collective-permute-start(f32[104,128]{1,0:T(8,128)S(1)} %fusion), channel_id=1, source_target_pairs={{0,24},{8,0},{16,8},{24,16},{1,25},{9,1},{17,9},{25,17},{2,26},{10... | collective-permute-start | bytes 159752 | tf_op jit(solution)/shard_map/ppermute | solution.py:462
  69.4 1.1 %collective-permute-start.4 = (f32[104,128]{1,0:T(8,128)S(1)}, f32[104,128]{1,0:T(8,128)S(1)}, u32[]{:S(2)}, u32[]{:S(2)}) collective-permute-start(f32[104,128]{1,0:T(8,128)S(1)} %fusion), channel_id=1, source_target_pairs={{0,16},{8,24},{16,0},{24,8},{1,17},{9,25},{17,1},{25,9},{2,18},{10... | collective-permute-start | bytes 159752 | tf_op jit(solution)/shard_map/ppermute | solution.py:462
  70.5 0.0 collective-permute-start.3
  70.5 5.9 %lat_back.3.refs_1_ = f32[2,48,96,128]{3,2,1,0:T(8,128)S(1)} custom-call(s32[10]{0:T(128)S(1)} %copy-done.4, f32[9216,256]{1,0:T(8,128)S(1)} %copy-done, f32[2,8,96,96]{3,2,1,0:T(8,128)S(1)} %copy-done.1, bf16[192,192]{1,0:T(8,128)(2,1)S(1)} %copy-done.2), custom_call_target="tpu_custom_call" | custom-call | tf_op jit(solution)/shard_map/lat_back/pallas_call | solution.py:413
  76.4 0.0 collective-permute-done.5
  76.4 0.0 collective-permute-done.4
  76.4 0.0 collective-permute-done.3
  76.5 0.1 collective-permute-start.9
  76.6 2.5 %collective-permute-start.8 = (f32[4,104,128]{2,1,0:T(8,128)S(1)}, f32[4,104,128]{2,1,0:T(8,128)S(1)}, u32[]{:S(2)}, u32[]{:S(2)}) collective-permute-start(f32[4,104,128]{2,1,0:T(8,128)S(1)} %pad_maximum_fusion.refs_0_), channel_id=1, source_target_pairs={{0,6},{1,7},{2,4},{3,5},{4,2},{5,3},{6,0},{7,1},{8,14},{9,15},{10,... | collective-permute-start | bytes 638984 | tf_op jit(solution)/shard_map/ppermute | solution.py:467
  79.1 0.5 collective-permute-start.7
  79.6 0.5 collective-permute-start.6
  80.1 9.6 %lon_back.1 = f32[2025,8,96]{2,1,0:T(8,128)} custom-call(f32[2,48,96,128]{3,2,1,0:T(8,128)S(1)} %lat_back.2.refs_0_, f32[2,48,96,128]{3,2,1,0:T(8,128)S(1)} %lat_back.3.refs_1_, bf16[192,576]{1,0:T(8,128)(2,1)S(1)} %copy-done.3), custom_call_target="tpu_custom_call" | custom-call | tf_op jit(solution)/shard_map/lon_back/pallas_call | solution.py:435
  89.8 0.0 collective-permute-done.6.refs_2_
  89.8 0.1 collective-permute-start.10
  89.9 0.5 collective-permute-start.11
  90.3 0.1 collective-permute-start.12
  90.4 0.9 collective-permute-done.10.refs_3_
  91.3 0.3 collective-permute-done.11.refs_5_
  91.6 0.3 collective-permute-done.12.refs_7_
  91.9 1.8 %assemble.1 = (f32[2,8,96,96]{3,2,1,0:T(8,128)}, f32[2,8,96,96]{3,2,1,0:T(8,128)}, f32[2,8,96]{2,1,0:T(8,128)}, f32[2,8,96]{2,1,0:T(8,128)}) custom-call(s32[10]{0:T(128)S(1)} %copy-done.4, f32[4,104,128]{2,1,0:T(8,128)S(1)} %pad_maximum_fusion.refs_0_, f32[4,104,128]{2,1,0:T(8,128)S(1)} %collective-permute-done.9.refs_1_, ...), custom_call_target="tpu_custom_call" | custom-call | tf_op jit(solution)/shard_map/assemble/pallas_call | solution.py:450
  (13 shorter events, 0.0 us)
Async XLA Ops:
  1.3 54.7 %copy-start.1 = (f32[2,8,96,96]{3,2,1,0:T(8,128)S(1)}, f32[2,8,96,96]{3,2,1,0:T(8,128)}, u32[]{:S(2)}) copy-start(f32[2,8,96,96]{3,2,1,0:T(8,128)} %wa_ref.5) | copy-start | bytes 1769476
  1.3 54.7 %copy-start.2 = (bf16[192,192]{1,0:T(8,128)(2,1)S(1)}, bf16[192,192]{1,0:T(8,128)(2,1)}, u32[]{:S(2)}) copy-start(bf16[192,192]{1,0:T(8,128)(2,1)} %constant.70.clone.f_ref) | copy-start | bytes 221188
  1.3 54.7 %copy-start.4 = (s32[10]{0:T(128)S(1)}, s32[10]{0:T(128)}, u32[]{:S(2)}) copy-start(s32[10]{0:T(128)} %stack.55.at_ref) | copy-start | bytes 124
  49.9 15.7 %collective-permute-start.2 = (f32[104,128]{1,0:T(8,128)S(1)}, f32[104,128]{1,0:T(8,128)S(1)}, u32[]{:S(2)}, u32[]{:S(2)}) collective-permute-start(f32[104,128]{1,0:T(8,128)S(1)} %get-tuple-element.47), channel_id=1, source_target_pairs={{0,24},{8,0},{16,8},{24,16},{1,25},{9,1},{17,9},{25,17},{2,26},{10... | collective-permute-start | bytes 159752 | tf_op jit(solution)/shard_map/ppermute | solution.py:462
  55.0 10.6 %collective-permute-start.1 = (f32[104,128]{1,0:T(8,128)S(1)}, f32[104,128]{1,0:T(8,128)S(1)}, u32[]{:S(2)}, u32[]{:S(2)}) collective-permute-start(f32[104,128]{1,0:T(8,128)S(1)} %get-tuple-element.48), channel_id=1, source_target_pairs={{0,16},{8,24},{16,0},{24,8},{1,17},{9,25},{17,1},{25,9},{2,18},{10... | collective-permute-start | bytes 159752 | tf_op jit(solution)/shard_map/ppermute | solution.py:462
  55.0 10.6 %collective-permute-start = (f32[104,128]{1,0:T(8,128)S(1)}, f32[104,128]{1,0:T(8,128)S(1)}, u32[]{:S(2)}, u32[]{:S(2)}) collective-permute-start(f32[104,128]{1,0:T(8,128)S(1)} %get-tuple-element.49), channel_id=1, source_target_pairs={{0,8},{8,16},{16,24},{24,0},{1,9},{9,17},{17,25},{25,1},{2,10},{10... | collective-permute-start | bytes 159752 | tf_op jit(solution)/shard_map/ppermute | solution.py:462
  56.0 3.7 %copy-start = (f32[9216,256]{1,0:T(8,128)S(1)}, f32[9216,256]{1,0:T(8,128)}, u32[]{:S(2)}) copy-start(f32[9216,256]{1,0:T(8,128)} %get-tuple-element.32.s_ref) | copy-start | bytes 28311556
  65.6 14.5 %copy-start.3 = (bf16[192,576]{1,0:T(8,128)(2,1)S(1)}, bf16[192,576]{1,0:T(8,128)(2,1)}, u32[]{:S(2)}) copy-start(bf16[192,576]{1,0:T(8,128)(2,1)} %constant.71.clone.refs_2_) | copy-start | bytes 663556
  66.5 9.9 %collective-permute-start.5 = (f32[104,128]{1,0:T(8,128)S(1)}, f32[104,128]{1,0:T(8,128)S(1)}, u32[]{:S(2)}, u32[]{:S(2)}) collective-permute-start(f32[104,128]{1,0:T(8,128)S(1)} %fusion), channel_id=1, source_target_pairs={{0,24},{8,0},{16,8},{24,16},{1,25},{9,1},{17,9},{25,17},{2,26},{10... | collective-permute-start | bytes 159752 | tf_op jit(solution)/shard_map/ppermute | solution.py:462
  69.4 7.0 %collective-permute-start.4 = (f32[104,128]{1,0:T(8,128)S(1)}, f32[104,128]{1,0:T(8,128)S(1)}, u32[]{:S(2)}, u32[]{:S(2)}) collective-permute-start(f32[104,128]{1,0:T(8,128)S(1)} %fusion), channel_id=1, source_target_pairs={{0,16},{8,24},{16,0},{24,8},{1,17},{9,25},{17,1},{25,9},{2,18},{10... | collective-permute-start | bytes 159752 | tf_op jit(solution)/shard_map/ppermute | solution.py:462
  70.5 5.9 %collective-permute-start.3 = (f32[104,128]{1,0:T(8,128)S(1)}, f32[104,128]{1,0:T(8,128)S(1)}, u32[]{:S(2)}, u32[]{:S(2)}) collective-permute-start(f32[104,128]{1,0:T(8,128)S(1)} %fusion), channel_id=1, source_target_pairs={{0,8},{8,16},{16,24},{24,0},{1,9},{9,17},{17,25},{25,1},{2,10},{10... | collective-permute-start | bytes 159752 | tf_op jit(solution)/shard_map/ppermute | solution.py:462
  76.5 13.3 %collective-permute-start.9 = (f32[4,104,128]{2,1,0:T(8,128)S(1)}, f32[4,104,128]{2,1,0:T(8,128)S(1)}, u32[]{:S(2)}, u32[]{:S(2)}) collective-permute-start(f32[4,104,128]{2,1,0:T(8,128)S(1)} %pad_maximum_fusion.refs_0_), channel_id=1, source_target_pairs={{0,1},{1,0},{2,3},{3,2},{4,5},{5,4},{6,7},{7,6},{8,9},{9,8},{10,11... | collective-permute-start | bytes 638984 | tf_op jit(solution)/shard_map/ppermute | solution.py:467
  76.6 13.2 %collective-permute-start.8 = (f32[4,104,128]{2,1,0:T(8,128)S(1)}, f32[4,104,128]{2,1,0:T(8,128)S(1)}, u32[]{:S(2)}, u32[]{:S(2)}) collective-permute-start(f32[4,104,128]{2,1,0:T(8,128)S(1)} %pad_maximum_fusion.refs_0_), channel_id=1, source_target_pairs={{0,6},{1,7},{2,4},{3,5},{4,2},{5,3},{6,0},{7,1},{8,14},{9,15},{10,... | collective-permute-start | bytes 638984 | tf_op jit(solution)/shard_map/ppermute | solution.py:467
  79.1 10.7 %collective-permute-start.7 = (f32[4,104,128]{2,1,0:T(8,128)S(1)}, f32[4,104,128]{2,1,0:T(8,128)S(1)}, u32[]{:S(2)}, u32[]{:S(2)}) collective-permute-start(f32[4,104,128]{2,1,0:T(8,128)S(1)} %pad_maximum_fusion.refs_0_), channel_id=1, source_target_pairs={{0,4},{1,5},{2,6},{3,7},{4,0},{5,1},{6,2},{7,3},{8,12},{9,13},{10,... | collective-permute-start | bytes 638984 | tf_op jit(solution)/shard_map/ppermute | solution.py:467
  79.6 10.2 %collective-permute-start.6 = (f32[4,104,128]{2,1,0:T(8,128)S(1)}, f32[4,104,128]{2,1,0:T(8,128)S(1)}, u32[]{:S(2)}, u32[]{:S(2)}) collective-permute-start(f32[4,104,128]{2,1,0:T(8,128)S(1)} %pad_maximum_fusion.refs_0_), channel_id=1, source_target_pairs={{0,2},{1,3},{2,0},{3,1},{4,6},{5,7},{6,4},{7,5},{8,10},{9,11},{10,... | collective-permute-start | bytes 638984 | tf_op jit(solution)/shard_map/ppermute | solution.py:467
  89.8 1.5 %collective-permute-start.10 = (f32[4,104,128]{2,1,0:T(8,128)S(1)}, f32[4,104,128]{2,1,0:T(8,128)S(1)}, u32[]{:S(2)}, u32[]{:S(2)}) collective-permute-start(f32[4,104,128]{2,1,0:T(8,128)S(1)} %collective-permute-done.6.refs_2_), channel_id=1, source_target_pairs={{0,1},{1,0},{2,3},{3,2},{4,5},{5,4},{6,7},{7,6},{8,9},{9,8},{10,11... | collective-permute-start | bytes 638984 | tf_op jit(solution)/shard_map/ppermute | solution.py:467
  89.9 1.8 %collective-permute-start.11 = (f32[4,104,128]{2,1,0:T(8,128)S(1)}, f32[4,104,128]{2,1,0:T(8,128)S(1)}, u32[]{:S(2)}, u32[]{:S(2)}) collective-permute-start(f32[4,104,128]{2,1,0:T(8,128)S(1)} %collective-permute-done.7.refs_4_), channel_id=1, source_target_pairs={{0,1},{1,0},{2,3},{3,2},{4,5},{5,4},{6,7},{7,6},{8,9},{9,8},{10,11... | collective-permute-start | bytes 638984 | tf_op jit(solution)/shard_map/ppermute | solution.py:467
  90.3 1.6 %collective-permute-start.12 = (f32[4,104,128]{2,1,0:T(8,128)S(1)}, f32[4,104,128]{2,1,0:T(8,128)S(1)}, u32[]{:S(2)}, u32[]{:S(2)}) collective-permute-start(f32[4,104,128]{2,1,0:T(8,128)S(1)} %collective-permute-done.8.refs_6_), channel_id=1, source_target_pairs={{0,1},{1,0},{2,3},{3,2},{4,5},{5,4},{6,7},{7,6},{8,9},{9,8},{10,11... | collective-permute-start | bytes 638984 | tf_op jit(solution)/shard_map/ppermute | solution.py:467

commit v5 on v4

--- a/solution.py
+++ b/solution.py
@@ -19,10 +19,11 @@
 F32 = jnp.float32
 BF16 = jnp.bfloat16
 CHUNK = 4
-BAND_MOST = 10
+LATS = 16
+BAND_MOST = 18
 PARTS = 2
 GRADIENT_VMEM = 54 << 20
-LAT_VMEM = 24 << 20
+LAT_VMEM = 46 << 20
 LON_VMEM = 24 << 20
 
 
@@ -121,9 +122,10 @@
     return dot(jnp.concatenate([high, low, high], axis=1), weight_ref[which])
 
 
-def fill_matrix(out, width, real, imag, turned):
+def fill_matrix(out, width, real, imag, turned, scale=1.0):
     if turned:
         real, imag = real.T, imag.T
+    real, imag = real * scale, imag * scale
     sign = -1.0 if turned else 1.0
     span = 2 * LANES
     for row, column, value in ((0, 0, real), (1, 1, real), (0, 1, sign * imag), (1, 0, -sign * imag)):
@@ -152,11 +154,11 @@
         w_ref[...] = jnp.zeros_like(w_ref)
         b_ref[...] = jnp.zeros_like(b_ref)
         fill_matrix(w_ref.at[0], width, wa_ref[0, 0], wa_ref[1, 0], False)
-        fill_matrix(w_ref.at[1], width, wb_ref[0, 0], wb_ref[1, 0], False)
+        fill_matrix(w_ref.at[1], width, wb_ref[0, 0], wb_ref[1, 0], False, 1.0 / SHRINK)
         fill_matrix(w_ref.at[2], width, wb_ref[0, 0], wb_ref[1, 0], True)
-        for layer, bias in enumerate((ba_ref, bb_ref)):
+        for layer, (bias, scale) in enumerate(((ba_ref, 1.0), (bb_ref, 1.0 / SHRINK))):
             for q in range(2):
-                row = bias[q, pl.ds(at_ref[1], 1), :]
+                row = bias[q, pl.ds(at_ref[1], 1), :] * scale
                 b_ref[layer, :, q * LANES : q * LANES + width] = jnp.broadcast_to(row, (SUB, width))
         for which in range(2):
             spectra[which, size.rows * stride :] = jnp.zeros(((size.row_slots - size.rows) * stride, LANES), F32)
@@ -220,16 +222,17 @@
                 a = plain[1, here] + b_ref[0, :1]
                 square = a * a
                 tangent = jnp.tanh(a * (GELU_SCALE + (GELU_SCALE * GELU_CUBE) * square))
-                part = 0.5 * a
-                plain[1, here] = 0.5 + 0.5 * tangent + part * (1.0 - tangent * tangent) * (
-                    GELU_SCALE + (3.0 * GELU_SCALE * GELU_CUBE) * square
+                share = 0.5 * tangent + 0.5
+                o = a * share
+                plain[1, here] = share + (o - o * share) * (
+                    2.0 * GELU_SCALE + (6.0 * GELU_SCALE * GELU_CUBE) * square
                 )
-                keep_split(1, here, part + part * tangent)
+                keep_split(1, here, o)
 
         def gate(chunk):
             sums = jnp.zeros((SUB, 2 * LANES), F32)
             for here in pieces(chunk):
-                tangent = jnp.tanh((plain[2, here] + b_ref[1, :1]) * (1.0 / SHRINK))
+                tangent = jnp.tanh(plain[2, here] + b_ref[1, :1])
                 e = plain[0, here] * (tangent * tangent)
                 for i in range(0, piece, SUB):
                     sums = sums + e[i : i + SUB]
@@ -326,14 +329,14 @@
     v_refs, (t_ref, out_ref) = refs[:PARTS], refs[PARTS:]
     cols = size.cols
     lines = size.slots // PARTS
-    flat = out_ref.reshape(SUB * cols, width)
-    rows = [ref.reshape(2 * lines * SUB, LANES) for ref in v_refs]
-    for pair in range(SUB // 2):
+    flat = out_ref.reshape(LATS * cols, width)
+    rows = [ref.reshape(2 * lines * LATS, LANES) for ref in v_refs]
+    for pair in range(LATS // 2):
         data = side_by_side(
             *(
                 jnp.concatenate(
                     [
-                        part[pl.ds(q * lines * SUB + 2 * pair + i, lines, stride=SUB), :]
+                        part[pl.ds(q * lines * LATS + 2 * pair + i, lines, stride=LATS), :]
                         for q in range(2)
                         for part in rows
                     ],
@@ -431,12 +434,12 @@
 
 def lon_back(size, width, v_parts):
     table = jnp.asarray(three_way(lon_table(size, False).T))
-    field = pl.BlockSpec((2, size.slots // PARTS, SUB, LANES), lambda i: (0, 0, i, 0))
+    field = pl.BlockSpec((2, size.slots // PARTS, LATS, LANES), lambda i: (0, 0, i, 0))
     return pl.pallas_call(
         functools.partial(lon_back_kernel, size, width),
-        grid=(size.row_slots // SUB,),
+        grid=(size.row_slots // LATS,),
         in_specs=[field] * PARTS + [whole_spec(table)],
-        out_specs=pl.BlockSpec((size.cols, SUB, width), lambda i: (i, 0, 0)),
+        out_specs=pl.BlockSpec((size.cols * LATS // SUB, SUB, width), lambda i: (i, 0, 0)),
         out_shape=jax.ShapeDtypeStruct((size.rows * size.cols // SUB, SUB, width), F32),
         compiler_params=pltpu.CompilerParams(vmem_limit_bytes=LON_VMEM),
         name="lon_back",

time: 94.2 us -> 91.7 us (0.973)
  local copies, waits for them, and re-layouts: 5.19 us -> 1.58 us
  waiting for transfers between devices: 1.56 us -> 2.95 us
    unnamed x10 -> x8, local copies, waits for them, and re-layouts: 3.7 us -> 0.02 us
    pallas_call x2, Pallas kernels: 11.8 us -> 15.1 us  [lat_back(): pl.pallas_call(functools.partial(lat_back_kernel, size, width), grid_spec...]
    pallas_call x1, Pallas kernels: 47.7 us -> 45.5 us  [spectral_gradients(): pl.pallas_call(functools.partial(gradient_kernel, size, width, bands, bat...]
    ppermute x7, waiting for transfers between devices: 1.51 us -> 2.93 us  [crossed(): return lax.ppermute(value, axis, [(i, i ^ mask) for i in range(count)])]
    pallas_call x1, Pallas kernels: 9.64 us -> 8.31 us  [lon_back(): pl.pallas_call(functools.partial(lon_back_kernel, size, width), grid=(siz...]
  transfers between devices with their start and end apart: 13 -> 13, of which waited for: 3 -> 5; matrix products, arithmetic and copies ran while one was open for 0% -> 0% of each run, Pallas kernels for 23% -> 26%
where the time goes in v5:
time: 91.7 us; the launch traced here: 91.3 us
  Pallas kernels  70.8 us (77%)
  starting transfers between devices  14.3 us (16%)
  waiting for transfers between devices  2.95 us (3%)
  local copies, waits for them, and re-layouts  1.58 us (2%)
  other arithmetic  0.92 us (1%)
    pallas_call x1, Pallas kernels, spectral_gradients(): pl.pallas_call(functools.partial(gradient_kernel, size, width, bands, bat...  45.5 us
    pallas_call x2, Pallas kernels, lat_back(): pl.pallas_call(functools.partial(lat_back_kernel, size, width), grid_spec...  15.1 us
    ppermute x6, starting transfers between devices, shifted(): lax.ppermute(value, axis, [(i, (i + shift) % count) for i in range(count)])  10.1 us
    pallas_call x1, Pallas kernels, lon_back(): pl.pallas_call(functools.partial(lon_back_kernel, size, width), grid=(siz...  8.31 us
    ppermute x7, starting transfers between devices, crossed(): return lax.ppermute(value, axis, [(i, i ^ mask) for i in range(count)])  4.14 us
    ppermute x7, waiting for transfers between devices, crossed(): return lax.ppermute(value, axis, [(i, i ^ mask) for i in range(count)])  2.93 us
  transfers between devices with their start and end apart: 13, of which 5 were waited for; matrix products, arithmetic and copies ran while one was open for 0% of the time, Pallas kernels for 26%

profile of v5, /device:TPU:0, one launch (start us, length us, event | category | flops | bytes accessed | tf_op | source)
XLA Modules:
  0.0 91.3 jit_solution(11441505603455575529)
XLA Ops:
  0.7 0.7 stack.55.at_ref
  1.4 45.5 %spectral_gradients.1 = (f32[9216,256]{1,0:T(8,128)}, f32[2,2,104,128]{3,2,1,0:T(8,128)}) custom-call(s32[10]{0:T(128)} %stack.55.at_ref, f32[2025,8,96]{2,1,0:T(8,128)} %bitcast.35, f32[2025,8,96]{2,1,0:T(8,128)} %bitcast.36, bf16[192,576]{1,0:T(8,128)(2,1)} %constant.66.clone.tx_ref, bf16[192,576]{1,0:T(8,128)(2,1)} %constant.67.clone.tg_ref, ...), custom_call_target="tpu_custom_call" | custom-call | tf_op jit(solution)/shard_map/spectral_gradients/pallas_call | solution.py:379
  46.9 0.9 dynamic-slice_bitcast_fusion
  47.8 5.1 %collective-permute-start.2 = (f32[104,128]{1,0:T(8,128)S(1)}, f32[104,128]{1,0:T(8,128)S(1)}, u32[]{:S(2)}, u32[]{:S(2)}) collective-permute-start(f32[104,128]{1,0:T(8,128)S(1)} %get-tuple-element.47), channel_id=1, source_target_pairs={{0,24},{8,0},{16,8},{24,16},{1,25},{9,1},{17,9},{25,17},{2,26},{10... | collective-permute-start | bytes 159752 | tf_op jit(solution)/shard_map/ppermute | solution.py:465
  52.9 0.0 collective-permute-start.1
  52.9 1.0 %collective-permute-start = (f32[104,128]{1,0:T(8,128)S(1)}, f32[104,128]{1,0:T(8,128)S(1)}, u32[]{:S(2)}, u32[]{:S(2)}) collective-permute-start(f32[104,128]{1,0:T(8,128)S(1)} %get-tuple-element.49), channel_id=1, source_target_pairs={{0,8},{8,16},{16,24},{24,0},{1,9},{9,17},{17,25},{25,1},{2,10},{10... | collective-permute-start | bytes 159752 | tf_op jit(solution)/shard_map/ppermute | solution.py:465
  53.9 7.6 %lat_back.2.refs_0_ = f32[2,48,96,128]{3,2,1,0:T(8,128)S(1)} custom-call(s32[10]{0:T(128)S(1)} %copy-done.3, f32[9216,256]{1,0:T(8,128)} %get-tuple-element.32.s_ref, f32[2,8,96,96]{3,2,1,0:T(8,128)S(1)} %copy-done, bf16[192,192]{1,0:T(8,128)(2,1)S(1)} %copy-done.1), custom_call_target="tpu_custom_call" | custom-call | tf_op jit(solution)/shard_map/lat_back/pallas_call | solution.py:416
  61.5 0.0 copy-start.2
  61.5 0.0 collective-permute-done.2
  61.5 0.0 collective-permute-done
  61.5 0.9 fusion
  62.4 2.9 %collective-permute-start.5 = (f32[104,128]{1,0:T(8,128)S(1)}, f32[104,128]{1,0:T(8,128)S(1)}, u32[]{:S(2)}, u32[]{:S(2)}) collective-permute-start(f32[104,128]{1,0:T(8,128)S(1)} %fusion), channel_id=1, source_target_pairs={{0,24},{8,0},{16,8},{24,16},{1,25},{9,1},{17,9},{25,17},{2,26},{10... | collective-permute-start | bytes 159752 | tf_op jit(solution)/shard_map/ppermute | solution.py:465
  65.3 1.1 %collective-permute-start.4 = (f32[104,128]{1,0:T(8,128)S(1)}, f32[104,128]{1,0:T(8,128)S(1)}, u32[]{:S(2)}, u32[]{:S(2)}) collective-permute-start(f32[104,128]{1,0:T(8,128)S(1)} %fusion), channel_id=1, source_target_pairs={{0,16},{8,24},{16,0},{24,8},{1,17},{9,25},{17,1},{25,9},{2,18},{10... | collective-permute-start | bytes 159752 | tf_op jit(solution)/shard_map/ppermute | solution.py:465
  66.4 0.0 collective-permute-start.3
  66.4 7.6 %lat_back.3.refs_1_ = f32[2,48,96,128]{3,2,1,0:T(8,128)S(1)} custom-call(s32[10]{0:T(128)S(1)} %copy-done.3, f32[9216,256]{1,0:T(8,128)} %get-tuple-element.32.s_ref, f32[2,8,96,96]{3,2,1,0:T(8,128)S(1)} %copy-done, bf16[192,192]{1,0:T(8,128)(2,1)S(1)} %copy-done.1), custom_call_target="tpu_custom_call" | custom-call | tf_op jit(solution)/shard_map/lat_back/pallas_call | solution.py:416
  74.0 0.0 collective-permute-done.5
  74.0 0.0 collective-permute-done.3
  74.1 0.1 collective-permute-start.9
  74.1 2.5 %collective-permute-start.8 = (f32[4,104,128]{2,1,0:T(8,128)S(1)}, f32[4,104,128]{2,1,0:T(8,128)S(1)}, u32[]{:S(2)}, u32[]{:S(2)}) collective-permute-start(f32[4,104,128]{2,1,0:T(8,128)S(1)} %pad_maximum_fusion.refs_0_), channel_id=1, source_target_pairs={{0,6},{1,7},{2,4},{3,5},{4,2},{5,3},{6,0},{7,1},{8,14},{9,15},{10,... | collective-permute-start | bytes 638984 | tf_op jit(solution)/shard_map/ppermute | solution.py:470
  76.7 0.5 collective-permute-start.7
  77.2 0.5 collective-permute-start.6
  77.7 8.3 %lon_back.1 = f32[2025,8,96]{2,1,0:T(8,128)} custom-call(f32[2,48,96,128]{3,2,1,0:T(8,128)S(1)} %lat_back.2.refs_0_, f32[2,48,96,128]{3,2,1,0:T(8,128)S(1)} %lat_back.3.refs_1_, bf16[192,576]{1,0:T(8,128)(2,1)S(1)} %copy-done.2), custom_call_target="tpu_custom_call" | custom-call | tf_op jit(solution)/shard_map/lon_back/pallas_call | solution.py:438
  86.0 0.0 collective-permute-done.9.refs_1_
  86.0 0.0 collective-permute-done.8.refs_6_
  86.0 1.3 %collective-permute-done.7.refs_4_ = f32[4,104,128]{2,1,0:T(8,128)S(1)} collective-permute-done((f32[4,104,128]{2,1,0:T(8,128)S(1)}, f32[4,104,128]{2,1,0:T(8,128)S(1)}, u32[]{:S(2)}, u32[]{:S(2)}) %collective-permute-start.7) | collective-permute-done | bytes 213024 | tf_op jit(solution)/shard_map/ppermute | solution.py:470
  87.3 0.1 collective-permute-done.6.refs_2_
  87.4 0.5 collective-permute-start.11
  87.9 0.0 collective-permute-start.12
  87.9 1.0 %collective-permute-done.10.refs_3_ = f32[4,104,128]{2,1,0:T(8,128)S(1)} collective-permute-done((f32[4,104,128]{2,1,0:T(8,128)S(1)}, f32[4,104,128]{2,1,0:T(8,128)S(1)}, u32[]{:S(2)}, u32[]{:S(2)}) %collective-permute-start.10) | collective-permute-done | bytes 213024 | tf_op jit(solution)/shard_map/ppermute | solution.py:470
  88.8 0.3 collective-permute-done.11.refs_5_
  89.2 0.3 collective-permute-done.12.refs_7_
  89.5 1.8 %assemble.1 = (f32[2,8,96,96]{3,2,1,0:T(8,128)}, f32[2,8,96,96]{3,2,1,0:T(8,128)}, f32[2,8,96]{2,1,0:T(8,128)}, f32[2,8,96]{2,1,0:T(8,128)}) custom-call(s32[10]{0:T(128)S(1)} %copy-done.3, f32[4,104,128]{2,1,0:T(8,128)S(1)} %pad_maximum_fusion.refs_0_, f32[4,104,128]{2,1,0:T(8,128)S(1)} %collective-permute-done.9.refs_1_, ...), custom_call_target="tpu_custom_call" | custom-call | tf_op jit(solution)/shard_map/assemble/pallas_call | solution.py:453
  (11 shorter events, 0.0 us)
Async XLA Ops:
  1.4 52.5 %copy-start = (f32[2,8,96,96]{3,2,1,0:T(8,128)S(1)}, f32[2,8,96,96]{3,2,1,0:T(8,128)}, u32[]{:S(2)}) copy-start(f32[2,8,96,96]{3,2,1,0:T(8,128)} %wa_ref.5) | copy-start | bytes 1769476
  1.4 52.5 %copy-start.1 = (bf16[192,192]{1,0:T(8,128)(2,1)S(1)}, bf16[192,192]{1,0:T(8,128)(2,1)}, u32[]{:S(2)}) copy-start(bf16[192,192]{1,0:T(8,128)(2,1)} %constant.70.clone.f_ref) | copy-start | bytes 221188
  1.4 52.5 %copy-start.3 = (s32[10]{0:T(128)S(1)}, s32[10]{0:T(128)}, u32[]{:S(2)}) copy-start(s32[10]{0:T(128)} %stack.55.at_ref) | copy-start | bytes 124
  47.8 13.7 %collective-permute-start.2 = (f32[104,128]{1,0:T(8,128)S(1)}, f32[104,128]{1,0:T(8,128)S(1)}, u32[]{:S(2)}, u32[]{:S(2)}) collective-permute-start(f32[104,128]{1,0:T(8,128)S(1)} %get-tuple-element.47), channel_id=1, source_target_pairs={{0,24},{8,0},{16,8},{24,16},{1,25},{9,1},{17,9},{25,17},{2,26},{10... | collective-permute-start | bytes 159752 | tf_op jit(solution)/shard_map/ppermute | solution.py:465
  52.9 8.6 %collective-permute-start.1 = (f32[104,128]{1,0:T(8,128)S(1)}, f32[104,128]{1,0:T(8,128)S(1)}, u32[]{:S(2)}, u32[]{:S(2)}) collective-permute-start(f32[104,128]{1,0:T(8,128)S(1)} %get-tuple-element.48), channel_id=1, source_target_pairs={{0,16},{8,24},{16,0},{24,8},{1,17},{9,25},{17,1},{25,9},{2,18},{10... | collective-permute-start | bytes 159752 | tf_op jit(solution)/shard_map/ppermute | solution.py:465
  52.9 8.6 %collective-permute-start = (f32[104,128]{1,0:T(8,128)S(1)}, f32[104,128]{1,0:T(8,128)S(1)}, u32[]{:S(2)}, u32[]{:S(2)}) collective-permute-start(f32[104,128]{1,0:T(8,128)S(1)} %get-tuple-element.49), channel_id=1, source_target_pairs={{0,8},{8,16},{16,24},{24,0},{1,9},{9,17},{17,25},{25,1},{2,10},{10... | collective-permute-start | bytes 159752 | tf_op jit(solution)/shard_map/ppermute | solution.py:465
  61.5 16.2 %copy-start.2 = (bf16[192,576]{1,0:T(8,128)(2,1)S(1)}, bf16[192,576]{1,0:T(8,128)(2,1)}, u32[]{:S(2)}) copy-start(bf16[192,576]{1,0:T(8,128)(2,1)} %constant.71.clone.refs_2_) | copy-start | bytes 663556
  62.4 11.6 %collective-permute-start.5 = (f32[104,128]{1,0:T(8,128)S(1)}, f32[104,128]{1,0:T(8,128)S(1)}, u32[]{:S(2)}, u32[]{:S(2)}) collective-permute-start(f32[104,128]{1,0:T(8,128)S(1)} %fusion), channel_id=1, source_target_pairs={{0,24},{8,0},{16,8},{24,16},{1,25},{9,1},{17,9},{25,17},{2,26},{10... | collective-permute-start | bytes 159752 | tf_op jit(solution)/shard_map/ppermute | solution.py:465
  65.3 8.7 %collective-permute-start.4 = (f32[104,128]{1,0:T(8,128)S(1)}, f32[104,128]{1,0:T(8,128)S(1)}, u32[]{:S(2)}, u32[]{:S(2)}) collective-permute-start(f32[104,128]{1,0:T(8,128)S(1)} %fusion), channel_id=1, source_target_pairs={{0,16},{8,24},{16,0},{24,8},{1,17},{9,25},{17,1},{25,9},{2,18},{10... | collective-permute-start | bytes 159752 | tf_op jit(solution)/shard_map/ppermute | solution.py:465
  66.4 7.6 %collective-permute-start.3 = (f32[104,128]{1,0:T(8,128)S(1)}, f32[104,128]{1,0:T(8,128)S(1)}, u32[]{:S(2)}, u32[]{:S(2)}) collective-permute-start(f32[104,128]{1,0:T(8,128)S(1)} %fusion), channel_id=1, source_target_pairs={{0,8},{8,16},{16,24},{24,0},{1,9},{9,17},{17,25},{25,1},{2,10},{10... | collective-permute-start | bytes 159752 | tf_op jit(solution)/shard_map/ppermute | solution.py:465
  74.1 11.9 %collective-permute-start.9 = (f32[4,104,128]{2,1,0:T(8,128)S(1)}, f32[4,104,128]{2,1,0:T(8,128)S(1)}, u32[]{:S(2)}, u32[]{:S(2)}) collective-permute-start(f32[4,104,128]{2,1,0:T(8,128)S(1)} %pad_maximum_fusion.refs_0_), channel_id=1, source_target_pairs={{0,1},{1,0},{2,3},{3,2},{4,5},{5,4},{6,7},{7,6},{8,9},{9,8},{10,11... | collective-permute-start | bytes 638984 | tf_op jit(solution)/shard_map/ppermute | solution.py:470
  74.1 11.9 %collective-permute-start.8 = (f32[4,104,128]{2,1,0:T(8,128)S(1)}, f32[4,104,128]{2,1,0:T(8,128)S(1)}, u32[]{:S(2)}, u32[]{:S(2)}) collective-permute-start(f32[4,104,128]{2,1,0:T(8,128)S(1)} %pad_maximum_fusion.refs_0_), channel_id=1, source_target_pairs={{0,6},{1,7},{2,4},{3,5},{4,2},{5,3},{6,0},{7,1},{8,14},{9,15},{10,... | collective-permute-start | bytes 638984 | tf_op jit(solution)/shard_map/ppermute | solution.py:470
  76.7 10.6 %collective-permute-start.7 = (f32[4,104,128]{2,1,0:T(8,128)S(1)}, f32[4,104,128]{2,1,0:T(8,128)S(1)}, u32[]{:S(2)}, u32[]{:S(2)}) collective-permute-start(f32[4,104,128]{2,1,0:T(8,128)S(1)} %pad_maximum_fusion.refs_0_), channel_id=1, source_target_pairs={{0,4},{1,5},{2,6},{3,7},{4,0},{5,1},{6,2},{7,3},{8,12},{9,13},{10,... | collective-permute-start | bytes 638984 | tf_op jit(solution)/shard_map/ppermute | solution.py:470
  77.2 10.2 %collective-permute-start.6 = (f32[4,104,128]{2,1,0:T(8,128)S(1)}, f32[4,104,128]{2,1,0:T(8,128)S(1)}, u32[]{:S(2)}, u32[]{:S(2)}) collective-permute-start(f32[4,104,128]{2,1,0:T(8,128)S(1)} %pad_maximum_fusion.refs_0_), channel_id=1, source_target_pairs={{0,2},{1,3},{2,0},{3,1},{4,6},{5,7},{6,4},{7,5},{8,10},{9,11},{10,... | collective-permute-start | bytes 638984 | tf_op jit(solution)/shard_map/ppermute | solution.py:470
  87.4 1.5 %collective-permute-start.10 = (f32[4,104,128]{2,1,0:T(8,128)S(1)}, f32[4,104,128]{2,1,0:T(8,128)S(1)}, u32[]{:S(2)}, u32[]{:S(2)}) collective-permute-start(f32[4,104,128]{2,1,0:T(8,128)S(1)} %collective-permute-done.6.refs_2_), channel_id=1, source_target_pairs={{0,1},{1,0},{2,3},{3,2},{4,5},{5,4},{6,7},{7,6},{8,9},{9,8},{10,11... | collective-permute-start | bytes 638984 | tf_op jit(solution)/shard_map/ppermute | solution.py:470
  87.4 1.8 %collective-permute-start.11 = (f32[4,104,128]{2,1,0:T(8,128)S(1)}, f32[4,104,128]{2,1,0:T(8,128)S(1)}, u32[]{:S(2)}, u32[]{:S(2)}) collective-permute-start(f32[4,104,128]{2,1,0:T(8,128)S(1)} %collective-permute-done.7.refs_4_), channel_id=1, source_target_pairs={{0,1},{1,0},{2,3},{3,2},{4,5},{5,4},{6,7},{7,6},{8,9},{9,8},{10,11... | collective-permute-start | bytes 638984 | tf_op jit(solution)/shard_map/ppermute | solution.py:470
  87.9 1.6 %collective-permute-start.12 = (f32[4,104,128]{2,1,0:T(8,128)S(1)}, f32[4,104,128]{2,1,0:T(8,128)S(1)}, u32[]{:S(2)}, u32[]{:S(2)}) collective-permute-start(f32[4,104,128]{2,1,0:T(8,128)S(1)} %collective-permute-done.8.refs_6_), channel_id=1, source_target_pairs={{0,1},{1,0},{2,3},{3,2},{4,5},{5,4},{6,7},{7,6},{8,9},{9,8},{10,11... | collective-permute-start | bytes 638984 | tf_op jit(solution)/shard_map/ppermute | solution.py:470

commit v6 on v5

--- a/solution.py
+++ b/solution.py
@@ -354,11 +354,10 @@
 def assemble_kernel(width, count, at_ref, *refs):
     parts, (wa_ref, wb_ref, ba_ref, bb_ref) = refs[:count], refs[count:]
     for l, (weight, bias) in enumerate(((wa_ref, ba_ref), (wa_ref, ba_ref), (wb_ref, bb_ref), (wb_ref, bb_ref))):
-        shift = lax.rem(at_ref[0] + 4 - l, 4)
         for x in range(count):
             block = at_ref[2 + x]
-            weight[l % 2, block] = parts[x][shift, :width, :width]
-            bias[l % 2, pl.ds(block, 1), :] = parts[x][shift, width : width + 1, :width]
+            weight[l % 2, block] = parts[x][l, :width, :width]
+            bias[l % 2, pl.ds(block, 1), :] = parts[x][l, width : width + 1, :width]
 
 
 def whole_spec(array):
@@ -460,11 +459,6 @@
     )(place, *parts)
 
 
-def shifted(value, axis, shift):
-    count = lax.axis_size(axis)
-    return lax.ppermute(value, axis, [(i, (i + shift) % count) for i in range(count)])
-
-
 def crossed(value, axis, mask):
     count = lax.axis_size(axis)
     return lax.ppermute(value, axis, [(i, i ^ mask) for i in range(count)])
@@ -482,18 +476,14 @@
         size, place, fields, first_weight, first_bias, second_weight, second_bias
     )
     matrices = partial.reshape(4, width + SUB, LANES)
-
-    def matrix(shift):
-        return lax.dynamic_index_in_dim(matrices, (at_lat + shift) % 4, 0, keepdims=False)
-
-    far = [shifted(matrix(shift), "lat", shift) for shift in (1, 2, 3)]
+    far = crossed(matrices, "lat", 1)
     v_first = lat_back(size, place, s_modes, first_weight, 0)
     far, v_first, s_modes = lax.optimization_barrier((far, v_first, s_modes))
-    mine = (matrix(0) + far[1]) + (far[0] + far[2])
-    others = [shifted(mine, "lat", shift) for shift in (1, 2, 3)]
+    pair = matrices + far
+    far = crossed(pair, "lat", 2)
     v_second = lat_back(size, place, s_modes, first_weight, 1)
-    others, v_first, v_second = lax.optimization_barrier((others, v_first, v_second))
-    own = jnp.stack([mine] + others)
+    far, v_first, v_second = lax.optimization_barrier((far, v_first, v_second))
+    own = pair + far
     chips = [crossed(own, "lon", mask) for mask in (2, 4, 6)]
     near = crossed(own, "lon", 1)
     out = lon_back(size, width, [v_first, v_second])

time: 91.7 us -> 87.3 us (0.952)
  starting transfers between devices: 14.3 us -> 9.89 us
  waiting for transfers between devices: 2.95 us -> 4.81 us
    ppermute x6 -> x0, starting transfers between devices: 10.1 us -> none  [shifted(): lax.ppermute(value, axis, [(i, (i + shift) % count) for i in range(count)])]
    ppermute x7 -> x9, starting transfers between devices: 4.14 us -> 9.89 us  [crossed(): return lax.ppermute(value, axis, [(i, i ^ mask) for i in range(count)])]
    ppermute x7 -> x9, waiting for transfers between devices: 2.93 us -> 4.81 us  [crossed(): return lax.ppermute(value, axis, [(i, i ^ mask) for i in range(count)])]
  transfers between devices with their start and end apart: 13 -> 9, of which waited for: 5 -> 6; matrix products, arithmetic and copies ran while one was open for 0% -> 0% of each run, Pallas kernels for 26% -> 27%
where the time goes in v6:
time: 87.3 us; the launch traced here: 86.9 us
  Pallas kernels  70.8 us (81%)
  starting transfers between devices  9.89 us (11%)
  waiting for transfers between devices  4.81 us (6%)
    pallas_call x1, Pallas kernels, spectral_gradients(): pl.pallas_call(functools.partial(gradient_kernel, size, width, bands, bat...  45.5 us
    pallas_call x2, Pallas kernels, lat_back(): pl.pallas_call(functools.partial(lat_back_kernel, size, width), grid_spec...  15.1 us
    ppermute x9, starting transfers between devices, crossed(): return lax.ppermute(value, axis, [(i, i ^ mask) for i in range(count)])  9.89 us
    pallas_call x1, Pallas kernels, lon_back(): pl.pallas_call(functools.partial(lon_back_kernel, size, width), grid=(siz...  8.31 us
    ppermute x9, waiting for transfers between devices, crossed(): return lax.ppermute(value, axis, [(i, i ^ mask) for i in range(count)])  4.81 us
    pallas_call x1, Pallas kernels, assemble(): pl.pallas_call(functools.partial(assemble_kernel, width, count), in_specs...  1.8 us
  transfers between devices with their start and end apart: 9, of which 6 were waited for; matrix products, arithmetic and copies ran while one was open for 0% of the time, Pallas kernels for 27%

profile of v6, /device:TPU:0, one launch (start us, length us, event | category | flops | bytes accessed | tf_op | source)
XLA Modules:
  0.0 86.9 jit_solution(5995424635940554438)
XLA Ops:
  0.6 0.7 stack.40.at_ref
  1.3 0.0 copy-start
  1.3 0.0 copy-start.1
  1.3 45.5 %spectral_gradients.1 = (f32[9216,256]{1,0:T(8,128)}, f32[2,2,104,128]{3,2,1,0:T(8,128)}) custom-call(s32[10]{0:T(128)} %stack.40.at_ref, f32[2025,8,96]{2,1,0:T(8,128)} %bitcast.22, f32[2025,8,96]{2,1,0:T(8,128)} %bitcast.23, bf16[192,576]{1,0:T(8,128)(2,1)} %constant.34.clone.tx_ref, bf16[192,576]{1,0:T(8,128)(2,1)} %constant.35.clone.tg_ref, ...), custom_call_target="tpu_custom_call" | custom-call | tf_op jit(solution)/shard_map/spectral_gradients/pallas_call | solution.py:378
  46.9 3.1 %collective-permute-start = (f32[4,104,128]{2,1,0:T(8,128)}, f32[4,104,128]{2,1,0:T(8,128)S(1)}, u32[]{:S(2)}, u32[]{:S(2)}) collective-permute-start(f32[4,104,128]{2,1,0:T(8,128)} %bitcast.25), channel_id=1, source_target_pairs={{0,8},{8,0},{16,24},{24,16},{1,9},{9,1},{17,25},{25,17},{2,10},{10... | collective-permute-start | bytes 638984 | tf_op jit(solution)/shard_map/ppermute | solution.py:464
  50.0 0.0 copy-done
  50.0 0.0 copy-done.1
  50.0 0.0 copy-done.3
  50.0 7.6 %lat_back.2.refs_0_ = f32[2,48,96,128]{3,2,1,0:T(8,128)S(1)} custom-call(s32[10]{0:T(128)S(1)} %copy-done.3, f32[9216,256]{1,0:T(8,128)} %get-tuple-element.26.s_ref, f32[2,8,96,96]{3,2,1,0:T(8,128)S(1)} %copy-done, bf16[192,192]{1,0:T(8,128)(2,1)S(1)} %copy-done.1), custom_call_target="tpu_custom_call" | custom-call | tf_op jit(solution)/shard_map/lat_back/pallas_call | solution.py:415
  57.5 0.0 copy-start.2
  57.5 0.0 collective-permute-done
  57.6 0.0 copy-done.4
  57.6 2.7 %collective-permute-start.1 = (f32[4,104,128]{2,1,0:T(8,128)S(1)}, f32[4,104,128]{2,1,0:T(8,128)S(1)}, u32[]{:S(2)}, u32[]{:S(2)}) collective-permute-start(f32[4,104,128]{2,1,0:T(8,128)S(1)} %bitcast_add_fusion), channel_id=1, source_target_pairs={{0,16},{8,24},{16,0},{24,8},{1,17},{9,25},{17,1},{25,9},{2,18},{10... | collective-permute-start | bytes 638984 | tf_op jit(solution)/shard_map/ppermute | solution.py:464
  60.3 7.6 %lat_back.3.refs_1_ = f32[2,48,96,128]{3,2,1,0:T(8,128)S(1)} custom-call(s32[10]{0:T(128)S(1)} %copy-done.3, f32[9216,256]{1,0:T(8,128)} %get-tuple-element.26.s_ref, f32[2,8,96,96]{3,2,1,0:T(8,128)S(1)} %copy-done, bf16[192,192]{1,0:T(8,128)(2,1)S(1)} %copy-done.1), custom_call_target="tpu_custom_call" | custom-call | tf_op jit(solution)/shard_map/lat_back/pallas_call | solution.py:415
  67.8 1.8 %collective-permute-done.1 = f32[4,104,128]{2,1,0:T(8,128)S(1)} collective-permute-done((f32[4,104,128]{2,1,0:T(8,128)S(1)}, f32[4,104,128]{2,1,0:T(8,128)S(1)}, u32[]{:S(2)}, u32[]{:S(2)}) %collective-permute-start.1) | collective-permute-done | bytes 213024 | tf_op jit(solution)/shard_map/ppermute | solution.py:464
  69.7 0.1 collective-permute-start.5
  69.8 2.6 %collective-permute-start.4 = (f32[4,104,128]{2,1,0:T(8,128)S(1)}, f32[4,104,128]{2,1,0:T(8,128)S(1)}, u32[]{:S(2)}, u32[]{:S(2)}) collective-permute-start(f32[4,104,128]{2,1,0:T(8,128)S(1)} %add.7.refs_0_), channel_id=1, source_target_pairs={{0,6},{1,7},{2,4},{3,5},{4,2},{5,3},{6,0},{7,1},{8,14},{9,15},{10,... | collective-permute-start | bytes 638984 | tf_op jit(solution)/shard_map/ppermute | solution.py:464
  72.3 0.5 collective-permute-start.3
  72.8 0.5 collective-permute-start.2
  73.3 0.0 copy-done.2
  73.3 8.3 %lon_back.1 = f32[2025,8,96]{2,1,0:T(8,128)} custom-call(f32[2,48,96,128]{3,2,1,0:T(8,128)S(1)} %lat_back.2.refs_0_, f32[2,48,96,128]{3,2,1,0:T(8,128)S(1)} %lat_back.3.refs_1_, bf16[192,576]{1,0:T(8,128)(2,1)S(1)} %copy-done.2), custom_call_target="tpu_custom_call" | custom-call | tf_op jit(solution)/shard_map/lon_back/pallas_call | solution.py:437
  81.6 0.0 collective-permute-done.5.refs_1_
  81.6 0.0 collective-permute-done.4.refs_6_
  81.6 1.3 %collective-permute-done.3.refs_4_ = f32[4,104,128]{2,1,0:T(8,128)S(1)} collective-permute-done((f32[4,104,128]{2,1,0:T(8,128)S(1)}, f32[4,104,128]{2,1,0:T(8,128)S(1)}, u32[]{:S(2)}, u32[]{:S(2)}) %collective-permute-start.3) | collective-permute-done | bytes 213024 | tf_op jit(solution)/shard_map/ppermute | solution.py:464
  82.9 0.2 collective-permute-done.2.refs_2_
  83.1 0.0 collective-permute-start.6
  83.1 0.5 collective-permute-start.7
  83.6 0.0 collective-permute-start.8
  83.6 1.0 %collective-permute-done.6.refs_3_ = f32[4,104,128]{2,1,0:T(8,128)S(1)} collective-permute-done((f32[4,104,128]{2,1,0:T(8,128)S(1)}, f32[4,104,128]{2,1,0:T(8,128)S(1)}, u32[]{:S(2)}, u32[]{:S(2)}) %collective-permute-start.6) | collective-permute-done | bytes 213024 | tf_op jit(solution)/shard_map/ppermute | solution.py:464
  84.5 0.3 collective-permute-done.7.refs_5_
  84.8 0.3 collective-permute-done.8.refs_7_
  85.1 1.8 %assemble.1 = (f32[2,8,96,96]{3,2,1,0:T(8,128)}, f32[2,8,96,96]{3,2,1,0:T(8,128)}, f32[2,8,96]{2,1,0:T(8,128)}, f32[2,8,96]{2,1,0:T(8,128)}) custom-call(s32[10]{0:T(128)S(1)} %copy-done.3, f32[4,104,128]{2,1,0:T(8,128)S(1)} %add.7.refs_0_, f32[4,104,128]{2,1,0:T(8,128)S(1)} %collective-permute-done.5.refs_1_, ...), custom_call_target="tpu_custom_call" | custom-call | tf_op jit(solution)/shard_map/assemble/pallas_call | solution.py:452
  (4 shorter events, 0.1 us)
Async XLA Ops:
  1.3 48.6 %copy-start = (f32[2,8,96,96]{3,2,1,0:T(8,128)S(1)}, f32[2,8,96,96]{3,2,1,0:T(8,128)}, u32[]{:S(2)}) copy-start(f32[2,8,96,96]{3,2,1,0:T(8,128)} %wa_ref.5) | copy-start | bytes 1769476
  1.3 48.6 %copy-start.1 = (bf16[192,192]{1,0:T(8,128)(2,1)S(1)}, bf16[192,192]{1,0:T(8,128)(2,1)}, u32[]{:S(2)}) copy-start(bf16[192,192]{1,0:T(8,128)(2,1)} %constant.38.clone.f_ref) | copy-start | bytes 221188
  1.3 48.6 %copy-start.3 = (s32[10]{0:T(128)S(1)}, s32[10]{0:T(128)}, u32[]{:S(2)}) copy-start(s32[10]{0:T(128)} %stack.40.at_ref) | copy-start | bytes 124
  46.9 10.7 %copy-start.4 = (f32[2,2,104,128]{3,2,1,0:T(8,128)S(1)}, f32[2,2,104,128]{3,2,1,0:T(8,128)}, u32[]{:S(2)}) copy-start(f32[2,2,104,128]{3,2,1,0:T(8,128)} %get-tuple-element.22) | copy-start | bytes 638980
  46.9 10.7 %collective-permute-start = (f32[4,104,128]{2,1,0:T(8,128)}, f32[4,104,128]{2,1,0:T(8,128)S(1)}, u32[]{:S(2)}, u32[]{:S(2)}) collective-permute-start(f32[4,104,128]{2,1,0:T(8,128)} %bitcast.25), channel_id=1, source_target_pairs={{0,8},{8,0},{16,24},{24,16},{1,9},{9,1},{17,25},{25,17},{2,10},{10... | collective-permute-start | bytes 638984 | tf_op jit(solution)/shard_map/ppermute | solution.py:464
  57.5 15.8 %copy-start.2 = (bf16[192,576]{1,0:T(8,128)(2,1)S(1)}, bf16[192,576]{1,0:T(8,128)(2,1)}, u32[]{:S(2)}) copy-start(bf16[192,576]{1,0:T(8,128)(2,1)} %constant.39.clone.refs_2_) | copy-start | bytes 663556
  57.6 12.1 %collective-permute-start.1 = (f32[4,104,128]{2,1,0:T(8,128)S(1)}, f32[4,104,128]{2,1,0:T(8,128)S(1)}, u32[]{:S(2)}, u32[]{:S(2)}) collective-permute-start(f32[4,104,128]{2,1,0:T(8,128)S(1)} %bitcast_add_fusion), channel_id=1, source_target_pairs={{0,16},{8,24},{16,0},{24,8},{1,17},{9,25},{17,1},{25,9},{2,18},{10... | collective-permute-start | bytes 638984 | tf_op jit(solution)/shard_map/ppermute | solution.py:464
  69.7 12.0 %collective-permute-start.5 = (f32[4,104,128]{2,1,0:T(8,128)S(1)}, f32[4,104,128]{2,1,0:T(8,128)S(1)}, u32[]{:S(2)}, u32[]{:S(2)}) collective-permute-start(f32[4,104,128]{2,1,0:T(8,128)S(1)} %add.7.refs_0_), channel_id=1, source_target_pairs={{0,1},{1,0},{2,3},{3,2},{4,5},{5,4},{6,7},{7,6},{8,9},{9,8},{10,11... | collective-permute-start | bytes 638984 | tf_op jit(solution)/shard_map/ppermute | solution.py:464
  69.8 11.9 %collective-permute-start.4 = (f32[4,104,128]{2,1,0:T(8,128)S(1)}, f32[4,104,128]{2,1,0:T(8,128)S(1)}, u32[]{:S(2)}, u32[]{:S(2)}) collective-permute-start(f32[4,104,128]{2,1,0:T(8,128)S(1)} %add.7.refs_0_), channel_id=1, source_target_pairs={{0,6},{1,7},{2,4},{3,5},{4,2},{5,3},{6,0},{7,1},{8,14},{9,15},{10,... | collective-permute-start | bytes 638984 | tf_op jit(solution)/shard_map/ppermute | solution.py:464
  72.3 10.6 %collective-permute-start.3 = (f32[4,104,128]{2,1,0:T(8,128)S(1)}, f32[4,104,128]{2,1,0:T(8,128)S(1)}, u32[]{:S(2)}, u32[]{:S(2)}) collective-permute-start(f32[4,104,128]{2,1,0:T(8,128)S(1)} %add.7.refs_0_), channel_id=1, source_target_pairs={{0,4},{1,5},{2,6},{3,7},{4,0},{5,1},{6,2},{7,3},{8,12},{9,13},{10,... | collective-permute-start | bytes 638984 | tf_op jit(solution)/shard_map/ppermute | solution.py:464
  72.8 10.2 %collective-permute-start.2 = (f32[4,104,128]{2,1,0:T(8,128)S(1)}, f32[4,104,128]{2,1,0:T(8,128)S(1)}, u32[]{:S(2)}, u32[]{:S(2)}) collective-permute-start(f32[4,104,128]{2,1,0:T(8,128)S(1)} %add.7.refs_0_), channel_id=1, source_target_pairs={{0,2},{1,3},{2,0},{3,1},{4,6},{5,7},{6,4},{7,5},{8,10},{9,11},{10,... | collective-permute-start | bytes 638984 | tf_op jit(solution)/shard_map/ppermute | solution.py:464
  83.1 1.5 %collective-permute-start.6 = (f32[4,104,128]{2,1,0:T(8,128)S(1)}, f32[4,104,128]{2,1,0:T(8,128)S(1)}, u32[]{:S(2)}, u32[]{:S(2)}) collective-permute-start(f32[4,104,128]{2,1,0:T(8,128)S(1)} %collective-permute-done.2.refs_2_), channel_id=1, source_target_pairs={{0,1},{1,0},{2,3},{3,2},{4,5},{5,4},{6,7},{7,6},{8,9},{9,8},{10,11... | collective-permute-start | bytes 638984 | tf_op jit(solution)/shard_map/ppermute | solution.py:464
  83.1 1.8 %collective-permute-start.7 = (f32[4,104,128]{2,1,0:T(8,128)S(1)}, f32[4,104,128]{2,1,0:T(8,128)S(1)}, u32[]{:S(2)}, u32[]{:S(2)}) collective-permute-start(f32[4,104,128]{2,1,0:T(8,128)S(1)} %collective-permute-done.3.refs_4_), channel_id=1, source_target_pairs={{0,1},{1,0},{2,3},{3,2},{4,5},{5,4},{6,7},{7,6},{8,9},{9,8},{10,11... | collective-permute-start | bytes 638984 | tf_op jit(solution)/shard_map/ppermute | solution.py:464
  83.6 1.6 %collective-permute-start.8 = (f32[4,104,128]{2,1,0:T(8,128)S(1)}, f32[4,104,128]{2,1,0:T(8,128)S(1)}, u32[]{:S(2)}, u32[]{:S(2)}) collective-permute-start(f32[4,104,128]{2,1,0:T(8,128)S(1)} %collective-permute-done.4.refs_6_), channel_id=1, source_target_pairs={{0,1},{1,0},{2,3},{3,2},{4,5},{5,4},{6,7},{7,6},{8,9},{9,8},{10,11... | collective-permute-start | bytes 638984 | tf_op jit(solution)/shard_map/ppermute | solution.py:464

commit v7 on v6

--- a/solution.py
+++ b/solution.py
@@ -193,7 +193,7 @@
                         spectra[which, pl.ds(first + k, size.row_slots, stride=stride), :],
                         spectra[which, pl.ds(first + k + slots, size.row_slots, stride=stride), :],
                     )
-                    out = four_product(table, data)
+                    out = three_product(table, *split(data))
                     cos_one, cos_two = out[:half, :LANES], out[:half, LANES:]
                     sin_one, sin_two = out[half:, :LANES], out[half:, LANES:]
                     plus = side_by_side(cos_one - sin_two, -(cos_two + sin_one))
@@ -313,7 +313,7 @@
                 ],
                 axis=0,
             )
-            out = four_product(f_ref, data)
+            out = three_product(f_ref, *split(data))
             for q in range(2):
                 v_ref[q, k] = out[:, q * LANES : (q + 1) * LANES]
 
@@ -368,7 +368,7 @@
 def spectral_gradients(size, place, fields, first_weight, first_bias, second_weight, second_bias):
     width = first_weight.shape[-1]
     tables = [three_way(lon_table(size, which)) for which in (False, True)]
-    tables += [four_way(lat_table(size, which)) for which in (False, True)]
+    tables += [three_way(lat_table(size, which)) for which in (False, True)]
     consts = [jnp.asarray(table) for table in tables]
     weight = pl.BlockSpec((2, 1, width, width), lambda i, at: (0, at[1], 0, 0))
     bias = whole_spec(first_bias)
@@ -409,7 +409,7 @@
     width = weight.shape[-1]
     lat = lat_table(size, False).T.copy()
     lat[:, size.half :] *= -1.0
-    table = jnp.asarray(four_way(lat))
+    table = jnp.asarray(three_way(lat))
     rows = size.batch * size.both
     steps = size.slots // size.batch // PARTS
     return pl.pallas_call(

time: 87.3 us -> 88 us (level)
  no operation moved by 1% of the time
where the time goes in v7:
time: 88 us; the launch traced here: 87.6 us
  Pallas kernels  71.6 us (81%)
  starting transfers between devices  9.89 us (11%)
  waiting for transfers between devices  4.68 us (5%)
    pallas_call x1, Pallas kernels, spectral_gradients(): pl.pallas_call(functools.partial(gradient_kernel, size, width, bands, bat...  46.1 us
    pallas_call x2, Pallas kernels, lat_back(): pl.pallas_call(functools.partial(lat_back_kernel, size, width), grid_spec...  15.4 us
    ppermute x9, starting transfers between devices, crossed(): return lax.ppermute(value, axis, [(i, i ^ mask) for i in range(count)])  9.89 us
    pallas_call x1, Pallas kernels, lon_back(): pl.pallas_call(functools.partial(lon_back_kernel, size, width), grid=(siz...  8.31 us
    ppermute x9, waiting for transfers between devices, crossed(): return lax.ppermute(value, axis, [(i, i ^ mask) for i in range(count)])  4.68 us
    pallas_call x1, Pallas kernels, assemble(): pl.pallas_call(functools.partial(assemble_kernel, width, count), in_specs...  1.8 us
  transfers between devices with their start and end apart: 9, of which 6 were waited for; matrix products, arithmetic and copies ran while one was open for 0% of the time, Pallas kernels for 27%

profile of v7, /device:TPU:0, one launch (start us, length us, event | category | flops | bytes accessed | tf_op | source)
XLA Modules:
  0.0 87.6 jit_solution(1323000579869137221)
XLA Ops:
  0.6 0.7 stack.40.at_ref
  1.3 0.0 copy-start
  1.3 0.0 copy-start.1
  1.3 46.1 %spectral_gradients.1 = (f32[9216,256]{1,0:T(8,128)}, f32[2,2,104,128]{3,2,1,0:T(8,128)}) custom-call(s32[10]{0:T(128)} %stack.40.at_ref, f32[2025,8,96]{2,1,0:T(8,128)} %bitcast.22, f32[2025,8,96]{2,1,0:T(8,128)} %bitcast.23, bf16[192,576]{1,0:T(8,128)(2,1)} %constant.34.clone.tx_ref, bf16[192,576]{1,0:T(8,128)(2,1)} %constant.35.clone.tg_ref, ...), custom_call_target="tpu_custom_call" | custom-call | tf_op jit(solution)/shard_map/spectral_gradients/pallas_call | solution.py:378
  47.5 3.1 %collective-permute-start = (f32[4,104,128]{2,1,0:T(8,128)}, f32[4,104,128]{2,1,0:T(8,128)S(1)}, u32[]{:S(2)}, u32[]{:S(2)}) collective-permute-start(f32[4,104,128]{2,1,0:T(8,128)} %bitcast.25), channel_id=1, source_target_pairs={{0,8},{8,0},{16,24},{24,16},{1,9},{9,1},{17,25},{25,17},{2,10},{10... | collective-permute-start | bytes 638984 | tf_op jit(solution)/shard_map/ppermute | solution.py:464
  50.5 0.0 copy-done
  50.5 0.0 copy-done.1
  50.6 0.0 copy-done.3
  50.6 7.7 %lat_back.2.refs_0_ = f32[2,48,96,128]{3,2,1,0:T(8,128)S(1)} custom-call(s32[10]{0:T(128)S(1)} %copy-done.3, f32[9216,256]{1,0:T(8,128)} %get-tuple-element.26.s_ref, f32[2,8,96,96]{3,2,1,0:T(8,128)S(1)} %copy-done, bf16[96,288]{1,0:T(8,128)(2,1)S(1)} %copy-done.1), custom_call_target="tpu_custom_call" | custom-call | tf_op jit(solution)/shard_map/lat_back/pallas_call | solution.py:415
  58.2 0.0 copy-start.2
  58.2 0.0 collective-permute-done
  58.3 0.0 copy-done.4
  58.3 2.7 %collective-permute-start.1 = (f32[4,104,128]{2,1,0:T(8,128)S(1)}, f32[4,104,128]{2,1,0:T(8,128)S(1)}, u32[]{:S(2)}, u32[]{:S(2)}) collective-permute-start(f32[4,104,128]{2,1,0:T(8,128)S(1)} %bitcast_add_fusion), channel_id=1, source_target_pairs={{0,16},{8,24},{16,0},{24,8},{1,17},{9,25},{17,1},{25,9},{2,18},{10... | collective-permute-start | bytes 638984 | tf_op jit(solution)/shard_map/ppermute | solution.py:464
  61.0 7.7 %lat_back.3.refs_1_ = f32[2,48,96,128]{3,2,1,0:T(8,128)S(1)} custom-call(s32[10]{0:T(128)S(1)} %copy-done.3, f32[9216,256]{1,0:T(8,128)} %get-tuple-element.26.s_ref, f32[2,8,96,96]{3,2,1,0:T(8,128)S(1)} %copy-done, bf16[96,288]{1,0:T(8,128)(2,1)S(1)} %copy-done.1), custom_call_target="tpu_custom_call" | custom-call | tf_op jit(solution)/shard_map/lat_back/pallas_call | solution.py:415
  68.7 1.7 %collective-permute-done.1 = f32[4,104,128]{2,1,0:T(8,128)S(1)} collective-permute-done((f32[4,104,128]{2,1,0:T(8,128)S(1)}, f32[4,104,128]{2,1,0:T(8,128)S(1)}, u32[]{:S(2)}, u32[]{:S(2)}) %collective-permute-start.1) | collective-permute-done | bytes 213024 | tf_op jit(solution)/shard_map/ppermute | solution.py:464
  70.4 0.1 collective-permute-start.5
  70.5 2.6 %collective-permute-start.4 = (f32[4,104,128]{2,1,0:T(8,128)S(1)}, f32[4,104,128]{2,1,0:T(8,128)S(1)}, u32[]{:S(2)}, u32[]{:S(2)}) collective-permute-start(f32[4,104,128]{2,1,0:T(8,128)S(1)} %add.7.refs_0_), channel_id=1, source_target_pairs={{0,6},{1,7},{2,4},{3,5},{4,2},{5,3},{6,0},{7,1},{8,14},{9,15},{10,... | collective-permute-start | bytes 638984 | tf_op jit(solution)/shard_map/ppermute | solution.py:464
  73.0 0.5 collective-permute-start.3
  73.5 0.5 collective-permute-start.2
  74.0 0.0 copy-done.2
  74.0 8.3 %lon_back.1 = f32[2025,8,96]{2,1,0:T(8,128)} custom-call(f32[2,48,96,128]{3,2,1,0:T(8,128)S(1)} %lat_back.2.refs_0_, f32[2,48,96,128]{3,2,1,0:T(8,128)S(1)} %lat_back.3.refs_1_, bf16[192,576]{1,0:T(8,128)(2,1)S(1)} %copy-done.2), custom_call_target="tpu_custom_call" | custom-call | tf_op jit(solution)/shard_map/lon_back/pallas_call | solution.py:437
  82.3 0.0 collective-permute-done.5.refs_1_
  82.4 0.0 collective-permute-done.4.refs_6_
  82.4 1.3 %collective-permute-done.3.refs_4_ = f32[4,104,128]{2,1,0:T(8,128)S(1)} collective-permute-done((f32[4,104,128]{2,1,0:T(8,128)S(1)}, f32[4,104,128]{2,1,0:T(8,128)S(1)}, u32[]{:S(2)}, u32[]{:S(2)}) %collective-permute-start.3) | collective-permute-done | bytes 213024 | tf_op jit(solution)/shard_map/ppermute | solution.py:464
  83.6 0.1 collective-permute-done.2.refs_2_
  83.8 0.0 collective-permute-start.6
  83.8 0.5 collective-permute-start.7
  84.3 0.0 collective-permute-start.8
  84.3 1.0 %collective-permute-done.6.refs_3_ = f32[4,104,128]{2,1,0:T(8,128)S(1)} collective-permute-done((f32[4,104,128]{2,1,0:T(8,128)S(1)}, f32[4,104,128]{2,1,0:T(8,128)S(1)}, u32[]{:S(2)}, u32[]{:S(2)}) %collective-permute-start.6) | collective-permute-done | bytes 213024 | tf_op jit(solution)/shard_map/ppermute | solution.py:464
  85.2 0.3 collective-permute-done.7.refs_5_
  85.5 0.3 collective-permute-done.8.refs_7_
  85.8 1.8 %assemble.1 = (f32[2,8,96,96]{3,2,1,0:T(8,128)}, f32[2,8,96,96]{3,2,1,0:T(8,128)}, f32[2,8,96]{2,1,0:T(8,128)}, f32[2,8,96]{2,1,0:T(8,128)}) custom-call(s32[10]{0:T(128)S(1)} %copy-done.3, f32[4,104,128]{2,1,0:T(8,128)S(1)} %add.7.refs_0_, f32[4,104,128]{2,1,0:T(8,128)S(1)} %collective-permute-done.5.refs_1_, ...), custom_call_target="tpu_custom_call" | custom-call | tf_op jit(solution)/shard_map/assemble/pallas_call | solution.py:452
  (4 shorter events, 0.1 us)
Async XLA Ops:
  1.3 49.2 %copy-start = (f32[2,8,96,96]{3,2,1,0:T(8,128)S(1)}, f32[2,8,96,96]{3,2,1,0:T(8,128)}, u32[]{:S(2)}) copy-start(f32[2,8,96,96]{3,2,1,0:T(8,128)} %wa_ref.5) | copy-start | bytes 1769476
  1.3 49.2 %copy-start.1 = (bf16[96,288]{1,0:T(8,128)(2,1)S(1)}, bf16[96,288]{1,0:T(8,128)(2,1)}, u32[]{:S(2)}) copy-start(bf16[96,288]{1,0:T(8,128)(2,1)} %constant.38.clone.f_ref) | copy-start | bytes 165892
  1.3 49.2 %copy-start.3 = (s32[10]{0:T(128)S(1)}, s32[10]{0:T(128)}, u32[]{:S(2)}) copy-start(s32[10]{0:T(128)} %stack.40.at_ref) | copy-start | bytes 124
  47.5 10.8 %copy-start.4 = (f32[2,2,104,128]{3,2,1,0:T(8,128)S(1)}, f32[2,2,104,128]{3,2,1,0:T(8,128)}, u32[]{:S(2)}) copy-start(f32[2,2,104,128]{3,2,1,0:T(8,128)} %get-tuple-element.22) | copy-start | bytes 638980
  47.5 10.8 %collective-permute-start = (f32[4,104,128]{2,1,0:T(8,128)}, f32[4,104,128]{2,1,0:T(8,128)S(1)}, u32[]{:S(2)}, u32[]{:S(2)}) collective-permute-start(f32[4,104,128]{2,1,0:T(8,128)} %bitcast.25), channel_id=1, source_target_pairs={{0,8},{8,0},{16,24},{24,16},{1,9},{9,1},{17,25},{25,17},{2,10},{10... | collective-permute-start | bytes 638984 | tf_op jit(solution)/shard_map/ppermute | solution.py:464
  58.2 15.8 %copy-start.2 = (bf16[192,576]{1,0:T(8,128)(2,1)S(1)}, bf16[192,576]{1,0:T(8,128)(2,1)}, u32[]{:S(2)}) copy-start(bf16[192,576]{1,0:T(8,128)(2,1)} %constant.39.clone.refs_2_) | copy-start | bytes 663556
  58.3 12.1 %collective-permute-start.1 = (f32[4,104,128]{2,1,0:T(8,128)S(1)}, f32[4,104,128]{2,1,0:T(8,128)S(1)}, u32[]{:S(2)}, u32[]{:S(2)}) collective-permute-start(f32[4,104,128]{2,1,0:T(8,128)S(1)} %bitcast_add_fusion), channel_id=1, source_target_pairs={{0,16},{8,24},{16,0},{24,8},{1,17},{9,25},{17,1},{25,9},{2,18},{10... | collective-permute-start | bytes 638984 | tf_op jit(solution)/shard_map/ppermute | solution.py:464
  70.4 12.0 %collective-permute-start.5 = (f32[4,104,128]{2,1,0:T(8,128)S(1)}, f32[4,104,128]{2,1,0:T(8,128)S(1)}, u32[]{:S(2)}, u32[]{:S(2)}) collective-permute-start(f32[4,104,128]{2,1,0:T(8,128)S(1)} %add.7.refs_0_), channel_id=1, source_target_pairs={{0,1},{1,0},{2,3},{3,2},{4,5},{5,4},{6,7},{7,6},{8,9},{9,8},{10,11... | collective-permute-start | bytes 638984 | tf_op jit(solution)/shard_map/ppermute | solution.py:464
  70.5 11.9 %collective-permute-start.4 = (f32[4,104,128]{2,1,0:T(8,128)S(1)}, f32[4,104,128]{2,1,0:T(8,128)S(1)}, u32[]{:S(2)}, u32[]{:S(2)}) collective-permute-start(f32[4,104,128]{2,1,0:T(8,128)S(1)} %add.7.refs_0_), channel_id=1, source_target_pairs={{0,6},{1,7},{2,4},{3,5},{4,2},{5,3},{6,0},{7,1},{8,14},{9,15},{10,... | collective-permute-start | bytes 638984 | tf_op jit(solution)/shard_map/ppermute | solution.py:464
  73.0 10.6 %collective-permute-start.3 = (f32[4,104,128]{2,1,0:T(8,128)S(1)}, f32[4,104,128]{2,1,0:T(8,128)S(1)}, u32[]{:S(2)}, u32[]{:S(2)}) collective-permute-start(f32[4,104,128]{2,1,0:T(8,128)S(1)} %add.7.refs_0_), channel_id=1, source_target_pairs={{0,4},{1,5},{2,6},{3,7},{4,0},{5,1},{6,2},{7,3},{8,12},{9,13},{10,... | collective-permute-start | bytes 638984 | tf_op jit(solution)/shard_map/ppermute | solution.py:464
  73.5 10.2 %collective-permute-start.2 = (f32[4,104,128]{2,1,0:T(8,128)S(1)}, f32[4,104,128]{2,1,0:T(8,128)S(1)}, u32[]{:S(2)}, u32[]{:S(2)}) collective-permute-start(f32[4,104,128]{2,1,0:T(8,128)S(1)} %add.7.refs_0_), channel_id=1, source_target_pairs={{0,2},{1,3},{2,0},{3,1},{4,6},{5,7},{6,4},{7,5},{8,10},{9,11},{10,... | collective-permute-start | bytes 638984 | tf_op jit(solution)/shard_map/ppermute | solution.py:464
  83.8 1.5 %collective-permute-start.6 = (f32[4,104,128]{2,1,0:T(8,128)S(1)}, f32[4,104,128]{2,1,0:T(8,128)S(1)}, u32[]{:S(2)}, u32[]{:S(2)}) collective-permute-start(f32[4,104,128]{2,1,0:T(8,128)S(1)} %collective-permute-done.2.refs_2_), channel_id=1, source_target_pairs={{0,1},{1,0},{2,3},{3,2},{4,5},{5,4},{6,7},{7,6},{8,9},{9,8},{10,11... | collective-permute-start | bytes 638984 | tf_op jit(solution)/shard_map/ppermute | solution.py:464
  83.8 1.8 %collective-permute-start.7 = (f32[4,104,128]{2,1,0:T(8,128)S(1)}, f32[4,104,128]{2,1,0:T(8,128)S(1)}, u32[]{:S(2)}, u32[]{:S(2)}) collective-permute-start(f32[4,104,128]{2,1,0:T(8,128)S(1)} %collective-permute-done.3.refs_4_), channel_id=1, source_target_pairs={{0,1},{1,0},{2,3},{3,2},{4,5},{5,4},{6,7},{7,6},{8,9},{9,8},{10,11... | collective-permute-start | bytes 638984 | tf_op jit(solution)/shard_map/ppermute | solution.py:464
  84.3 1.6 %collective-permute-start.8 = (f32[4,104,128]{2,1,0:T(8,128)S(1)}, f32[4,104,128]{2,1,0:T(8,128)S(1)}, u32[]{:S(2)}, u32[]{:S(2)}) collective-permute-start(f32[4,104,128]{2,1,0:T(8,128)S(1)} %collective-permute-done.4.refs_6_), channel_id=1, source_target_pairs={{0,1},{1,0},{2,3},{3,2},{4,5},{5,4},{6,7},{7,6},{8,9},{9,8},{10,11... | collective-permute-start | bytes 638984 | tf_op jit(solution)/shard_map/ppermute | solution.py:464
